TPU v7x, 128 devices: a whole 4x4x4 slice. The times are simulated.
128 devices in a mesh: gene: 8 (over y, x_lo), bin: 16 (over z, x_hi, core).
Axes of the slice: x: 4 (x_hi: 2, x_lo: 2; x = x_hi * 2 + x_lo), y: 4, z: 4, core: 2. Of those that a mesh axis runs over, the one named last changes fastest.
Arguments:
- counts: bfloat16 [49152, 18432], P('bin', 'gene'), may hold values from 2 to 80
- factors: float32 [49152, 256], P('bin'), may hold values from 0.01 to 1
- loadings: float32 [256, 18432], P(None, 'gene'), may hold values from 0.01 to 1
- position: int32 [49152], P('bin'), may hold values from 0 to 49151, as said below
- edge_codes: int32 [192, 256], P('bin'), may hold values from 1 to 15
Outputs:
- factors_new: float32 [49152, 256], P('bin')
- loadings_new: float32 [256, 18432], P(None, 'gene')
Inputs may be any that keep to these rules, and one draw needn't show every extreme that they name: Each grid position is named by exactly one barcode. The barcodes of one index s of bin (rows s * 3072 on) fall in 16 aligned groups of 192; group t holds positions in grid rows t * 12 to (t + 1) * 12 - 1, 192 from every such index.
All inputs are finite; a program needn't handle non-finite values.
Results may differ from a plain program's by a relative error of at most 0.0003.
Values sent between devices are 32-bit elements; how exact they have to be, the bound alone decides.
A program may use at most 128 MiB of HBM per device.

v0:
```python
import jax
import jax.numpy as jnp
from jax import lax
from jax.sharding import PartitionSpec as P

K = 256
G = 18432


def passed_along(block, axis, distance):
    devices = range(lax.axis_size(axis))
    route = [(i - distance, i) for i in devices if i - distance in devices]
    return lax.ppermute(block, axis, route)


def neighbour_sum(values, from_above, from_below):
    upper = jnp.concatenate([from_above[None], values[:-1]], 0)
    lower = jnp.concatenate([values[1:], from_below[None]], 0)
    beside = jnp.pad(values[:, 1:], ((0, 0), (0, 1), (0, 0))) + jnp.pad(
        values[:, :-1], ((0, 0), (1, 0), (0, 0))
    )
    return beside + 0.5 * (lower + upper)


def neighbour_first(values, from_above, from_below):
    upper = jnp.concatenate([from_above[:, None], values[:, :-1]], 1)
    lower = jnp.concatenate([values[:, 1:], from_below[:, None]], 1)
    beside = jnp.pad(values[:, :, 1:], ((0, 0), (0, 0), (0, 1))) + jnp.pad(
        values[:, :, :-1], ((0, 0), (0, 0), (1, 0))
    )
    return beside + 0.5 * (lower + upper)


def stencil_term(payload, col_width, position, edge_codes):
    bin_count = lax.axis_size("bin")
    row_count = position.shape[0]
    group_size = row_count // bin_count
    grid_rows, grid_cols = edge_codes.shape
    pos_float = position.astype(jnp.float32).reshape(bin_count, group_size)
    got_rows, got_pos = (
        lax.all_to_all(payload, "bin", split_axis=0, concat_axis=0, tiled=True),
        lax.all_to_all(pos_float, "bin", split_axis=0, concat_axis=0, tiled=True),
    )
    tile_slot = got_pos.reshape(row_count).astype(jnp.int32) - lax.axis_index("bin") * row_count
    cell_scale = edge_codes.astype(jnp.float32) / 8.0
    tile_rows = (
        jnp.zeros((row_count, col_width), jnp.float32)
        .at[tile_slot]
        .set(got_rows.reshape(row_count, col_width))
    )
    weighted = cell_scale[:, :, None] * tile_rows.reshape(grid_rows, grid_cols, col_width)
    rim_last, rim_first = (weighted[-1], weighted[0])
    upper_rows, upper_scale = passed_along((rim_last, cell_scale[-1]), "bin", 1)
    lower_rows, lower_scale = passed_along((rim_first, cell_scale[0]), "bin", -1)
    degree_grid = (
        cell_scale * neighbour_first(cell_scale[None], upper_scale[None], lower_scale[None])[0]
    )
    back_degree = degree_grid.reshape(row_count)[tile_slot]
    smooth_grid = cell_scale[:, :, None] * neighbour_sum(weighted, upper_rows, lower_rows)
    back_send = smooth_grid.reshape(row_count, col_width)[tile_slot].reshape(
        bin_count, group_size * col_width
    )
    smooth, degree = (
        lax.all_to_all(back_send, "bin", split_axis=0, concat_axis=0, tiled=True),
        lax.all_to_all(
            back_degree.reshape(bin_count, group_size),
            "bin",
            split_axis=0,
            concat_axis=0,
            tiled=True,
        ),
    )
    smooth = smooth.reshape(row_count, col_width)
    return (smooth, degree.reshape(row_count))


def on_device(counts, factors, loadings, position, edge_codes):
    bin_count = lax.axis_size("bin")
    row_count, width_all = factors.shape
    group_size = row_count // bin_count
    load_bf = loadings.astype(jnp.bfloat16)
    right_dims = (((1,), (1,)), ((), ()))
    load_gram = lax.psum(
        lax.dot_general(load_bf, load_bf, right_dims, preferred_element_type=jnp.float32), "gene"
    )
    payload = factors.reshape(bin_count, group_size * width_all)
    smooth, degree = stencil_term(payload, width_all, position, edge_codes)
    penalty = float(G * K) / 64.0
    numer = lax.psum(
        lax.dot_general(counts, load_bf, right_dims, preferred_element_type=jnp.float32), "gene"
    )
    denom = (
        jnp.dot(factors, load_gram, precision=lax.Precision.HIGHEST)
        + penalty * degree[:, None] * factors
    )
    factors_new = factors * (numer + penalty * smooth) / denom
    fac_bf = factors_new.astype(jnp.bfloat16)
    left_dims = (((0,), (0,)), ((), ()))
    cross_part = lax.dot_general(fac_bf, counts, left_dims, preferred_element_type=jnp.float32)
    gram_part = lax.dot_general(fac_bf, fac_bf, left_dims, preferred_element_type=jnp.float32)
    cross, fac_gram = lax.psum((cross_part, gram_part), "bin")
    loadings_new = loadings * cross / jnp.dot(fac_gram, loadings, precision=lax.Precision.HIGHEST)
    return (factors_new, loadings_new)


def solution(mesh):
    placed = (P("bin", "gene"), P("bin", None), P(None, "gene"), P("bin"), P("bin", None))
    return jax.shard_map(
        on_device,
        mesh=mesh,
        in_specs=placed,
        out_specs=(P("bin", None), P(None, "gene")),
        check_vma=False,
    )
```

profile of v0, /device:TPU:1, one launch (start us, length us, event | category | flops | bytes accessed | tf_op | source)
XLA Modules:
  0.0 520.0 jit_solution(17406114707212245582)
XLA Ops:
  7.2 0.7 convert_element_type.33
  7.9 0.7 all_to_all.24
  8.6 9.3 %all-to-all-start = ((f32[16,1,192]{2,1,0:T(1,128)}), f32[16,1,192]{2,1,0:T(1,128)S(1)}, u32[]{:S(2)}, u32[]{:S(2)}) async-start(f32[16,1,192]{2,1,0:T(1,128)} %all_to_all.24), calls=%async_computation | async-start | bytes 32768 | tf_op jit(solution)/shard_map/all_to_all | solution.py:42
  17.9 0.7 fusion.19
  18.6 2.0 collective-permute-start.2
  20.6 5.1 collective-permute-start.3
  25.7 6.4 %all_to_all.26 = f32[16,1,49152]{2,1,0:T(1,128)} reshape(f32[3072,256]{1,0:T(8,128)} %param.6) | data formatting | bytes 6291456 | tf_op jit(solution)/shard_map/all_to_all | solution.py:41
  32.1 0.0 all-to-all-done
  32.1 7.9 %all-to-all-start.1 = ((f32[16,1,49152]{2,1,0:T(1,128)}), f32[16,1,49152]{2,1,0:T(1,128)S(1)}, u32[]{:S(2)}, u32[]{:S(2)}) async-start(f32[16,1,49152]{2,1,0:T(1,128)} %all_to_all.26), calls=%async_computation.1 | async-start | bytes 6291456 | tf_op jit(solution)/shard_map/all_to_all | solution.py:41
  39.9 0.1 fusion.22
  40.0 0.0 copy-start.3
  40.0 11.4 %fusion.13 = f32[3072,256]{1,0:T(8,128)} fusion(bf16[3072,2304]{1,0:T(8,128)(2,1)} %param.5, f32[256,2304]{1,0:T(8,128)} %param.7), kind=kOutput, calls=%fused_computation.21 | convolution fusion | flops 3624468480 | bytes 19660800 | tf_op jit(solution)/shard_map/dot_general | solution.py:90
  51.4 0.0 collective-permute-done.2
  51.4 0.0 collective-permute-done.3
  51.4 0.0 copy-done.3
  51.4 0.1 fusion.18
  51.5 0.1 subtract_reduce_fusion
  51.6 0.1 sub.18
  51.7 17.4 %gather_fusion.1 = f32[3072]{0:T(1024)S(1)} fusion(f32[3072]{0:T(1024)S(1)} %reshape.142, s32[3072]{0:T(1024)S(1)} %broadcast_clamp_fusion), kind=kCustom, calls=%fused_computation.1 | custom fusion | bytes 36864 | tf_op jit(solution)/shard_map/gather | solution.py:58
  69.1 0.7 all_to_all.30
  69.8 9.9 %all-to-all-done.1 = f32[16,1,49152]{2,1,0:T(1,128)S(1)} async-done(((f32[16,1,49152]{2,1,0:T(1,128)}), f32[16,1,49152]{2,1,0:T(1,128)S(1)}, u32[]{:S(2)}, u32[]{:S(2)}) %all-to-all-start.1) | async-done | bytes 3145760 | tf_op jit(solution)/shard_map/all_to_all | solution.py:41
  79.7 4.7 all-to-all-start.3
  84.4 10.1 %reduce.1 = f32[16,49152]{1,0:T(8,128)} reduce(f32[16,1,49152]{2,1,0:T(1,128)S(1)} %all-to-all-done.1, f32[]{:T(128)} %constant.32), dimensions={1}, to_apply=%all_to_all.27.reduce_sub_computation | reduce | bytes 6291460 | tf_op jit(solution)/shard_map/all_to_all | solution.py:41
  94.5 3.3 reshape.163
  97.8 24.1 %scatter_custom_fusion = f32[3072,256]{1,0:T(8,128)S(1)} fusion(s32[3072]{0:T(1024)S(1)} %bitcast.36, f32[3072,256]{1,0:T(8,128)} %reshape.163, f32[]{:T(128)} %constant.8.clone.1), kind=kCustom, calls=%fused_computation.12 | custom fusion | bytes 3146240 | tf_op jit(solution)/shard_map/scatter | solution.py:49
  121.9 0.5 broadcast_multiply_fusion
  122.4 0.6 fusion.20
  123.1 2.0 collective-permute-start
  125.1 5.0 collective-permute-start.1
  130.1 0.6 fusion.21
  130.8 1.5 collective-permute-done
  132.3 1.2 collective-permute-done.1
  133.4 1.3 fusion.4
  134.7 12.3 %gather_fusion = f32[3072,256]{1,0:T(8,128)} fusion(f32[3072,256]{1,0:T(8,128)S(1)} %bitcast.31, s32[3072]{0:T(1024)S(1)} %broadcast_clamp_fusion), kind=kCustom, calls=%fused_computation | custom fusion | bytes 6303744 | tf_op jit(solution)/shard_map/gather | solution.py:60
  147.1 6.4 %all_to_all.32 = f32[16,1,49152]{2,1,0:T(1,128)} reshape(f32[3072,256]{1,0:T(8,128)} %gather_fusion) | data formatting | bytes 6291456 | tf_op jit(solution)/shard_map/all_to_all | solution.py:64
  153.4 0.0 all-to-all-done.3
  153.5 9.2 %all-to-all-start.2 = ((f32[16,1,49152]{2,1,0:T(1,128)}), f32[16,1,49152]{2,1,0:T(1,128)S(1)}, u32[]{:S(2)}, u32[]{:S(2)}) async-start(f32[16,1,49152]{2,1,0:T(1,128)} %all_to_all.32), calls=%async_computation.2 | async-start | bytes 6291456 | tf_op jit(solution)/shard_map/all_to_all | solution.py:64
  162.7 0.0 all-reduce.11.cloned.1.call-start
  162.7 3.6 fusion.11
  166.3 0.0 all-reduce.11.cloned.1.call-update
  166.4 0.0 all-reduce.9.cloned.1.call-start
  166.5 0.1 mul.92
  166.5 55.6 %all-to-all-done.2 = f32[16,1,49152]{2,1,0:T(1,128)S(1)} async-done(((f32[16,1,49152]{2,1,0:T(1,128)}), f32[16,1,49152]{2,1,0:T(1,128)S(1)}, u32[]{:S(2)}, u32[]{:S(2)}) %all-to-all-start.2) | async-done | bytes 3145760 | tf_op jit(solution)/shard_map/all_to_all | solution.py:64
  222.1 10.8 %multiply_reduce_fusion = f32[16,49152]{1,0:T(8,128)} fusion(f32[16,1,49152]{2,1,0:T(1,128)S(1)} %all-to-all-done.2), kind=kLoop, calls=%fused_computation.11 | loop fusion | flops 786432 | bytes 6291456 | tf_op jit(solution)/shard_map/mul | solution.py:96
  232.9 0.0 copy-start.1
  232.9 3.5 mul.85
  236.4 106.7 %all-reduce.11.cloned.1.call-done = (f32[256,256]{1,0:T(8,128)}, f32[3072,256]{1,0:T(8,128)}) async-done(((f32[256,256]{1,0:T(8,128)}, f32[3072,256]{1,0:T(8,128)}), (f32[256,256]{1,0:T(8,128)}, f32[3072,256]{1,0:T(8,128)})) %all-reduce.11.cloned.1.call-update) | async-done | bytes 3407888 | tf_op jit(solution)/shard_map/psum | solution.py:83
  343.1 0.0 copy-done.1
  343.1 5.4 %fusion.1 = f32[3072,256]{1,0:T(8,128)S(1)} fusion(f32[256,256]{1,0:T(8,128)} %get-tuple-element.4, f32[3072,256]{1,0:T(8,128)S(1)} %copy-done.1, f32[3072,256]{1,0:T(8,128)} %get-tuple-element.5, f32[3072,256]{1,0:T(8,128)} %mul.85, f32[3072]{0:T(1024)S(1)} %mul.92), kind=kOutput, calls=%fused_computation.6 | convolution fusion | flops 2419851264 | bytes 12857344 | tf_op jit(solution)/shard_map/dot_general | solution.py:93
  348.6 0.0 copy-start
  348.6 9.7 %fusion.9 = f32[256,2304]{1,0:T(8,128)} fusion(bf16[3072,2304]{1,0:T(8,128)(2,1)} %param.5, f32[3072,256]{1,0:T(8,128)S(1)} %fusion.1), kind=kOutput, calls=%fused_computation.17 | convolution fusion | flops 3624665088 | bytes 19660800 | tf_op jit(solution)/shard_map/dot_general | solution.py:99
  358.3 0.0 copy-done
  358.3 0.0 copy-start.2
  358.3 1.3 fusion.7
  359.6 0.0 all-reduce.9.cloned.1.call-update
  359.6 147.9 %all-reduce.9.cloned.1.call-done = (f32[256,256]{1,0:T(8,128)}, f32[256,2304]{1,0:T(8,128)}) async-done(((f32[256,256]{1,0:T(8,128)}, f32[256,2304]{1,0:T(8,128)}), (f32[256,256]{1,0:T(8,128)}, f32[256,2304]{1,0:T(8,128)})) %all-reduce.9.cloned.1.call-update) | async-done | bytes 2621456 | tf_op jit(solution)/shard_map/psum | solution.py:101
  507.5 0.0 copy-done.2
  507.5 5.4 %convolution_divide_fusion = f32[256,2304]{1,0:T(8,128)} fusion(f32[256,256]{1,0:T(8,128)} %get-tuple-element.2, f32[256,2304]{1,0:T(8,128)S(1)} %copy-done.2, f32[256,2304]{1,0:T(8,128)} %get-tuple-element.3), kind=kOutput, calls=%fused_computation.5 | convolution fusion | flops 1813118976 | bytes 7340032 | tf_op jit(solution)/shard_map/dot_general | solution.py:102
  (7 shorter events, 0.1 us)
Async XLA Ops:
  8.6 23.5 %all-to-all-start = ((f32[16,1,192]{2,1,0:T(1,128)}), f32[16,1,192]{2,1,0:T(1,128)S(1)}, u32[]{:S(2)}, u32[]{:S(2)}) async-start(f32[16,1,192]{2,1,0:T(1,128)} %all_to_all.24), calls=%async_computation | async-start | bytes 32768 | tf_op jit(solution)/shard_map/all_to_all | solution.py:42
  18.6 32.8 %collective-permute-start.2 = (f32[256]{0:T(256)S(1)}, f32[256]{0:T(256)S(1)}, u32[]{:S(2)}, u32[]{:S(2)}) collective-permute-start(f32[256]{0:T(256)S(1)} %bitcast.40), channel_id=1, source_target_pairs={{1,0},{2,1},{3,2},{4,3},{5,4},{6,5},{7,6},{8,7},{9,8},{10,9},{11,1... | collective-permute-start | bytes 3080 | tf_op jit(solution)/shard_map/ppermute | solution.py:13
  20.6 30.8 %collective-permute-start.3 = (f32[256]{0:T(256)S(1)}, f32[256]{0:T(256)S(1)}, u32[]{:S(2)}, u32[]{:S(2)}) collective-permute-start(f32[256]{0:T(256)S(1)} %bitcast.39), channel_id=1, source_target_pairs={{0,1},{1,2},{2,3},{3,4},{4,5},{5,6},{6,7},{7,8},{8,9},{9,10},{10,1... | collective-permute-start | bytes 3080 | tf_op jit(solution)/shard_map/ppermute | solution.py:13
  32.1 47.6 %all-to-all-start.1 = ((f32[16,1,49152]{2,1,0:T(1,128)}), f32[16,1,49152]{2,1,0:T(1,128)S(1)}, u32[]{:S(2)}, u32[]{:S(2)}) async-start(f32[16,1,49152]{2,1,0:T(1,128)} %all_to_all.26), calls=%async_computation.1 | async-start | bytes 6291456 | tf_op jit(solution)/shard_map/all_to_all | solution.py:41
  40.0 11.4 %copy-start.3 = (s32[12,256]{1,0:T(8,128)S(1)}, s32[12,256]{1,0:T(8,128)}, u32[]{:S(2)}) copy-start(s32[12,256]{1,0:T(8,128)} %param.9) | copy-start | bytes 36868
  79.7 73.8 %all-to-all-start.3 = ((f32[16,1,192]{2,1,0:T(1,128)}), f32[16,1,192]{2,1,0:T(1,128)S(1)}, u32[]{:S(2)}, u32[]{:S(2)}) async-start(f32[16,1,192]{2,1,0:T(1,128)} %all_to_all.30), calls=%async_computation.3 | async-start | bytes 32768 | tf_op jit(solution)/shard_map/all_to_all | solution.py:65
  123.1 9.2 %collective-permute-start = (f32[256,256]{1,0:T(8,128)S(1)}, f32[256,256]{1,0:T(8,128)S(1)}, u32[]{:S(2)}, u32[]{:S(2)}) collective-permute-start(f32[256,256]{1,0:T(8,128)S(1)} %get-tuple-element.9), channel_id=1, source_target_pairs={{1,0},{2,1},{3,2},{4,3},{5,4},{6,5},{7,6},{8,7},{9,8},{10,9},{11,1... | collective-permute-start | bytes 786440 | tf_op jit(solution)/shard_map/ppermute | solution.py:13
  125.1 8.3 %collective-permute-start.1 = (f32[256,256]{1,0:T(8,128)S(1)}, f32[256,256]{1,0:T(8,128)S(1)}, u32[]{:S(2)}, u32[]{:S(2)}) collective-permute-start(f32[256,256]{1,0:T(8,128)S(1)} %get-tuple-element.8), channel_id=1, source_target_pairs={{0,1},{1,2},{2,3},{3,4},{4,5},{5,6},{6,7},{7,8},{8,9},{9,10},{10,1... | collective-permute-start | bytes 786440 | tf_op jit(solution)/shard_map/ppermute | solution.py:13
  153.5 68.7 %all-to-all-start.2 = ((f32[16,1,49152]{2,1,0:T(1,128)}), f32[16,1,49152]{2,1,0:T(1,128)S(1)}, u32[]{:S(2)}, u32[]{:S(2)}) async-start(f32[16,1,49152]{2,1,0:T(1,128)} %all_to_all.32), calls=%async_computation.2 | async-start | bytes 6291456 | tf_op jit(solution)/shard_map/all_to_all | solution.py:64
  162.7 180.4 %all-reduce.11.cloned.1.call-start = ((), (), s32[]{:S(2)}) async-start(), calls=%async_computation.5 | async-start | bytes 6815744 | tf_op jit(solution)/shard_map/psum | solution.py:83
  166.4 341.2 %all-reduce.9.cloned.1.call-start = ((), (), s32[]{:S(2)}) async-start(), calls=%async_computation.4 | async-start | bytes 5242880 | tf_op jit(solution)/shard_map/psum | solution.py:101
  232.9 110.2 %copy-start.1 = (f32[3072,256]{1,0:T(8,128)S(1)}, f32[3072,256]{1,0:T(8,128)}, u32[]{:S(2)}) copy-start(f32[3072,256]{1,0:T(8,128)} %param.6) | copy-start | bytes 9437188
  348.6 9.7 %copy-start = (f32[3072,256]{1,0:T(8,128)}, f32[3072,256]{1,0:T(8,128)S(1)}, u32[]{:S(2)}) copy-start(f32[3072,256]{1,0:T(8,128)S(1)} %fusion.1) | copy-start | bytes 9437188
  358.3 149.2 %copy-start.2 = (f32[256,2304]{1,0:T(8,128)S(1)}, f32[256,2304]{1,0:T(8,128)}, u32[]{:S(2)}) copy-start(f32[256,2304]{1,0:T(8,128)} %param.7) | copy-start | bytes 7077892
Sparse Core Ops, SparseCore 0:
  166.7 176.3 all-reduce.10
  359.7 147.7 all-reduce.8
where the time goes:
time: 526 us; the launch traced here: 520 us
  waiting for transfers between devices  323 us (61%)
  local copies, waits for them, and re-layouts  76.3 us (15%)
  starting transfers between devices  45.3 us (9%)
  matrix products  36.8 us (7%)
  other arithmetic  24.3 us (5%)
  between operations  14.4 us (3%)
    psum x1, waiting for transfers between devices, on_device(): cross, fac_gram = lax.psum((cross_part, gram_part), 'bin')  148 us
    psum x1, waiting for transfers between devices, on_device(): lax.psum(lax.dot_general(load_bf, load_bf, right_dims, preferred_element_...  107 us
    all_to_all x1, waiting for transfers between devices, stencil_term(): lax.all_to_all(back_send, 'bin', split_axis=0, concat_axis=0, tiled=True)  55.6 us
    scatter x1, local copies, waits for them, and re-layouts, stencil_term(): tile_rows = jnp.zeros((row_count, col_width), jnp.float32).at[tile_slot]....  24.1 us
    gather x1, local copies, waits for them, and re-layouts, stencil_term(): back_degree = degree_grid.reshape(row_count)[tile_slot]  17.4 us
    ppermute x4, starting transfers between devices, passed_along(): return lax.ppermute(block, axis, route)  14.1 us
    gather x1, local copies, waits for them, and re-layouts, stencil_term(): smooth_grid.reshape(row_count, col_width)[tile_slot]  12.3 us
    dot_general x1, matrix products, on_device(): lax.dot_general(counts, load_bf, right_dims, preferred_element_type=jnp.f...  11.4 us
  transfers between devices with their start and end apart: 10, of which 6 were waited for; matrix products, arithmetic and copies ran while one was open for 19% of the time, Pallas kernels for 0%

commit v1 on v0

--- a/solution.py
+++ b/solution.py
@@ -76,30 +76,40 @@
 
 def on_device(counts, factors, loadings, position, edge_codes):
     bin_count = lax.axis_size("bin")
+    gene_count = lax.axis_size("gene")
     row_count, width_all = factors.shape
     group_size = row_count // bin_count
+    width = width_all // gene_count
+    k_rows = width_all // bin_count
+    gene_at = lax.axis_index("gene")
+    bin_at = lax.axis_index("bin")
     load_bf = loadings.astype(jnp.bfloat16)
     right_dims = (((1,), (1,)), ((), ()))
-    load_gram = lax.psum(
-        lax.dot_general(load_bf, load_bf, right_dims, preferred_element_type=jnp.float32), "gene"
+    numer_part = lax.dot_general(counts, load_bf, right_dims, preferred_element_type=jnp.float32)
+    gram_part = lax.dot_general(load_bf, load_bf, right_dims, preferred_element_type=jnp.float32)
+    numer, load_gram = lax.psum_scatter(
+        (numer_part, gram_part), "gene", scatter_dimension=1, tiled=True
     )
-    payload = factors.reshape(bin_count, group_size * width_all)
-    smooth, degree = stencil_term(payload, width_all, position, edge_codes)
+    own = lax.dynamic_slice_in_dim(factors, gene_at * width, width, 1)
+    payload = own.reshape(bin_count, group_size * width)
+    smooth, degree = stencil_term(payload, width, position, edge_codes)
     penalty = float(G * K) / 64.0
-    numer = lax.psum(
-        lax.dot_general(counts, load_bf, right_dims, preferred_element_type=jnp.float32), "gene"
-    )
     denom = (
         jnp.dot(factors, load_gram, precision=lax.Precision.HIGHEST)
-        + penalty * degree[:, None] * factors
+        + penalty * degree[:, None] * own
     )
-    factors_new = factors * (numer + penalty * smooth) / denom
+    new_own = own * (numer + penalty * smooth) / denom
+    factors_new = lax.all_gather(new_own, "gene", axis=1, tiled=True)
     fac_bf = factors_new.astype(jnp.bfloat16)
     left_dims = (((0,), (0,)), ((), ()))
     cross_part = lax.dot_general(fac_bf, counts, left_dims, preferred_element_type=jnp.float32)
-    gram_part = lax.dot_general(fac_bf, fac_bf, left_dims, preferred_element_type=jnp.float32)
-    cross, fac_gram = lax.psum((cross_part, gram_part), "bin")
-    loadings_new = loadings * cross / jnp.dot(fac_gram, loadings, precision=lax.Precision.HIGHEST)
+    fgram_part = lax.dot_general(fac_bf, fac_bf, left_dims, preferred_element_type=jnp.float32)
+    cross, fac_gram = lax.psum_scatter(
+        (cross_part, fgram_part), "bin", scatter_dimension=0, tiled=True
+    )
+    own_load = lax.dynamic_slice_in_dim(loadings, bin_at * k_rows, k_rows, 0)
+    new_load = own_load * cross / jnp.dot(fac_gram, loadings, precision=lax.Precision.HIGHEST)
+    loadings_new = lax.all_gather(new_load, "bin", axis=0, tiled=True)
     return (factors_new, loadings_new)
 
 

time: 526 us -> 451 us (0.86)
  waiting for transfers between devices: 323 us -> 250 us
  other arithmetic: 24.3 us -> 9.34 us
  local copies, waits for them, and re-layouts: 76.3 us -> 89.9 us
    psum x2 -> x0, waiting for transfers between devices: 255 us -> none  [the longest x1 148 us: on_device(): cross, fac_gram = lax.psum((cross_part, gram_part), 'bin')]
    reduce_scatter x0 -> x3, waiting for transfers between devices: none -> 129 us  [the longest x2 129 us: on_device(): lax.psum_scatter((cross_part, fgram_part), 'bin', scatter_dimension=0, ti...]
    all_gather x0 -> x2, waiting for transfers between devices: none -> 115 us  [the longest x1 68.6 us: on_device(): factors_new = lax.all_gather(new_own, 'gene', axis=1, tiled=True)]
    all_to_all x1, waiting for transfers between devices: 55.6 us -> 5.8 us  [stencil_term(): lax.all_to_all(back_send, 'bin', split_axis=0, concat_axis=0, tiled=True)]
    scatter x1, local copies, waits for them, and re-layouts: 24.1 us -> 9.63 us  [stencil_term(): tile_rows = jnp.zeros((row_count, col_width), jnp.float32).at[tile_slot]....]
    gather x1, local copies, waits for them, and re-layouts: 17.4 us -> 30.6 us  [stencil_term(): back_degree = degree_grid.reshape(row_count)[tile_slot]]
    unnamed x8 -> x25, local copies, waits for them, and re-layouts: 0.02 us -> 11.9 us
    all_to_all x1, waiting for transfers between devices: 9.92 us -> 0.01 us  [stencil_term(): lax.all_to_all(payload, 'bin', split_axis=0, concat_axis=0, tiled=True)]
  transfers between devices with their start and end apart: 10 -> 14, of which waited for: 6 -> 7; matrix products, arithmetic and copies ran while one was open for 19% -> 24% of each run, Pallas kernels for 0% -> 0%
where the time goes in v1:
time: 451 us; the launch traced here: 449 us
  waiting for transfers between devices  250 us (55%)
  local copies, waits for them, and re-layouts  89.9 us (20%)
  starting transfers between devices  47 us (10%)
  matrix products  38.7 us (9%)
  between operations  14.3 us (3%)
  other arithmetic  9.34 us (2%)
    reduce_scatter x2, waiting for transfers between devices, on_device(): lax.psum_scatter((cross_part, fgram_part), 'bin', scatter_dimension=0, ti...  129 us
    all_gather x1, waiting for transfers between devices, on_device(): factors_new = lax.all_gather(new_own, 'gene', axis=1, tiled=True)  68.6 us
    all_gather x1, waiting for transfers between devices, on_device(): loadings_new = lax.all_gather(new_load, 'bin', axis=0, tiled=True)  46.4 us
    gather x1, local copies, waits for them, and re-layouts, stencil_term(): back_degree = degree_grid.reshape(row_count)[tile_slot]  30.6 us
    ppermute x4, starting transfers between devices, passed_along(): return lax.ppermute(block, axis, route)  14.2 us
    gather x1, local copies, waits for them, and re-layouts, stencil_term(): smooth_grid.reshape(row_count, col_width)[tile_slot]  12.2 us
    unnamed x25, local copies, waits for them, and re-layouts  11.9 us
    dot_general x1, matrix products, on_device(): lax.dot_general(counts, load_bf, right_dims, preferred_element_type=jnp.f...  11.2 us
  transfers between devices with their start and end apart: 14, of which 7 were waited for; matrix products, arithmetic and copies ran while one was open for 24% of the time, Pallas kernels for 0%

profile of v1, /device:TPU:1, one launch (start us, length us, event | category | flops | bytes accessed | tf_op | source)
XLA Modules:
  0.0 449.5 jit_solution(1883265635426053663)
XLA Ops:
  7.2 0.0 reduce-scatter.13.cloned.1.call-start
  7.2 3.8 convolution_bitcast_fusion.1
  11.0 0.0 reduce-scatter.13.cloned.1.call-update
  11.0 0.0 reduce-scatter.7.cloned.1.call-start
  11.1 11.2 %fusion.9 = f32[3072,256]{0,1:T(8,128)} fusion(bf16[3072,2304]{1,0:T(8,128)(2,1)} %param.5, f32[256,2304]{1,0:T(8,128)} %param.7), kind=kOutput, calls=%fused_computation.15 | convolution fusion | flops 3624468480 | bytes 19660800 | tf_op jit(solution)/shard_map/dot_general | solution.py:88
  22.3 0.0 reduce-scatter.7.cloned.1.call-update
  22.3 0.7 copy-done.9
  23.0 0.7 all_to_all.24
  23.7 9.3 %all-to-all-start = ((f32[16,1,192]{2,1,0:T(1,128)}), f32[16,1,192]{2,1,0:T(1,128)S(1)}, u32[]{:S(2)}, u32[]{:S(2)}) async-start(f32[16,1,192]{2,1,0:T(1,128)} %all_to_all.24), calls=%async_computation.1 | async-start | bytes 32768 | tf_op jit(solution)/shard_map/all_to_all | solution.py:42
  33.0 0.6 copy-done.2
  33.6 5.0 %collective-permute-start.3 = (f32[256]{0:T(256)S(1)}, f32[256]{0:T(256)S(1)}, u32[]{:S(2)}, u32[]{:S(2)}) collective-permute-start(f32[256]{0:T(256)S(1)} %bitcast.48), channel_id=1, source_target_pairs={{0,1},{1,2},{2,3},{3,4},{4,5},{5,6},{6,7},{7,8},{8,9},{9,10},{10,1... | collective-permute-start | bytes 3080 | tf_op jit(solution)/shard_map/ppermute | solution.py:13
  38.6 1.9 collective-permute-start.2
  40.5 0.1 fusion.23
  40.6 1.6 constant_dynamic-slice_fusion
  42.2 2.8 all_to_all.32
  45.1 0.3 collective-permute-done.2
  45.4 0.1 fusion.18
  45.5 0.6 copy-done.6
  46.1 7.0 %all-to-all-start.1 = ((f32[16,1,6144]{2,1,0:T(1,128)}), f32[16,1,6144]{2,1,0:T(1,128)S(1)}, u32[]{:S(2)}, u32[]{:S(2)}) async-start(f32[16,1,6144]{2,1,0:T(1,128)} %all_to_all.32), calls=%async_computation.2 | async-start | bytes 786432 | tf_op jit(solution)/shard_map/all_to_all | solution.py:41
  53.1 1.4 subtract_reduce_fusion
  54.5 1.4 sub.18
  55.9 0.7 compare_select_fusion
  56.6 0.6 copy-done.7
  57.2 0.6 broadcast_clamp_fusion
  57.8 30.6 %gather_fusion.1 = f32[3072]{0:T(1024)} fusion(f32[3072]{0:T(1024)S(1)} %reshape.142, s32[3072]{0:T(1024)} %broadcast_clamp_fusion), kind=kCustom, calls=%fused_computation.1 | custom fusion | bytes 36864 | tf_op jit(solution)/shard_map/gather | solution.py:58
  88.4 1.4 all_to_all.30
  89.8 7.2 %all-to-all-start.3 = ((f32[16,1,192]{2,1,0:T(1,128)}), f32[16,1,192]{2,1,0:T(1,128)}, u32[]{:S(2)}, u32[]{:S(2)}) async-start(f32[16,1,192]{2,1,0:T(1,128)} %all_to_all.30), calls=%async_computation.4 | async-start | bytes 32768 | tf_op jit(solution)/shard_map/all_to_all | solution.py:65
  97.1 1.8 reduce.1
  98.9 2.7 reshape.163
  101.6 9.6 %scatter_custom_fusion = f32[3072,32]{1,0:T(8,128)} fusion(s32[3072]{0:T(1024)} %bitcast.42, f32[3072,32]{1,0:T(8,128)} %reshape.163, f32[]{:T(128)} %constant.7.clone.1), kind=kCustom, calls=%fused_computation.12 | custom fusion | bytes 393728 | tf_op jit(solution)/shard_map/scatter | solution.py:49
  111.2 2.9 copy.58
  114.1 1.1 broadcast_multiply_fusion
  115.2 2.1 collective-permute-start
  117.3 5.2 %collective-permute-start.1 = (f32[256,32]{0,1:T(8,128)S(1)}, f32[256,32]{0,1:T(8,128)S(1)}, u32[]{:S(2)}, u32[]{:S(2)}) collective-permute-start(f32[256,32]{0,1:T(8,128)S(1)} %bitcast.44), channel_id=1, source_target_pairs={{0,1},{1,2},{2,3},{3,4},{4,5},{5,6},{6,7},{7,8},{8,9},{9,10},{10,1... | collective-permute-start | bytes 98312 | tf_op jit(solution)/shard_map/ppermute | solution.py:13
  122.5 0.2 fusion.20
  122.7 0.1 fusion.22
  122.8 0.0 collective-permute-done
  122.8 0.5 collective-permute-done.1
  123.4 1.1 fusion.13
  124.5 2.7 copy.52
  127.2 12.2 %gather_fusion = f32[3072,32]{1,0:T(8,128)} fusion(f32[3072,32]{1,0:T(8,128)} %bitcast.39, s32[3072]{0:T(1024)S(1)} %copy-done.4), kind=kCustom, calls=%fused_computation | custom fusion | bytes 798720 | tf_op jit(solution)/shard_map/gather | solution.py:60
  139.4 2.8 all_to_all.33
  142.3 9.0 %all-to-all-start.2 = ((f32[16,1,6144]{2,1,0:T(1,128)}), f32[16,1,6144]{2,1,0:T(1,128)S(1)}, u32[]{:S(2)}, u32[]{:S(2)}) async-start(f32[16,1,6144]{2,1,0:T(1,128)} %all_to_all.33), calls=%async_computation.3 | async-start | bytes 786432 | tf_op jit(solution)/shard_map/all_to_all | solution.py:64
  151.3 0.0 all-gather.3.cloned.1.call-start
  151.3 2.6 copy.61
  153.9 0.8 multiply_reduce_fusion.1
  154.7 0.7 mul.99
  155.4 5.8 %all-to-all-done.2 = f32[16,1,6144]{2,1,0:T(1,128)S(1)} async-done(((f32[16,1,6144]{2,1,0:T(1,128)}), f32[16,1,6144]{2,1,0:T(1,128)S(1)}, u32[]{:S(2)}, u32[]{:S(2)}) %all-to-all-start.2) | async-done | bytes 393248 | tf_op jit(solution)/shard_map/all_to_all | solution.py:64
  161.2 1.8 multiply_reduce_fusion
  163.0 2.7 mul.92
  165.7 2.6 copy.54
  168.3 4.8 %fusion.1 = f32[3072,32]{0,1:T(8,128)} fusion(f32[3072,256]{1,0:T(8,128)S(1)} %copy-done, f32[3072,32]{0,1:T(8,128)S(1)} %copy-done.1, f32[3072,32]{0,1:T(8,128)} %reduce-scatter.7.cloned.1.call-done, f32[3072,32]{0,1:T(8,128)} %copy.54, f32[3072]{0:T(1024)S(1)} %copy-done.8, f32[32,256]{1,0:T(8,128)} %reduce-scatter.13.cloned.1.call-done), kind=kOutput, calls=%fused_computation.5 | convolution fusion | flops 302481408 | bytes 4763648 | tf_op jit(solution)/shard_map/dot_general | solution.py:98
  173.2 0.0 reduce-scatter.11.cloned.1.call-start
  173.2 68.6 %all-gather.3.cloned.1.call-done = f32[3072,256]{0,1:T(8,128)} async-done(((f32[3072,32]{0,1:T(8,128)}), f32[3072,256]{0,1:T(8,128)}) %all-gather.3.cloned.1.call-update) | async-done | bytes 3145744 | tf_op jit(solution)/shard_map/all_gather | solution.py:102
  241.8 4.2 fusion.2
  246.0 0.0 reduce-scatter.9.cloned.1.call-start
  246.1 11.2 %fusion.4 = f32[256,2304]{1,0:T(8,128)} fusion(bf16[3072,2304]{1,0:T(8,128)(2,1)} %param.5, f32[3072,256]{0,1:T(8,128)} %all-gather.3.cloned.1.call-done), kind=kOutput, calls=%fused_computation.10 | convolution fusion | flops 3624665088 | bytes 19660800 | tf_op jit(solution)/shard_map/dot_general | solution.py:105
  257.3 0.0 all-gather.5.cloned.1.call-start
  257.3 52.2 %reduce-scatter.11.cloned.1.call-done = f32[16,256]{1,0:T(8,128)} async-done(((f32[256,256]{1,0:T(8,128)}), f32[16,256]{1,0:T(8,128)}) %reduce-scatter.11.cloned.1.call-update) | async-done | bytes 16400 | tf_op jit(solution)/shard_map/reduce_scatter | solution.py:107
  309.6 76.3 %reduce-scatter.9.cloned.1.call-done = f32[16,2304]{1,0:T(8,128)} async-done(((f32[256,2304]{1,0:T(8,128)}), f32[16,2304]{1,0:T(8,128)}) %reduce-scatter.9.cloned.1.call-update) | async-done | bytes 147472 | tf_op jit(solution)/shard_map/reduce_scatter | solution.py:107
  385.9 3.5 convolution_divide_fusion
  389.5 3.5 copy.56
  393.0 46.4 %all-gather.5.cloned.1.call-done = f32[256,2304]{1,0:T(8,128)} async-done(((f32[16,2304]{1,0:T(8,128)}), f32[256,2304]{1,0:T(8,128)}) %all-gather.5.cloned.1.call-update) | async-done | bytes 2359312 | tf_op jit(solution)/shard_map/all_gather | solution.py:112
  439.4 3.2 copy.69
  (36 shorter events, 0.2 us)
Async XLA Ops:
  7.2 33.5 %copy-start = (f32[3072,256]{1,0:T(8,128)S(1)}, f32[3072,256]{1,0:T(8,128)}, u32[]{:S(2)}) copy-start(f32[3072,256]{1,0:T(8,128)} %param.6) | copy-start | bytes 9437188
  7.2 161.1 %reduce-scatter.13.cloned.1.call-start = ((), (), s32[]{:S(2)}) async-start(), calls=%async_computation.13 | async-start | bytes 294912
  11.0 157.3 %reduce-scatter.7.cloned.1.call-start = ((), (), s32[]{:S(2)}) async-start(), calls=%async_computation.8 | async-start | bytes 3538944 | tf_op jit(solution)/shard_map/reduce_scatter | solution.py:90
  22.3 0.7 copy-start.9
  22.3 10.7 %copy-start.5 = (s32[12,256]{1,0:T(8,128)S(1)}, s32[12,256]{1,0:T(8,128)}, u32[]{:S(2)}) copy-start(s32[12,256]{1,0:T(8,128)} %param.9) | copy-start | bytes 36868
  23.7 21.8 %all-to-all-start = ((f32[16,1,192]{2,1,0:T(1,128)}), f32[16,1,192]{2,1,0:T(1,128)S(1)}, u32[]{:S(2)}, u32[]{:S(2)}) async-start(f32[16,1,192]{2,1,0:T(1,128)} %all_to_all.24), calls=%async_computation.1 | async-start | bytes 32768 | tf_op jit(solution)/shard_map/all_to_all | solution.py:42
  33.0 0.6 copy-start.2
  33.6 11.5 %collective-permute-start.3 = (f32[256]{0:T(256)S(1)}, f32[256]{0:T(256)S(1)}, u32[]{:S(2)}, u32[]{:S(2)}) collective-permute-start(f32[256]{0:T(256)S(1)} %bitcast.48), channel_id=1, source_target_pairs={{0,1},{1,2},{2,3},{3,4},{4,5},{5,6},{6,7},{7,8},{8,9},{9,10},{10,1... | collective-permute-start | bytes 3080 | tf_op jit(solution)/shard_map/ppermute | solution.py:13
  38.6 6.8 %collective-permute-start.2 = (f32[256]{0:T(256)S(1)}, f32[256]{0:T(256)S(1)}, u32[]{:S(2)}, u32[]{:S(2)}) collective-permute-start(f32[256]{0:T(256)S(1)} %bitcast.47), channel_id=1, source_target_pairs={{1,0},{2,1},{3,2},{4,3},{5,4},{6,5},{7,6},{8,7},{9,8},{10,9},{11,1... | collective-permute-start | bytes 3080 | tf_op jit(solution)/shard_map/ppermute | solution.py:13
  45.5 0.6 copy-start.6
  46.1 43.8 %all-to-all-start.1 = ((f32[16,1,6144]{2,1,0:T(1,128)}), f32[16,1,6144]{2,1,0:T(1,128)S(1)}, u32[]{:S(2)}, u32[]{:S(2)}) async-start(f32[16,1,6144]{2,1,0:T(1,128)} %all_to_all.32), calls=%async_computation.2 | async-start | bytes 786432 | tf_op jit(solution)/shard_map/all_to_all | solution.py:41
  56.6 0.6 copy-start.7
  89.8 52.4 %all-to-all-start.3 = ((f32[16,1,192]{2,1,0:T(1,128)}), f32[16,1,192]{2,1,0:T(1,128)}, u32[]{:S(2)}, u32[]{:S(2)}) async-start(f32[16,1,192]{2,1,0:T(1,128)} %all_to_all.30), calls=%async_computation.4 | async-start | bytes 32768 | tf_op jit(solution)/shard_map/all_to_all | solution.py:65
  98.9 15.2 %copy-start.3 = (f32[12,256]{1,0:T(8,128)S(1)}, f32[12,256]{1,0:T(8,128)}, u32[]{:S(2)}) copy-start(f32[12,256]{1,0:T(8,128)} %copy-done.2) | copy-start | bytes 36868
  115.2 7.6 %collective-permute-start = (f32[256,32]{0,1:T(8,128)S(1)}, f32[256,32]{0,1:T(8,128)S(1)}, u32[]{:S(2)}, u32[]{:S(2)}) collective-permute-start(f32[256,32]{0,1:T(8,128)S(1)} %bitcast.43), channel_id=1, source_target_pairs={{1,0},{2,1},{3,2},{4,3},{5,4},{6,5},{7,6},{8,7},{9,8},{10,9},{11,1... | collective-permute-start | bytes 98312 | tf_op jit(solution)/shard_map/ppermute | solution.py:13
  117.3 6.0 %collective-permute-start.1 = (f32[256,32]{0,1:T(8,128)S(1)}, f32[256,32]{0,1:T(8,128)S(1)}, u32[]{:S(2)}, u32[]{:S(2)}) collective-permute-start(f32[256,32]{0,1:T(8,128)S(1)} %bitcast.44), channel_id=1, source_target_pairs={{0,1},{1,2},{2,3},{3,4},{4,5},{5,6},{6,7},{7,8},{8,9},{9,10},{10,1... | collective-permute-start | bytes 98312 | tf_op jit(solution)/shard_map/ppermute | solution.py:13
  123.3 3.8 copy-start.4
  142.3 18.9 %all-to-all-start.2 = ((f32[16,1,6144]{2,1,0:T(1,128)}), f32[16,1,6144]{2,1,0:T(1,128)S(1)}, u32[]{:S(2)}, u32[]{:S(2)}) async-start(f32[16,1,6144]{2,1,0:T(1,128)} %all_to_all.33), calls=%async_computation.3 | async-start | bytes 786432 | tf_op jit(solution)/shard_map/all_to_all | solution.py:64
  151.3 90.5 %all-gather.3.cloned.1.call-start = ((), (), s32[]{:S(2)}) async-start(), calls=%async_computation.9 | async-start | bytes 3538944 | tf_op jit(solution)/shard_map/all_gather | solution.py:102
  155.4 12.9 %copy-start.8 = (f32[3072]{0:T(1024)S(1)}, f32[3072]{0:T(1024)}, u32[]{:S(2)}) copy-start(f32[3072]{0:T(1024)} %mul.99) | copy-start | bytes 36868
  163.0 5.3 %copy-start.1 = (f32[3072,32]{0,1:T(8,128)S(1)}, f32[3072,32]{0,1:T(8,128)}, u32[]{:S(2)}) copy-start(f32[3072,32]{0,1:T(8,128)} %copy.61) | copy-start | bytes 1179652
  173.2 136.4 %reduce-scatter.11.cloned.1.call-start = ((), (), s32[]{:S(2)}) async-start(), calls=%async_computation.11 | async-start | bytes 278528 | tf_op jit(solution)/shard_map/reduce_scatter | solution.py:107
  246.0 139.9 %reduce-scatter.9.cloned.1.call-start = ((), (), s32[]{:S(2)}) async-start(), calls=%async_computation.10 | async-start | bytes 2506752 | tf_op jit(solution)/shard_map/reduce_scatter | solution.py:107
  257.3 182.1 %all-gather.5.cloned.1.call-start = ((), (), s32[]{:S(2)}) async-start(), calls=%async_computation.12 | async-start | bytes 2506752 | tf_op jit(solution)/shard_map/all_gather | solution.py:112
Sparse Core Ops, SparseCore 0:
  11.1 35.2 reduce-scatter.12
  49.5 75.7 reduce-scatter.6
  173.3 68.5 all-gather.2
  246.4 63.1 reduce-scatter.10
  314.5 71.3 reduce-scatter.8
  389.6 49.7 all-gather.4

commit v2 on v1

--- a/solution.py
+++ b/solution.py
@@ -31,47 +31,54 @@
     return beside + 0.5 * (lower + upper)
 
 
-def stencil_term(payload, col_width, position, edge_codes):
+def split_three(values):
+    high = lax.reduce_precision(values, exponent_bits=8, mantissa_bits=7)
+    rest = values - high
+    mid = lax.reduce_precision(rest, exponent_bits=8, mantissa_bits=7)
+    low = rest - mid
+    return jnp.concatenate([high, mid, low], 1).astype(jnp.bfloat16)
+
+
+def join_three(parts, width):
+    return (parts[:, :width] + parts[:, width : 2 * width]) + parts[:, 2 * width :]
+
+
+def stencil_term(own, position, edge_codes):
     bin_count = lax.axis_size("bin")
-    row_count = position.shape[0]
+    row_count, width = own.shape
     group_size = row_count // bin_count
     grid_rows, grid_cols = edge_codes.shape
-    pos_float = position.astype(jnp.float32).reshape(bin_count, group_size)
-    got_rows, got_pos = (
-        lax.all_to_all(payload, "bin", split_axis=0, concat_axis=0, tiled=True),
-        lax.all_to_all(pos_float, "bin", split_axis=0, concat_axis=0, tiled=True),
+    payload = jnp.concatenate([own, position.astype(jnp.float32)[:, None]], 1)
+    got = lax.all_to_all(
+        payload.reshape(bin_count, group_size * (width + 1)), "bin", 0, 0, tiled=True
+    ).reshape(row_count, width + 1)
+    tile_slot = got[:, width].astype(jnp.int32) - lax.axis_index("bin") * row_count
+    cells = lax.broadcasted_iota(jnp.int32, (row_count, row_count), 1)
+    onehot = (tile_slot[:, None] == cells).astype(jnp.bfloat16)
+    placed = lax.dot_general(
+        onehot, split_three(got[:, :width]), (((0,), (0,)), ((), ())),
+        preferred_element_type=jnp.float32,
     )
-    tile_slot = got_pos.reshape(row_count).astype(jnp.int32) - lax.axis_index("bin") * row_count
+    tile_rows = join_three(placed, width)
     cell_scale = edge_codes.astype(jnp.float32) / 8.0
-    tile_rows = (
-        jnp.zeros((row_count, col_width), jnp.float32)
-        .at[tile_slot]
-        .set(got_rows.reshape(row_count, col_width))
-    )
-    weighted = cell_scale[:, :, None] * tile_rows.reshape(grid_rows, grid_cols, col_width)
+    weighted = cell_scale[:, :, None] * tile_rows.reshape(grid_rows, grid_cols, width)
     rim_last, rim_first = (weighted[-1], weighted[0])
     upper_rows, upper_scale = passed_along((rim_last, cell_scale[-1]), "bin", 1)
     lower_rows, lower_scale = passed_along((rim_first, cell_scale[0]), "bin", -1)
     degree_grid = (
         cell_scale * neighbour_first(cell_scale[None], upper_scale[None], lower_scale[None])[0]
     )
-    back_degree = degree_grid.reshape(row_count)[tile_slot]
     smooth_grid = cell_scale[:, :, None] * neighbour_sum(weighted, upper_rows, lower_rows)
-    back_send = smooth_grid.reshape(row_count, col_width)[tile_slot].reshape(
-        bin_count, group_size * col_width
+    back = jnp.concatenate(
+        [smooth_grid.reshape(row_count, width), degree_grid.reshape(row_count, 1)], 1
     )
-    smooth, degree = (
-        lax.all_to_all(back_send, "bin", split_axis=0, concat_axis=0, tiled=True),
-        lax.all_to_all(
-            back_degree.reshape(bin_count, group_size),
-            "bin",
-            split_axis=0,
-            concat_axis=0,
-            tiled=True,
-        ),
+    back_rows = join_three(
+        jnp.dot(onehot, split_three(back), preferred_element_type=jnp.float32), width + 1
     )
-    smooth = smooth.reshape(row_count, col_width)
-    return (smooth, degree.reshape(row_count))
+    ret = lax.all_to_all(
+        back_rows.reshape(bin_count, group_size * (width + 1)), "bin", 0, 0, tiled=True
+    ).reshape(row_count, width + 1)
+    return (ret[:, :width], ret[:, width])
 
 
 def on_device(counts, factors, loadings, position, edge_codes):
@@ -87,12 +94,12 @@
     right_dims = (((1,), (1,)), ((), ()))
     numer_part = lax.dot_general(counts, load_bf, right_dims, preferred_element_type=jnp.float32)
     gram_part = lax.dot_general(load_bf, load_bf, right_dims, preferred_element_type=jnp.float32)
-    numer, load_gram = lax.psum_scatter(
-        (numer_part, gram_part), "gene", scatter_dimension=1, tiled=True
+    both = lax.psum_scatter(
+        jnp.concatenate([numer_part, gram_part], 0), "gene", scatter_dimension=1, tiled=True
     )
+    numer, load_gram = both[:row_count], both[row_count:]
     own = lax.dynamic_slice_in_dim(factors, gene_at * width, width, 1)
-    payload = own.reshape(bin_count, group_size * width)
-    smooth, degree = stencil_term(payload, width, position, edge_codes)
+    smooth, degree = stencil_term(own, position, edge_codes)
     penalty = float(G * K) / 64.0
     denom = (
         jnp.dot(factors, load_gram, precision=lax.Precision.HIGHEST)
@@ -104,9 +111,10 @@
     left_dims = (((0,), (0,)), ((), ()))
     cross_part = lax.dot_general(fac_bf, counts, left_dims, preferred_element_type=jnp.float32)
     fgram_part = lax.dot_general(fac_bf, fac_bf, left_dims, preferred_element_type=jnp.float32)
-    cross, fac_gram = lax.psum_scatter(
-        (cross_part, fgram_part), "bin", scatter_dimension=0, tiled=True
+    both_bin = lax.psum_scatter(
+        jnp.concatenate([cross_part, fgram_part], 1), "bin", scatter_dimension=0, tiled=True
     )
+    cross, fac_gram = both_bin[:, : cross_part.shape[1]], both_bin[:, cross_part.shape[1] :]
     own_load = lax.dynamic_slice_in_dim(loadings, bin_at * k_rows, k_rows, 0)
     new_load = own_load * cross / jnp.dot(fac_gram, loadings, precision=lax.Precision.HIGHEST)
     loadings_new = lax.all_gather(new_load, "bin", axis=0, tiled=True)

time: 451 us -> 375 us (0.83); the launches traced: 449 us -> 369 us
  waiting for transfers between devices: 250 us -> 187 us
  local copies, waits for them, and re-layouts: 89.9 us -> 50.9 us
  blocking collectives: 0 us -> 25.5 us
  starting transfers between devices: 47 us -> 24.2 us
  other arithmetic: 9.34 us -> 21.8 us
  matrix products: 38.7 us -> 45 us
    reduce_scatter x3 -> x1, waiting for transfers between devices: 129 us -> 71.9 us  [on_device(): lax.psum_scatter(jnp.concatenate([cross_part, fgram_part], 1), 'bin', sca...]
    gather x2 -> x0, local copies, waits for them, and re-layouts: 42.9 us -> none  [the longest x1 30.6 us: stencil_term(): back_degree = degree_grid.reshape(row_count)[tile_slot]]
    all_to_all x0 -> x1, blocking collectives: none -> 25.5 us  [stencil_term(): lax.all_to_all(back_rows.reshape(bin_count, group_size * (width + 1)), 'b...]
    all_to_all x4 -> x1, starting transfers between devices: 32.6 us -> 9.29 us  [stencil_term(): lax.all_to_all(payload.reshape(bin_count, group_size * (width + 1)), 'bin...]
    dot_general x0 -> x3, matrix products: none -> 18.5 us  [the longest x1 8.05 us: stencil_term(): jnp.dot(onehot, split_three(back), preferred_element_type=jnp.float32)]
    unnamed x25 -> x27, local copies, waits for them, and re-layouts: 11.9 us -> 22.6 us
    scatter x1 -> x0, local copies, waits for them, and re-layouts: 9.63 us -> none  [stencil_term(): tile_rows = jnp.zeros((row_count, col_width), jnp.float32).at[tile_slot]....]
    mul x4 -> x0, local copies, waits for them, and re-layouts: 8.68 us -> none  [the longest x2 5.31 us: on_device(): new_own = own * (numer + penalty * smooth) / denom]
  transfers between devices with their start and end apart: 14 -> 9, of which waited for: 7 -> 4; matrix products, arithmetic and copies ran while one was open for 24% -> 21% of each run, Pallas kernels for 0% -> 0%
where the time goes in v2:
time: 375 us; the launch traced here: 369 us
  waiting for transfers between devices  187 us (50%)
  local copies, waits for them, and re-layouts  50.9 us (14%)
  matrix products  45 us (12%)
  blocking collectives  25.5 us (7%)
  starting transfers between devices  24.2 us (6%)
  other arithmetic  21.8 us (6%)
  between operations  14.3 us (4%)
    reduce_scatter x1, waiting for transfers between devices, on_device(): lax.psum_scatter(jnp.concatenate([cross_part, fgram_part], 1), 'bin', sca...  71.9 us
    all_gather x1, waiting for transfers between devices, on_device(): factors_new = lax.all_gather(new_own, 'gene', axis=1, tiled=True)  68.1 us
    all_gather x1, waiting for transfers between devices, on_device(): loadings_new = lax.all_gather(new_load, 'bin', axis=0, tiled=True)  45.8 us
    all_to_all x1, blocking collectives, stencil_term(): lax.all_to_all(back_rows.reshape(bin_count, group_size * (width + 1)), 'b...  25.5 us
    unnamed x27, local copies, waits for them, and re-layouts  22.6 us
    ppermute x4, starting transfers between devices, passed_along(): return lax.ppermute(block, axis, route)  14.3 us
    dot_general x1, matrix products, on_device(): lax.dot_general(fac_bf, counts, left_dims, preferred_element_type=jnp.flo...  10.3 us
    all_to_all x1, starting transfers between devices, stencil_term(): lax.all_to_all(payload.reshape(bin_count, group_size * (width + 1)), 'bin...  9.29 us
  transfers between devices with their start and end apart: 9, of which 4 were waited for; matrix products, arithmetic and copies ran while one was open for 21% of the time, Pallas kernels for 0%

profile of v2, /device:TPU:1, one launch (start us, length us, event | category | flops | bytes accessed | tf_op | source)
XLA Modules:
  0.0 368.8 jit_solution(11523954443179676951)
XLA Ops:
  7.2 1.9 copy-done
  9.1 1.6 constant_dynamic-slice_fusion
  10.7 1.8 copy.43
  12.5 0.8 pad_maximum_fusion.2
  13.4 2.7 copy.30
  16.0 3.8 %all_to_all.16 = f32[16,1,6336]{2,1,0:T(1,128)} reshape(f32[3072,33]{1,0:T(8,128)} %copy.30) | data formatting | bytes 811008 | tf_op jit(solution)/shard_map/all_to_all | solution.py:52
  19.9 9.3 %all-to-all-start = ((f32[16,1,6336]{2,1,0:T(1,128)}), f32[16,1,6336]{2,1,0:T(1,128)}, u32[]{:S(2)}, u32[]{:S(2)}) async-start(f32[16,1,6336]{2,1,0:T(1,128)} %all_to_all.16), calls=%async_computation | async-start | bytes 819200 | tf_op jit(solution)/shard_map/all_to_all | solution.py:52
  29.2 0.0 reduce-scatter.7.cloned.1.call-start
  29.2 0.9 fusion.42
  30.1 0.6 fusion.47
  30.7 2.0 collective-permute-start.2
  32.7 5.0 %collective-permute-start.3 = (f32[256]{0:T(256)}, f32[256]{0:T(256)}, u32[]{:S(2)}, u32[]{:S(2)}) collective-permute-start(f32[256]{0:T(256)} %bitcast.6), channel_id=1, source_target_pairs={{0,1},{1,2},{2,3},{3,4},{4,5},{5,6},{6,7},{7,8},{8,9},{9,10},{10,1... | collective-permute-start | bytes 3080 | tf_op jit(solution)/shard_map/ppermute | solution.py:13
  37.8 2.9 fusion.23
  40.7 7.2 %fusion.25 = f32[3072,256]{1,0:T(8,128)S(1)} fusion(bf16[3072,2304]{1,0:T(8,128)(2,1)} %param.5, f32[256,2304]{1,0:T(8,128)S(1)} %copy-done.2), kind=kOutput, calls=%fused_computation.36 | convolution fusion | flops 3624468480 | bytes 19660800 | tf_op jit(solution)/shard_map/dot_general | solution.py:95
  47.9 2.0 pad_maximum_fusion
  49.9 5.0 %copy.41 = f32[3328,256]{0,1:T(8,128)} copy(f32[3328,256]{1,0:T(8,128)} %pad_maximum_fusion) | data formatting | bytes 6815744
  55.0 0.5 all-gather.3.cloned.1.call-start
  55.5 0.7 fusion.46
  56.1 0.6 fusion.48
  56.8 0.9 fusion.39
  57.6 0.6 copy.50
  58.2 2.7 reduce
  61.0 4.0 %reshape.94 = f32[3072,33]{1,0:T(8,128)} reshape(f32[16,6336]{1,0:T(8,128)} %reduce) | data formatting | bytes 811008 | tf_op jit(solution)/shard_map/reshape | solution.py:54
  64.9 2.9 copy.44
  67.8 2.3 fusion.8
  70.1 1.1 reduce-precision_convert_fusion.3
  71.2 7.5 %fusion.1 = f32[3072,96]{0,1:T(8,128)S(1)} fusion(s32[3072]{0:T(1024)S(1)} %fusion.8, bf16[3072,32]{0,1:T(8,128)(2,1)S(1)} %get-tuple-element.16, bf16[3072,32]{0,1:T(8,128)(2,1)S(1)} %get-tuple-element.17, bf16[3072,32]{0,1:T(8,128)(2,1)S(1)} %get-tuple-element.15), kind=kOutput, calls=%fused_computation.2 | convolution fusion | flops 1823145984 | bytes 1781760 | tf_op jit(solution)/shard_map/dot_general | solution.py:58
  78.8 0.8 slice_add_fusion.2
  79.6 1.9 reshape.95
  81.5 1.1 broadcast_multiply_fusion
  82.6 1.9 collective-permute-start
  84.6 5.3 %collective-permute-start.1 = (f32[256,32]{0,1:T(8,128)S(1)}, f32[256,32]{0,1:T(8,128)S(1)}, u32[]{:S(2)}, u32[]{:S(2)}) collective-permute-start(f32[256,32]{0,1:T(8,128)S(1)} %bitcast.56), channel_id=1, source_target_pairs={{0,1},{1,2},{2,3},{3,4},{4,5},{5,6},{6,7},{7,8},{8,9},{9,10},{10,1... | collective-permute-start | bytes 98312 | tf_op jit(solution)/shard_map/ppermute | solution.py:13
  89.9 0.1 fusion.45
  90.0 0.2 fusion.43
  90.2 0.0 collective-permute-done
  90.3 1.2 collective-permute-done.1
  91.5 0.3 fusion.29
  91.8 0.2 copy.49
  92.0 0.8 constant_dynamic-update-slice_fusion
  92.8 1.6 dynamic-update-slice.1
  94.4 1.1 reduce-precision_convert_fusion.1
  95.5 8.0 %fusion = f32[3072,99]{0,1:T(8,128)S(1)} fusion(s32[3072]{0:T(1024)S(1)} %copy-done.6, bf16[3072,33]{0,1:T(8,128)(2,1)S(1)} %get-tuple-element.13, bf16[3072,33]{0,1:T(8,128)(2,1)S(1)} %get-tuple-element.14, bf16[3072,33]{0,1:T(8,128)(2,1)S(1)} %get-tuple-element.12), kind=kOutput, calls=%fused_computation.1 | convolution fusion | flops 1879824384 | bytes 1837056 | tf_op jit(solution)/shard_map/dot_general | solution.py:76
  103.6 0.9 slice_add_fusion
  104.5 2.7 copy.35
  107.1 3.8 %all_to_all.17 = f32[16,1,6336]{2,1,0:T(1,128)} reshape(f32[3072,33]{1,0:T(8,128)} %copy.35) | data formatting | bytes 811008 | tf_op jit(solution)/shard_map/all_to_all | solution.py:78
  111.0 25.5 %all_to_all.20 = f32[16,1,6336]{2,1,0:T(1,128)} all-to-all(f32[16,1,6336]{2,1,0:T(1,128)} %all_to_all.17), channel_id=1, replica_groups=mesh['gene'=8,'bin'=16] {'bin'}, dimensions={0} | all-to-all | bytes 811008 | tf_op jit(solution)/shard_map/all_to_all | solution.py:78
  136.4 2.7 reduce.2
  139.2 4.0 %reshape.98 = f32[3072,33]{1,0:T(8,128)} reshape(f32[16,6336]{1,0:T(8,128)} %reduce.2) | data formatting | bytes 811008 | tf_op jit(solution)/shard_map/reshape | solution.py:80
  143.1 2.6 copy.47
  145.7 2.3 fusion.6
  148.0 0.0 reduce-scatter.7.cloned.1.call-done
  148.1 4.8 %fusion.5 = f32[3072,32]{0,1:T(8,128)} fusion(f32[3072,256]{1,0:T(8,128)S(1)} %copy-done, f32[3072,32]{0,1:T(8,128)S(1)} %copy.43, f32[3328,32]{0,1:T(8,128)} %bitcast.57, f32[3072,32]{0,1:T(8,128)} %copy.47, f32[3072]{0:T(1024)S(1)} %fusion.6), kind=kOutput, calls=%fused_computation.7 | convolution fusion | flops 302579712 | bytes 4763648 | tf_op jit(solution)/shard_map/dot_general | solution.py:105
  152.9 0.0 all-gather.3.cloned.1.call-update
  152.9 0.0 reduce-scatter.5.cloned.1.call-start
  153.0 68.1 %all-gather.3.cloned.1.call-done = f32[3072,256]{0,1:T(8,128)} async-done(((f32[3072,32]{0,1:T(8,128)}), f32[3072,256]{0,1:T(8,128)}) %all-gather.3.cloned.1.call-update) | async-done | bytes 3145744 | tf_op jit(solution)/shard_map/all_gather | solution.py:109
  221.1 10.3 %fusion.11 = f32[256,2304]{1,0:T(8,128)S(1)} fusion(bf16[3072,2304]{1,0:T(8,128)(2,1)} %param.5, f32[3072,256]{0,1:T(8,128)} %all-gather.3.cloned.1.call-done), kind=kOutput, calls=%fused_computation.18 | convolution fusion | flops 3624665088 | bytes 19660800 | tf_op jit(solution)/shard_map/dot_general | solution.py:112
  231.4 0.6 fusion.9
  232.1 1.8 pad_maximum_fusion.1
  233.9 0.0 all-gather.5.cloned.1.call-start
  234.0 71.9 %reduce-scatter.5.cloned.1.call-done = f32[16,2560]{1,0:T(8,128)} async-done(((f32[256,2560]{1,0:T(8,128)}), f32[16,2560]{1,0:T(8,128)}) %reduce-scatter.5.cloned.1.call-update) | async-done | bytes 163856 | tf_op jit(solution)/shard_map/reduce_scatter | solution.py:114
  305.9 3.5 convolution_divide_fusion
  309.5 3.5 copy.39
  313.0 45.8 %all-gather.5.cloned.1.call-done = f32[256,2304]{1,0:T(8,128)} async-done(((f32[16,2304]{1,0:T(8,128)}), f32[256,2304]{1,0:T(8,128)}) %all-gather.5.cloned.1.call-update) | async-done | bytes 2359312 | tf_op jit(solution)/shard_map/all_gather | solution.py:120
  358.8 3.2 copy.57
  (27 shorter events, 0.2 us)
Async XLA Ops:
  7.2 1.9 copy-start
  9.1 3.5 copy-start.7
  19.9 38.4 %all-to-all-start = ((f32[16,1,6336]{2,1,0:T(1,128)}), f32[16,1,6336]{2,1,0:T(1,128)}, u32[]{:S(2)}, u32[]{:S(2)}) async-start(f32[16,1,6336]{2,1,0:T(1,128)} %all_to_all.16), calls=%async_computation | async-start | bytes 819200 | tf_op jit(solution)/shard_map/all_to_all | solution.py:52
  29.2 118.9 %reduce-scatter.7.cloned.1.call-start = ((), (), s32[]{:S(2)}) async-start(), calls=%async_computation.7 | async-start | bytes 3833856
  29.2 11.5 %copy-start.2 = (f32[256,2304]{1,0:T(8,128)S(1)}, f32[256,2304]{1,0:T(8,128)}, u32[]{:S(2)}) copy-start(f32[256,2304]{1,0:T(8,128)} %param.7) | copy-start | bytes 7077892
  30.1 7.7 %copy-start.3 = (f32[12,256]{1,0:T(8,128)}, f32[12,256]{1,0:T(8,128)S(1)}, u32[]{:S(2)}) copy-start(f32[12,256]{1,0:T(8,128)S(1)} %get-tuple-element.25) | copy-start | bytes 36868
  30.7 26.1 %collective-permute-start.2 = (f32[256]{0:T(256)}, f32[256]{0:T(256)}, u32[]{:S(2)}, u32[]{:S(2)}) collective-permute-start(f32[256]{0:T(256)} %bitcast.4), channel_id=1, source_target_pairs={{1,0},{2,1},{3,2},{4,3},{5,4},{6,5},{7,6},{8,7},{9,8},{10,9},{11,1... | collective-permute-start | bytes 3080 | tf_op jit(solution)/shard_map/ppermute | solution.py:13
  32.7 24.0 %collective-permute-start.3 = (f32[256]{0:T(256)}, f32[256]{0:T(256)}, u32[]{:S(2)}, u32[]{:S(2)}) collective-permute-start(f32[256]{0:T(256)} %bitcast.6), channel_id=1, source_target_pairs={{0,1},{1,2},{2,3},{3,4},{4,5},{5,6},{6,7},{7,8},{8,9},{9,10},{10,1... | collective-permute-start | bytes 3080 | tf_op jit(solution)/shard_map/ppermute | solution.py:13
  55.0 166.1 %all-gather.3.cloned.1.call-start = ((), (), s32[]{:S(2)}) async-start(), calls=%async_computation.4 | async-start | bytes 3538944 | tf_op jit(solution)/shard_map/all_gather | solution.py:109
  70.1 8.6 %copy-start.5 = (s32[3072]{0:T(1024)}, s32[3072]{0:T(1024)S(1)}, u32[]{:S(2)}) copy-start(s32[3072]{0:T(1024)S(1)} %fusion.8) | copy-start | bytes 36868
  78.8 2.7 copy-start.4
  82.6 7.6 %collective-permute-start = (f32[256,32]{0,1:T(8,128)S(1)}, f32[256,32]{0,1:T(8,128)S(1)}, u32[]{:S(2)}, u32[]{:S(2)}) collective-permute-start(f32[256,32]{0,1:T(8,128)S(1)} %bitcast.55), channel_id=1, source_target_pairs={{1,0},{2,1},{3,2},{4,3},{5,4},{6,5},{7,6},{8,7},{9,8},{10,9},{11,1... | collective-permute-start | bytes 98312 | tf_op jit(solution)/shard_map/ppermute | solution.py:13
  84.6 6.9 %collective-permute-start.1 = (f32[256,32]{0,1:T(8,128)S(1)}, f32[256,32]{0,1:T(8,128)S(1)}, u32[]{:S(2)}, u32[]{:S(2)}) collective-permute-start(f32[256,32]{0,1:T(8,128)S(1)} %bitcast.56), channel_id=1, source_target_pairs={{0,1},{1,2},{2,3},{3,4},{4,5},{5,6},{6,7},{7,8},{8,9},{9,10},{10,1... | collective-permute-start | bytes 98312 | tf_op jit(solution)/shard_map/ppermute | solution.py:13
  91.8 3.8 %copy-start.6 = (s32[3072]{0:T(1024)S(1)}, s32[3072]{0:T(1024)}, u32[]{:S(2)}) copy-start(s32[3072]{0:T(1024)} %copy-done.5) | copy-start | bytes 36868
  152.9 153.0 %reduce-scatter.5.cloned.1.call-start = ((), (), s32[]{:S(2)}) async-start(), calls=%async_computation.5 | async-start | bytes 2785280 | tf_op jit(solution)/shard_map/reduce_scatter | solution.py:114
  221.1 10.3 %copy-start.1 = (f32[3072,256]{0,1:T(8,128)S(1)}, f32[3072,256]{0,1:T(8,128)}, u32[]{:S(2)}) copy-start(f32[3072,256]{0,1:T(8,128)} %all-gather.3.cloned.1.call-done) | copy-start | bytes 9437188
  233.9 124.9 %all-gather.5.cloned.1.call-start = ((), (), s32[]{:S(2)}) async-start(), calls=%async_computation.6 | async-start | bytes 2506752 | tf_op jit(solution)/shard_map/all_gather | solution.py:120
Sparse Core Ops, SparseCore 0:
  55.1 83.0 reduce-scatter.6
  153.0 68.0 all-gather.2
  234.0 71.8 reduce-scatter.4
  309.6 49.1 all-gather.4

commit v3 on v2

--- a/solution.py
+++ b/solution.py
@@ -1,6 +1,10 @@
+import functools
+
 import jax
 import jax.numpy as jnp
 from jax import lax
+from jax.experimental import pallas as pl
+from jax.experimental.pallas import tpu as pltpu
 from jax.sharding import PartitionSpec as P
 
 K = 256
@@ -29,6 +33,75 @@
         values[:, :, :-1], ((0, 0), (0, 0), (1, 0))
     )
     return beside + 0.5 * (lower + upper)
+
+
+def snake_gene(place, count):
+    wide = 1 - ((place + count - 1) % count) // (count // 2)
+    row = wide * (place - 1) + (1 - wide) * ((count - place) % count)
+    return 2 * row + wide
+
+
+def snake_place(index, count):
+    row, wide = index // 2, index % 2
+    return wide * (1 + row) + (1 - wide) * ((count - row) % count)
+
+
+def gather_kernel(count, x_ref, out_ref, send_sem, recv_sem):
+    me = lax.axis_index("gene")
+    place = snake_place(me, count)
+    ahead = snake_gene((place + 1) % count, count)
+    behind = snake_gene((place + count - 1) % count, count)
+    half = x_ref.shape[0] // 2
+    barrier = pltpu.get_barrier_semaphore()
+    for peer in (ahead, behind):
+        pl.semaphore_signal(barrier, inc=1, device_id={"gene": peer},
+                            device_id_type=pl.DeviceIdType.MESH)
+    pl.semaphore_wait(barrier, 2)
+    out_ref[me] = x_ref[...]
+
+    def copy(step, way):
+        rows = pl.ds(way * half, half)
+        if way == 0:
+            origin = snake_gene((place - step + count) % count, count)
+            target = ahead
+        else:
+            origin = snake_gene((place + step) % count, count)
+            target = behind
+        src = x_ref.at[rows] if step == 0 else out_ref.at[origin, rows]
+        return pltpu.make_async_remote_copy(
+            src_ref=src,
+            dst_ref=out_ref.at[origin, rows],
+            send_sem=send_sem.at[way, step],
+            recv_sem=recv_sem.at[way, step],
+            device_id={"gene": target},
+            device_id_type=pl.DeviceIdType.MESH,
+        )
+
+    for step in range(count - 1):
+        for way in (0, 1):
+            if step >= 1:
+                copy(step - 1, way).wait_recv()
+            copy(step, way).start()
+    for way in (0, 1):
+        copy(count - 2, way).wait_recv()
+    for step in range(count - 1):
+        for way in (0, 1):
+            copy(step, way).wait_send()
+
+
+def gene_gather(x):
+    count = lax.axis_size("gene")
+    return pl.pallas_call(
+        functools.partial(gather_kernel, count),
+        out_shape=jax.ShapeDtypeStruct((count,) + x.shape, x.dtype),
+        in_specs=[pl.BlockSpec(memory_space=pltpu.VMEM)],
+        out_specs=pl.BlockSpec(memory_space=pltpu.VMEM),
+        scratch_shapes=[
+            pltpu.SemaphoreType.DMA((2, count - 1)),
+            pltpu.SemaphoreType.DMA((2, count - 1)),
+        ],
+        compiler_params=pltpu.CompilerParams(collective_id=0, has_side_effects=True),
+    )(x)
 
 
 def split_three(values):
@@ -106,11 +179,11 @@
         + penalty * degree[:, None] * own
     )
     new_own = own * (numer + penalty * smooth) / denom
-    factors_new = lax.all_gather(new_own, "gene", axis=1, tiled=True)
-    fac_bf = factors_new.astype(jnp.bfloat16)
-    left_dims = (((0,), (0,)), ((), ()))
-    cross_part = lax.dot_general(fac_bf, counts, left_dims, preferred_element_type=jnp.float32)
-    fgram_part = lax.dot_general(fac_bf, fac_bf, left_dims, preferred_element_type=jnp.float32)
+    factors_t = gene_gather(new_own.T).reshape(width_all, row_count)
+    factors_new = factors_t.T
+    fac_bf_t = factors_t.astype(jnp.bfloat16)
+    cross_part = jnp.dot(fac_bf_t, counts, preferred_element_type=jnp.float32)
+    fgram_part = lax.dot_general(fac_bf_t, fac_bf_t, right_dims, preferred_element_type=jnp.float32)
     both_bin = lax.psum_scatter(
         jnp.concatenate([cross_part, fgram_part], 1), "bin", scatter_dimension=0, tiled=True
     )

time: 375 us -> 343 us (0.915)
  waiting for transfers between devices: 187 us -> 121 us
  Pallas kernels: 0 us -> 39.9 us
  local copies, waits for them, and re-layouts: 50.9 us -> 46.5 us
    all_gather x1 -> x0, waiting for transfers between devices: 68.1 us -> none  [on_device(): factors_new = lax.all_gather(new_own, 'gene', axis=1, tiled=True)]
    pallas_call x0 -> x1, Pallas kernels: none -> 39.9 us  [gene_gather(): pl.pallas_call(functools.partial(gather_kernel, count), out_shape=jax.Sha...]
    unnamed x27 -> x25, local copies, waits for them, and re-layouts: 22.6 us -> 14.6 us
  transfers between devices with their start and end apart: 9 -> 8, of which waited for: 4 -> 3; matrix products, arithmetic and copies ran while one was open for 21% -> 21% of each run, Pallas kernels for 0% -> 0%
where the time goes in v3:
time: 343 us; the launch traced here: 337 us
  waiting for transfers between devices  121 us (35%)
  local copies, waits for them, and re-layouts  46.5 us (14%)
  matrix products  42.1 us (12%)
  Pallas kernels  39.9 us (12%)
  blocking collectives  25.5 us (7%)
  starting transfers between devices  24.2 us (7%)
  other arithmetic  24 us (7%)
  between operations  14.3 us (4%)
    reduce_scatter x1, waiting for transfers between devices, on_device(): lax.psum_scatter(jnp.concatenate([cross_part, fgram_part], 1), 'bin', sca...  73.6 us
    all_gather x1, waiting for transfers between devices, on_device(): loadings_new = lax.all_gather(new_load, 'bin', axis=0, tiled=True)  45.8 us
    pallas_call x1, Pallas kernels, gene_gather(): pl.pallas_call(functools.partial(gather_kernel, count), out_shape=jax.Sha...  39.9 us
    all_to_all x1, blocking collectives, stencil_term(): lax.all_to_all(back_rows.reshape(bin_count, group_size * (width + 1)), 'b...  25.5 us
    unnamed x25, local copies, waits for them, and re-layouts  14.6 us
    ppermute x4, starting transfers between devices, passed_along(): return lax.ppermute(block, axis, route)  14.3 us
    all_to_all x1, starting transfers between devices, stencil_term(): lax.all_to_all(payload.reshape(bin_count, group_size * (width + 1)), 'bin...  9.29 us
    dot_general x1, matrix products, stencil_term(): jnp.dot(onehot, split_three(back), preferred_element_type=jnp.float32)  8.05 us
  transfers between devices with their start and end apart: 8, of which 3 were waited for; matrix products, arithmetic and copies ran while one was open for 21% of the time, Pallas kernels for 0%

profile of v3, /device:TPU:1, one launch (start us, length us, event | category | flops | bytes accessed | tf_op | source)
XLA Modules:
  0.0 337.1 jit_solution(3155232243634704080)
XLA Ops:
  7.2 1.9 copy-done
  9.1 1.6 constant_dynamic-slice_fusion
  10.7 1.8 copy.62
  12.5 0.8 pad_maximum_fusion.2
  13.4 2.7 copy.49
  16.0 3.8 %all_to_all.16 = f32[16,1,6336]{2,1,0:T(1,128)} reshape(f32[3072,33]{1,0:T(8,128)} %copy.49) | data formatting | bytes 811008 | tf_op jit(solution)/shard_map/all_to_all | solution.py:125
  19.9 9.3 %all-to-all-start = ((f32[16,1,6336]{2,1,0:T(1,128)}), f32[16,1,6336]{2,1,0:T(1,128)}, u32[]{:S(2)}, u32[]{:S(2)}) async-start(f32[16,1,6336]{2,1,0:T(1,128)} %all_to_all.16), calls=%async_computation.1 | async-start | bytes 819200 | tf_op jit(solution)/shard_map/all_to_all | solution.py:125
  29.2 0.0 reduce-scatter.3.cloned.1.call-start
  29.2 0.9 fusion.41
  30.1 0.6 fusion.46
  30.7 2.0 collective-permute-start.2
  32.7 5.0 %collective-permute-start.3 = (f32[256]{0:T(256)}, f32[256]{0:T(256)}, u32[]{:S(2)}, u32[]{:S(2)}) collective-permute-start(f32[256]{0:T(256)} %bitcast.6), channel_id=1, source_target_pairs={{0,1},{1,2},{2,3},{3,4},{4,5},{5,6},{6,7},{7,8},{8,9},{9,10},{10,1... | collective-permute-start | bytes 3080 | tf_op jit(solution)/shard_map/ppermute | solution.py:17
  37.8 2.9 fusion.22
  40.7 7.1 %fusion.24 = f32[3072,256]{0,1:T(8,128)S(1)} fusion(bf16[3072,2304]{1,0:T(8,128)(2,1)} %param.5, f32[256,2304]{1,0:T(8,128)S(1)} %copy-done.2), kind=kOutput, calls=%fused_computation.35 | convolution fusion | flops 3624468480 | bytes 19660800 | tf_op jit(solution)/shard_map/dot_general | solution.py:168
  47.8 2.0 pad_maximum_fusion
  49.7 0.0 reduce-scatter.3.cloned.1.call-update
  49.8 0.5 reduce-scatter.5.cloned.1.call-start
  50.3 0.7 fusion.45
  50.9 0.6 fusion.47
  51.6 0.9 fusion.38
  52.4 0.6 copy.68
  53.1 2.7 reduce
  55.8 4.0 %reshape.99 = f32[3072,33]{1,0:T(8,128)} reshape(f32[16,6336]{1,0:T(8,128)} %reduce) | data formatting | bytes 811008 | tf_op jit(solution)/shard_map/reshape | solution.py:127
  59.7 2.9 copy.63
  62.6 2.3 fusion.9
  64.9 1.1 reduce-precision_convert_fusion.3
  66.0 7.5 %fusion.1 = f32[3072,96]{0,1:T(8,128)S(1)} fusion(s32[3072]{0:T(1024)S(1)} %fusion.9, bf16[3072,32]{0,1:T(8,128)(2,1)S(1)} %get-tuple-element.12, bf16[3072,32]{0,1:T(8,128)(2,1)S(1)} %get-tuple-element.13, bf16[3072,32]{0,1:T(8,128)(2,1)S(1)} %get-tuple-element.11), kind=kOutput, calls=%fused_computation.2 | convolution fusion | flops 1823145984 | bytes 1781760 | tf_op jit(solution)/shard_map/dot_general | solution.py:131
  73.6 0.8 slice_add_fusion.2
  74.4 1.9 reshape.100
  76.3 1.1 broadcast_multiply_fusion
  77.4 1.9 collective-permute-start
  79.4 5.3 %collective-permute-start.1 = (f32[256,32]{0,1:T(8,128)S(1)}, f32[256,32]{0,1:T(8,128)S(1)}, u32[]{:S(2)}, u32[]{:S(2)}) collective-permute-start(f32[256,32]{0,1:T(8,128)S(1)} %bitcast.66), channel_id=1, source_target_pairs={{0,1},{1,2},{2,3},{3,4},{4,5},{5,6},{6,7},{7,8},{8,9},{9,10},{10,1... | collective-permute-start | bytes 98312 | tf_op jit(solution)/shard_map/ppermute | solution.py:17
  84.7 0.2 fusion.42
  84.9 0.1 fusion.44
  85.0 0.0 collective-permute-done
  85.1 1.2 collective-permute-done.1
  86.2 0.3 fusion.28
  86.6 0.2 copy.67
  86.8 0.8 constant_dynamic-update-slice_fusion
  87.6 1.6 dynamic-update-slice.1
  89.2 1.1 reduce-precision_convert_fusion.1
  90.3 8.0 %fusion = f32[3072,99]{0,1:T(8,128)S(1)} fusion(s32[3072]{0:T(1024)S(1)} %copy-done.6, bf16[3072,33]{0,1:T(8,128)(2,1)S(1)} %get-tuple-element.9, bf16[3072,33]{0,1:T(8,128)(2,1)S(1)} %get-tuple-element.10, bf16[3072,33]{0,1:T(8,128)(2,1)S(1)} %get-tuple-element.8), kind=kOutput, calls=%fused_computation.1 | convolution fusion | flops 1879824384 | bytes 1837056 | tf_op jit(solution)/shard_map/dot_general | solution.py:149
  98.4 0.9 slice_add_fusion
  99.3 2.7 copy.54
  101.9 3.8 %all_to_all.17 = f32[16,1,6336]{2,1,0:T(1,128)} reshape(f32[3072,33]{1,0:T(8,128)} %copy.54) | data formatting | bytes 811008 | tf_op jit(solution)/shard_map/all_to_all | solution.py:151
  105.8 25.5 %all_to_all.20 = f32[16,1,6336]{2,1,0:T(1,128)} all-to-all(f32[16,1,6336]{2,1,0:T(1,128)} %all_to_all.17), channel_id=1, replica_groups=mesh['gene'=8,'bin'=16] {'bin'}, dimensions={0} | all-to-all | bytes 811008 | tf_op jit(solution)/shard_map/all_to_all | solution.py:151
  131.2 2.7 reduce.2
  133.9 4.0 %reshape.103 = f32[3072,33]{1,0:T(8,128)} reshape(f32[16,6336]{1,0:T(8,128)} %reduce.2) | data formatting | bytes 811008 | tf_op jit(solution)/shard_map/reshape | solution.py:153
  137.9 2.6 copy.66
  140.5 2.3 fusion.7
  142.8 0.0 reduce-scatter.3.cloned.1.call-done
  142.8 4.8 %fusion.6.x_ref = f32[32,3072]{1,0:T(8,128)} fusion(f32[3072,256]{1,0:T(8,128)S(1)} %copy-done, f32[3072,32]{0,1:T(8,128)S(1)} %copy.62, f32[3328,32]{0,1:T(8,128)} %reduce-scatter.3.cloned.1.call-done, f32[3072,32]{0,1:T(8,128)} %copy.66, f32[3072]{0:T(1024)S(1)} %fusion.7), kind=kOutput, calls=%fused_computation.8 | convolution fusion | flops 302579712 | bytes 4763648 | tf_op jit(solution)/shard_map/dot_general | solution.py:178
  147.7 39.9 %shard_map.68 = f32[8,32,3072]{2,1,0:T(8,128)} custom-call(f32[32,3072]{1,0:T(8,128)} %fusion.6.x_ref), custom_call_target="tpu_custom_call" | custom-call | tf_op jit(solution)/shard_map/pallas_call | solution.py:94
  187.6 2.2 convert_element_type.38
  189.9 0.6 copy-done.1
  190.5 7.6 %fusion.10 = f32[256,2304]{1,0:T(8,128)S(1)} fusion(bf16[3072,2304]{1,0:T(8,128)(2,1)} %param.5, f32[256,3072]{1,0:T(8,128)S(1)} %bitcast.56), kind=kOutput, calls=%fused_computation.17 | convolution fusion | flops 3624665088 | bytes 19660800 | tf_op jit(solution)/shard_map/dot_general | solution.py:185
  198.0 0.6 fusion.48
  198.6 1.8 pad_maximum_fusion.1
  200.5 0.0 all-gather.2.cloned.1.call-start
  200.6 73.6 %reduce-scatter.5.cloned.1.call-done = f32[16,2560]{1,0:T(8,128)} async-done(((f32[256,2560]{1,0:T(8,128)}), f32[16,2560]{1,0:T(8,128)}) %reduce-scatter.5.cloned.1.call-update) | async-done | bytes 163856 | tf_op jit(solution)/shard_map/reduce_scatter | solution.py:187
  274.2 3.5 %convolution_divide_fusion = f32[16,2304]{1,0:T(8,128)} fusion(f32[256,2304]{1,0:T(8,128)} %param.7, f32[16,2560]{1,0:T(8,128)} %reduce-scatter.5.cloned.1.call-done, s32[]{:T(128)S(6)} %select_n.7), kind=kOutput, calls=%fused_computation.10 | convolution fusion | flops 113319936 | bytes 2818052 | tf_op jit(solution)/shard_map/dot_general | solution.py:192
  277.7 3.5 %copy.57 = f32[256,3072]{0,1:T(8,128)} copy(f32[256,3072]{1,0:T(8,128)} %bitcast.55) | data formatting | bytes 6291456 | tf_op jit(solution)/shard_map/reshape | solution.py:182
  281.3 45.8 %all-gather.2.cloned.1.call-done = f32[256,2304]{1,0:T(8,128)} async-done(((f32[16,2304]{1,0:T(8,128)}), f32[256,2304]{1,0:T(8,128)}) %all-gather.2.cloned.1.call-update) | async-done | bytes 2359312 | tf_op jit(solution)/shard_map/all_gather | solution.py:193
  327.1 3.2 copy.75
  (25 shorter events, 0.2 us)
Async XLA Ops:
  7.2 1.9 copy-start
  9.1 3.5 %copy-start.7 = (s32[3072]{0:T(1024)S(1)}, s32[3072]{0:T(1024)}, u32[]{:S(2)}) copy-start(s32[3072]{0:T(1024)} %param.8) | copy-start | bytes 36868
  19.9 33.2 %all-to-all-start = ((f32[16,1,6336]{2,1,0:T(1,128)}), f32[16,1,6336]{2,1,0:T(1,128)}, u32[]{:S(2)}, u32[]{:S(2)}) async-start(f32[16,1,6336]{2,1,0:T(1,128)} %all_to_all.16), calls=%async_computation.1 | async-start | bytes 819200 | tf_op jit(solution)/shard_map/all_to_all | solution.py:125
  29.2 113.7 %reduce-scatter.3.cloned.1.call-start = ((), (), s32[]{:S(2)}) async-start(), calls=%async_computation.4 | async-start | bytes 3833856 | tf_op jit(solution)/shard_map/reduce_scatter | solution.py:170
  29.2 11.5 %copy-start.2 = (f32[256,2304]{1,0:T(8,128)S(1)}, f32[256,2304]{1,0:T(8,128)}, u32[]{:S(2)}) copy-start(f32[256,2304]{1,0:T(8,128)} %param.7) | copy-start | bytes 7077892
  30.1 7.7 %copy-start.3 = (f32[12,256]{1,0:T(8,128)}, f32[12,256]{1,0:T(8,128)S(1)}, u32[]{:S(2)}) copy-start(f32[12,256]{1,0:T(8,128)S(1)} %get-tuple-element.21) | copy-start | bytes 36868
  30.7 20.9 %collective-permute-start.2 = (f32[256]{0:T(256)}, f32[256]{0:T(256)}, u32[]{:S(2)}, u32[]{:S(2)}) collective-permute-start(f32[256]{0:T(256)} %bitcast.4), channel_id=1, source_target_pairs={{1,0},{2,1},{3,2},{4,3},{5,4},{6,5},{7,6},{8,7},{9,8},{10,9},{11,1... | collective-permute-start | bytes 3080 | tf_op jit(solution)/shard_map/ppermute | solution.py:17
  32.7 18.8 %collective-permute-start.3 = (f32[256]{0:T(256)}, f32[256]{0:T(256)}, u32[]{:S(2)}, u32[]{:S(2)}) collective-permute-start(f32[256]{0:T(256)} %bitcast.6), channel_id=1, source_target_pairs={{0,1},{1,2},{2,3},{3,4},{4,5},{5,6},{6,7},{7,8},{8,9},{9,10},{10,1... | collective-permute-start | bytes 3080 | tf_op jit(solution)/shard_map/ppermute | solution.py:17
  49.8 224.4 %reduce-scatter.5.cloned.1.call-start = ((), (), s32[]{:S(2)}) async-start(), calls=%async_computation.5 | async-start | bytes 2785280 | tf_op jit(solution)/shard_map/reduce_scatter | solution.py:187
  64.9 8.6 %copy-start.5 = (s32[3072]{0:T(1024)}, s32[3072]{0:T(1024)S(1)}, u32[]{:S(2)}) copy-start(s32[3072]{0:T(1024)S(1)} %fusion.9) | copy-start | bytes 36868
  73.6 2.7 copy-start.4
  77.4 7.6 %collective-permute-start = (f32[256,32]{0,1:T(8,128)S(1)}, f32[256,32]{0,1:T(8,128)S(1)}, u32[]{:S(2)}, u32[]{:S(2)}) collective-permute-start(f32[256,32]{0,1:T(8,128)S(1)} %bitcast.65), channel_id=1, source_target_pairs={{1,0},{2,1},{3,2},{4,3},{5,4},{6,5},{7,6},{8,7},{9,8},{10,9},{11,1... | collective-permute-start | bytes 98312 | tf_op jit(solution)/shard_map/ppermute | solution.py:17
  79.4 6.9 %collective-permute-start.1 = (f32[256,32]{0,1:T(8,128)S(1)}, f32[256,32]{0,1:T(8,128)S(1)}, u32[]{:S(2)}, u32[]{:S(2)}) collective-permute-start(f32[256,32]{0,1:T(8,128)S(1)} %bitcast.66), channel_id=1, source_target_pairs={{0,1},{1,2},{2,3},{3,4},{4,5},{5,6},{6,7},{7,8},{8,9},{9,10},{10,1... | collective-permute-start | bytes 98312 | tf_op jit(solution)/shard_map/ppermute | solution.py:17
  86.6 3.8 %copy-start.6 = (s32[3072]{0:T(1024)S(1)}, s32[3072]{0:T(1024)}, u32[]{:S(2)}) copy-start(s32[3072]{0:T(1024)} %copy-done.5) | copy-start | bytes 36868
  187.6 2.8 copy-start.1
  200.5 126.6 %all-gather.2.cloned.1.call-start = ((), (), s32[]{:S(2)}) async-start(), calls=%async_computation.6 | async-start | bytes 2506752 | tf_op jit(solution)/shard_map/all_gather | solution.py:193
Sparse Core Ops, SparseCore 0:
  49.9 83.0 reduce-scatter.2
  200.6 73.4 reduce-scatter.4
  277.8 49.2 all-gather.1

commit v4 on v3

--- a/solution.py
+++ b/solution.py
@@ -35,45 +35,67 @@
     return beside + 0.5 * (lower + upper)
 
 
-def snake_gene(place, count):
+def gray(value):
+    return value + (value // 2) * (1 - 2 * (value % 2))
+
+
+def gene_at_place(place, count):
     wide = 1 - ((place + count - 1) % count) // (count // 2)
     row = wide * (place - 1) + (1 - wide) * ((count - place) % count)
     return 2 * row + wide
 
 
-def snake_place(index, count):
+def gene_place(index, count):
     row, wide = index // 2, index % 2
     return wide * (1 + row) + (1 - wide) * ((count - row) % count)
 
 
-def gather_kernel(count, x_ref, out_ref, send_sem, recv_sem):
-    me = lax.axis_index("gene")
-    place = snake_place(me, count)
-    ahead = snake_gene((place + 1) % count, count)
-    behind = snake_gene((place + count - 1) % count, count)
+def bin_at_place(place, count):
+    plane, step = place // 4, place % 4
+    turned = step + (plane % 2) * (3 - 2 * step)
+    return plane * 4 + gray(turned)
+
+
+def bin_place(index, count):
+    plane = index // 4
+    turned = gray(index % 4)
+    return plane * 4 + turned + (plane % 2) * (3 - 2 * turned)
+
+
+RINGS = {"gene": (gene_at_place, gene_place), "bin": (bin_at_place, bin_place)}
+
+
+def ring_peers(axis, count):
+    at_place, place_of = RINGS[axis]
+    place = place_of(lax.axis_index(axis), count)
+    return place, (lambda shift: at_place((place + shift + count) % count, count))
+
+
+def enter(axis, peers):
+    barrier = pltpu.get_barrier_semaphore()
+    for peer in peers:
+        pl.semaphore_signal(barrier, inc=1, device_id={axis: peer},
+                            device_id_type=pl.DeviceIdType.MESH)
+    pl.semaphore_wait(barrier, len(peers))
+
+
+def gather_kernel(axis, count, x_ref, out_ref, send_sem, recv_sem):
+    place, member = ring_peers(axis, count)
+    ahead, behind = member(1), member(-1)
     half = x_ref.shape[0] // 2
-    barrier = pltpu.get_barrier_semaphore()
-    for peer in (ahead, behind):
-        pl.semaphore_signal(barrier, inc=1, device_id={"gene": peer},
-                            device_id_type=pl.DeviceIdType.MESH)
-    pl.semaphore_wait(barrier, 2)
-    out_ref[me] = x_ref[...]
+    enter(axis, (ahead, behind))
+    out_ref[member(0)] = x_ref[...]
 
     def copy(step, way):
         rows = pl.ds(way * half, half)
-        if way == 0:
-            origin = snake_gene((place - step + count) % count, count)
-            target = ahead
-        else:
-            origin = snake_gene((place + step) % count, count)
-            target = behind
+        origin = member(-step) if way == 0 else member(step)
         src = x_ref.at[rows] if step == 0 else out_ref.at[origin, rows]
         return pltpu.make_async_remote_copy(
             src_ref=src,
             dst_ref=out_ref.at[origin, rows],
             send_sem=send_sem.at[way, step],
             recv_sem=recv_sem.at[way, step],
-            device_id={"gene": target},
+            device_id={axis: ahead if way == 0 else behind},
             device_id_type=pl.DeviceIdType.MESH,
         )
 
@@ -89,10 +111,10 @@
             copy(step, way).wait_send()
 
 
-def gene_gather(x):
-    count = lax.axis_size("gene")
+def ring_gather(x, axis, collective_id):
+    count = lax.axis_size(axis)
     return pl.pallas_call(
-        functools.partial(gather_kernel, count),
+        functools.partial(gather_kernel, axis, count),
         out_shape=jax.ShapeDtypeStruct((count,) + x.shape, x.dtype),
         in_specs=[pl.BlockSpec(memory_space=pltpu.VMEM)],
         out_specs=pl.BlockSpec(memory_space=pltpu.VMEM),
@@ -100,7 +122,66 @@
             pltpu.SemaphoreType.DMA((2, count - 1)),
             pltpu.SemaphoreType.DMA((2, count - 1)),
         ],
-        compiler_params=pltpu.CompilerParams(collective_id=0, has_side_effects=True),
+        compiler_params=pltpu.CompilerParams(
+            collective_id=collective_id, has_side_effects=True
+        ),
+    )(x)
+
+
+def scatter_kernel(axis, count, x_ref, out_ref, got, sent, send_sem, recv_sem):
+    place, member = ring_peers(axis, count)
+    ahead, behind = member(1), member(-1)
+    half = x_ref.shape[2] // 2
+    enter(axis, (ahead, behind))
+
+    def copy(step, way):
+        lanes = pl.ds(way * half, half)
+        if step == 0:
+            source = x_ref.at[member(-1) if way == 0 else member(1), :, lanes]
+        else:
+            source = sent.at[way, step]
+        return pltpu.make_async_remote_copy(
+            src_ref=source,
+            dst_ref=got.at[way, step],
+            send_sem=send_sem.at[way, step],
+            recv_sem=recv_sem.at[way, step],
+            device_id={axis: ahead if way == 0 else behind},
+            device_id_type=pl.DeviceIdType.MESH,
+        )
+
+    for step in range(count - 1):
+        for way in (0, 1):
+            if step >= 1:
+                lanes = pl.ds(way * half, half)
+                owner = member(-step - 1) if way == 0 else member(step + 1)
+                copy(step - 1, way).wait_recv()
+                sent[way, step] = got[way, step - 1] + x_ref[owner, :, lanes]
+            copy(step, way).start()
+    for way in (0, 1):
+        lanes = pl.ds(way * half, half)
+        copy(count - 2, way).wait_recv()
+        out_ref[:, lanes] = got[way, count - 2] + x_ref[member(0), :, lanes]
+    for step in range(count - 1):
+        for way in (0, 1):
+            copy(step, way).wait_send()
+
+
+def ring_scatter(x, axis, collective_id):
+    count, rows, lanes = x.shape
+    return pl.pallas_call(
+        functools.partial(scatter_kernel, axis, count),
+        out_shape=jax.ShapeDtypeStruct((rows, lanes), x.dtype),
+        in_specs=[pl.BlockSpec(memory_space=pltpu.VMEM)],
+        out_specs=pl.BlockSpec(memory_space=pltpu.VMEM),
+        scratch_shapes=[
+            pltpu.VMEM((2, count - 1, rows, lanes // 2), x.dtype),
+            pltpu.VMEM((2, count - 1, rows, lanes // 2), x.dtype),
+            pltpu.SemaphoreType.DMA((2, count - 1)),
+            pltpu.SemaphoreType.DMA((2, count - 1)),
+        ],
+        compiler_params=pltpu.CompilerParams(
+            collective_id=collective_id, has_side_effects=True
+        ),
     )(x)
 
 
@@ -158,39 +239,37 @@
     bin_count = lax.axis_size("bin")
     gene_count = lax.axis_size("gene")
     row_count, width_all = factors.shape
-    group_size = row_count // bin_count
     width = width_all // gene_count
     k_rows = width_all // bin_count
     gene_at = lax.axis_index("gene")
     bin_at = lax.axis_index("bin")
     load_bf = loadings.astype(jnp.bfloat16)
     right_dims = (((1,), (1,)), ((), ()))
-    numer_part = lax.dot_general(counts, load_bf, right_dims, preferred_element_type=jnp.float32)
+    numer_part = lax.dot_general(load_bf, counts, right_dims, preferred_element_type=jnp.float32)
     gram_part = lax.dot_general(load_bf, load_bf, right_dims, preferred_element_type=jnp.float32)
-    both = lax.psum_scatter(
-        jnp.concatenate([numer_part, gram_part], 0), "gene", scatter_dimension=1, tiled=True
-    )
-    numer, load_gram = both[:row_count], both[row_count:]
+    both = jnp.concatenate([numer_part, gram_part], 1)
+    both = ring_scatter(both.reshape(gene_count, width, -1), "gene", 1)
+    numer_t, gram_rows = both[:, :row_count], both[:, row_count:]
     own = lax.dynamic_slice_in_dim(factors, gene_at * width, width, 1)
     smooth, degree = stencil_term(own, position, edge_codes)
     penalty = float(G * K) / 64.0
-    denom = (
-        jnp.dot(factors, load_gram, precision=lax.Precision.HIGHEST)
-        + penalty * degree[:, None] * own
-    )
-    new_own = own * (numer + penalty * smooth) / denom
-    factors_t = gene_gather(new_own.T).reshape(width_all, row_count)
+    own_t = own.T
+    denom_t = (
+        lax.dot_general(gram_rows, factors, right_dims, precision=lax.Precision.HIGHEST)
+        + penalty * degree[None, :] * own_t
+    )
+    new_t = own_t * (numer_t + penalty * smooth.T) / denom_t
+    factors_t = ring_gather(new_t, "gene", 0).reshape(width_all, row_count)
     factors_new = factors_t.T
     fac_bf_t = factors_t.astype(jnp.bfloat16)
     cross_part = jnp.dot(fac_bf_t, counts, preferred_element_type=jnp.float32)
     fgram_part = lax.dot_general(fac_bf_t, fac_bf_t, right_dims, preferred_element_type=jnp.float32)
-    both_bin = lax.psum_scatter(
-        jnp.concatenate([cross_part, fgram_part], 1), "bin", scatter_dimension=0, tiled=True
-    )
+    both_bin = jnp.concatenate([cross_part, fgram_part], 1)
+    both_bin = ring_scatter(both_bin.reshape(bin_count, k_rows, -1), "bin", 2)
     cross, fac_gram = both_bin[:, : cross_part.shape[1]], both_bin[:, cross_part.shape[1] :]
     own_load = lax.dynamic_slice_in_dim(loadings, bin_at * k_rows, k_rows, 0)
     new_load = own_load * cross / jnp.dot(fac_gram, loadings, precision=lax.Precision.HIGHEST)
-    loadings_new = lax.all_gather(new_load, "bin", axis=0, tiled=True)
+    loadings_new = ring_gather(new_load, "bin", 3).reshape(width_all, -1)
     return (factors_new, loadings_new)
 
 

time: 343 us -> 347 us (1.012)
  Pallas kernels: 39.9 us -> 182 us
  waiting for transfers between devices: 121 us -> 0.88 us
  blocking collectives: 25.5 us -> 0 us
  between operations: 14.3 us -> 1.18 us
  starting transfers between devices: 24.2 us -> 34.2 us
  matrix products: 42.1 us -> 50.2 us
  other arithmetic: 24 us -> 27.7 us
    pallas_call x1 -> x4, Pallas kernels: 39.9 us -> 182 us  [the longest x2 99.8 us: ring_scatter(): pl.pallas_call(functools.partial(scatter_kernel, axis, count), out_shape=...]
    reduce_scatter x2 -> x0, waiting for transfers between devices: 73.6 us -> none  [the longest x1 73.6 us: on_device(): lax.psum_scatter(jnp.concatenate([cross_part, fgram_part], 1), 'bin', sca...]
    all_gather x1 -> x0, waiting for transfers between devices: 45.8 us -> none  [on_device(): loadings_new = lax.all_gather(new_load, 'bin', axis=0, tiled=True)]
    all_to_all x1 -> x0, blocking collectives: 25.5 us -> none  [stencil_term(): lax.all_to_all(back_rows.reshape(bin_count, group_size * (width + 1)), 'b...]
    all_to_all x0 -> x1, starting transfers between devices: none -> 10.3 us  [stencil_term(): lax.all_to_all(back_rows.reshape(bin_count, group_size * (width + 1)), 'b...]
    dot_general x2, matrix products: 11.9 us -> 15.5 us  [the longest x1 10.7 us: on_device(): lax.dot_general(load_bf, counts, right_dims, preferred_element_type=jnp.f...]
    unnamed x25 -> x21, local copies, waits for them, and re-layouts: 14.6 us -> 13.8 us
  transfers between devices with their start and end apart: 8 -> 6, of which waited for: 3 -> 1; matrix products, arithmetic and copies ran while one was open for 21% -> 7% of each run, Pallas kernels for 0% -> 12%
where the time goes in v4:
time: 347 us; the launch traced here: 342 us
  Pallas kernels  182 us (52%)
  matrix products  50.2 us (14%)
  local copies, waits for them, and re-layouts  45.9 us (13%)
  starting transfers between devices  34.2 us (10%)
  other arithmetic  27.7 us (8%)
    pallas_call x2, Pallas kernels, ring_scatter(): pl.pallas_call(functools.partial(scatter_kernel, axis, count), out_shape=...  99.8 us
    pallas_call x2, Pallas kernels, ring_gather(): pl.pallas_call(functools.partial(gather_kernel, axis, count), out_shape=j...  82.5 us
    ppermute x4, starting transfers between devices, passed_along(): return lax.ppermute(block, axis, route)  14.6 us
    unnamed x21, local copies, waits for them, and re-layouts  13.8 us
    dot_general x1, matrix products, on_device(): lax.dot_general(load_bf, counts, right_dims, preferred_element_type=jnp.f...  10.7 us
    all_to_all x1, starting transfers between devices, stencil_term(): lax.all_to_all(back_rows.reshape(bin_count, group_size * (width + 1)), 'b...  10.3 us
    all_to_all x1, starting transfers between devices, stencil_term(): lax.all_to_all(payload.reshape(bin_count, group_size * (width + 1)), 'bin...  9.29 us
    dot_general x1, matrix products, on_device(): cross_part = jnp.dot(fac_bf_t, counts, preferred_element_type=jnp.float32)  8.51 us
  transfers between devices with their start and end apart: 6, of which 1 were waited for; matrix products, arithmetic and copies ran while one was open for 7% of the time, Pallas kernels for 12%

profile of v4, /device:TPU:1, one launch (start us, length us, event | category | flops | bytes accessed | tf_op | source)
XLA Modules:
  0.0 342.4 jit_solution(8280039068652029623)
XLA Ops:
  0.6 0.0 copy-start
  0.7 1.9 copy-done
  2.5 1.6 constant_dynamic-slice_fusion
  4.1 1.8 copy.56
  6.0 0.8 pad_maximum_fusion.2
  6.8 2.7 copy.44
  9.5 3.8 %all_to_all.16 = f32[16,1,6336]{2,1,0:T(1,128)} reshape(f32[3072,33]{1,0:T(8,128)} %copy.44) | data formatting | bytes 811008 | tf_op jit(solution)/shard_map/all_to_all | solution.py:206
  13.3 9.3 %all-to-all-start = ((f32[16,1,6336]{2,1,0:T(1,128)}), f32[16,1,6336]{2,1,0:T(1,128)}, u32[]{:S(2)}, u32[]{:S(2)}) async-start(f32[16,1,6336]{2,1,0:T(1,128)} %all_to_all.16), calls=%async_computation | async-start | bytes 819200 | tf_op jit(solution)/shard_map/all_to_all | solution.py:206
  22.6 0.9 fusion.39
  23.5 0.6 fusion.44
  24.1 2.0 collective-permute-start.2
  26.2 5.5 %collective-permute-start.3 = (f32[256]{0:T(256)}, f32[256]{0:T(256)}, u32[]{:S(2)}, u32[]{:S(2)}) collective-permute-start(f32[256]{0:T(256)} %bitcast.8), channel_id=1, source_target_pairs={{0,1},{1,2},{2,3},{3,4},{4,5},{5,6},{6,7},{7,8},{8,9},{9,10},{10,1... | collective-permute-start | bytes 3080 | tf_op jit(solution)/shard_map/ppermute | solution.py:17
  31.7 0.7 fusion.43
  32.4 3.6 %fusion.20 = f32[256,256]{1,0:T(8,128)} fusion(f32[256,2304]{1,0:T(8,128)} %param.7), kind=kOutput, calls=%fused_computation.31 | convolution fusion | flops 302579712 | bytes 2621440 | tf_op jit(solution)/shard_map/dot_general | solution.py:249
  36.0 10.7 %fusion.22 = f32[256,3072]{1,0:T(8,128)} fusion(bf16[3072,2304]{1,0:T(8,128)(2,1)} %param.5, f32[256,2304]{1,0:T(8,128)S(1)} %copy-done.2), kind=kOutput, calls=%fused_computation.33 | convolution fusion | flops 3624468480 | bytes 19660800 | tf_op jit(solution)/shard_map/dot_general | solution.py:248
  46.7 0.6 fusion.45
  47.3 0.0 collective-permute-done.2
  47.3 0.0 collective-permute-done.3
  47.3 0.9 fusion.35
  48.1 0.6 copy.62
  48.8 0.0 all-to-all-done
  48.8 2.7 reduce
  51.5 4.0 %reshape.118 = f32[3072,33]{1,0:T(8,128)} reshape(f32[16,6336]{1,0:T(8,128)} %reduce) | data formatting | bytes 811008 | tf_op jit(solution)/shard_map/reshape | solution.py:208
  55.5 2.9 fusion.7
  58.4 2.6 copy.57
  61.0 1.1 reduce-precision_convert_fusion.3
  62.1 8.4 %fusion.1 = f32[3072,96]{0,1:T(8,128)S(1)} fusion(s32[3072]{0:T(1024)} %fusion.7, bf16[3072,32]{0,1:T(8,128)(2,1)S(1)} %get-tuple-element.12, bf16[3072,32]{0,1:T(8,128)(2,1)S(1)} %get-tuple-element.13, bf16[3072,32]{0,1:T(8,128)(2,1)S(1)} %get-tuple-element.11), kind=kOutput, calls=%fused_computation.2 | convolution fusion | flops 1823145984 | bytes 1781760 | tf_op jit(solution)/shard_map/dot_general | solution.py:212
  70.5 0.8 slice_add_fusion.2
  71.3 1.9 reshape.119
  73.2 1.1 broadcast_multiply_fusion
  74.2 0.2 fusion.40
  74.5 1.9 collective-permute-start
  76.5 5.1 %collective-permute-start.1 = (f32[256,32]{0,1:T(8,128)S(1)}, f32[256,32]{0,1:T(8,128)S(1)}, u32[]{:S(2)}, u32[]{:S(2)}) collective-permute-start(f32[256,32]{0,1:T(8,128)S(1)} %bitcast.73), channel_id=1, source_target_pairs={{0,1},{1,2},{2,3},{3,4},{4,5},{5,6},{6,7},{7,8},{8,9},{9,10},{10,1... | collective-permute-start | bytes 98312 | tf_op jit(solution)/shard_map/ppermute | solution.py:17
  81.6 0.1 fusion.42
  81.7 0.0 collective-permute-done
  81.7 0.9 collective-permute-done.1
  82.6 0.3 fusion.26
  83.0 0.2 copy.61
  83.2 0.8 constant_dynamic-update-slice_fusion
  84.0 1.6 dynamic-update-slice.1
  85.5 1.1 reduce-precision_convert_fusion.1
  86.7 8.1 %fusion = f32[3072,99]{0,1:T(8,128)S(1)} fusion(s32[3072]{0:T(1024)S(1)} %copy-done.4, bf16[3072,33]{0,1:T(8,128)(2,1)S(1)} %get-tuple-element.9, bf16[3072,33]{0,1:T(8,128)(2,1)S(1)} %get-tuple-element.10, bf16[3072,33]{0,1:T(8,128)(2,1)S(1)} %get-tuple-element.8), kind=kOutput, calls=%fused_computation.1 | convolution fusion | flops 1879824384 | bytes 1837056 | tf_op jit(solution)/shard_map/dot_general | solution.py:230
  94.8 0.9 slice_add_fusion
  95.7 2.7 copy.49
  98.3 3.9 %all_to_all.17 = f32[16,1,6336]{2,1,0:T(1,128)} reshape(f32[3072,33]{1,0:T(8,128)} %copy.49) | data formatting | bytes 811008 | tf_op jit(solution)/shard_map/all_to_all | solution.py:232
  102.2 10.3 %all-to-all-start.1 = ((f32[16,1,6336]{2,1,0:T(1,128)}), f32[16,1,6336]{2,1,0:T(1,128)}, u32[]{:S(2)}, u32[]{:S(2)}) async-start(f32[16,1,6336]{2,1,0:T(1,128)} %all_to_all.17), calls=%async_computation.1 | async-start | bytes 819200 | tf_op jit(solution)/shard_map/all_to_all | solution.py:232
  112.4 3.9 %pad_maximum_fusion = f32[256,3328]{1,0:T(8,128)} fusion(f32[256,256]{1,0:T(8,128)} %fusion.20, f32[256,3072]{1,0:T(8,128)} %fusion.22), kind=kLoop, calls=%fused_computation.7 | loop fusion | flops 851968 | bytes 6815744 | tf_op jit(solution)/shard_map/concatenate | solution.py:250
  116.4 42.3 %shard_map.68 = f32[32,3328]{1,0:T(8,128)} custom-call(f32[8,32,3328]{2,1,0:T(8,128)} %bitcast.64), custom_call_target="tpu_custom_call" | custom-call | tf_op jit(solution)/shard_map/pallas_call | solution.py:171
  158.7 2.7 reduce.2
  161.5 4.0 %reshape.122 = f32[3072,33]{1,0:T(8,128)} reshape(f32[16,6336]{1,0:T(8,128)} %reduce.2) | data formatting | bytes 811008 | tf_op jit(solution)/shard_map/reshape | solution.py:234
  165.4 2.3 fusion.5
  167.8 2.6 copy.60
  170.4 4.8 %fusion.4.x_ref = f32[32,3072]{1,0:T(8,128)} fusion(f32[3072,256]{1,0:T(8,128)S(1)} %copy-done, f32[3072,32]{0,1:T(8,128)S(1)} %copy.56, f32[3072,32]{0,1:T(8,128)} %copy.60, f32[32,3328]{1,0:T(8,128)} %shard_map.68, f32[3072]{0:T(1024)S(1)} %fusion.5), kind=kOutput, calls=%fused_computation.6 | convolution fusion | flops 302579712 | bytes 4763648 | tf_op jit(solution)/shard_map/dot_general | solution.py:258
  175.2 37.3 %shard_map.69 = f32[8,32,3072]{2,1,0:T(8,128)} custom-call(f32[32,3072]{1,0:T(8,128)} %fusion.4.x_ref), custom_call_target="tpu_custom_call" | custom-call | tf_op jit(solution)/shard_map/pallas_call | solution.py:116
  212.5 3.4 convert_element_type.38
  215.9 8.5 %fusion.8 = f32[256,2304]{1,0:T(8,128)} fusion(bf16[3072,2304]{1,0:T(8,128)(2,1)} %param.5, f32[256,3072]{1,0:T(8,128)S(1)} %bitcast.60), kind=kOutput, calls=%fused_computation.15 | convolution fusion | flops 3624665088 | bytes 19660800 | tf_op jit(solution)/shard_map/dot_general | solution.py:265
  224.4 3.8 %copy.52 = f32[256,3072]{0,1:T(8,128)} copy(f32[256,3072]{1,0:T(8,128)} %bitcast.59) | data formatting | bytes 6291456 | tf_op jit(solution)/shard_map/reshape | solution.py:262
  228.2 0.0 copy-start.3
  228.2 2.6 fusion.46
  230.8 1.8 pad_maximum_fusion.1
  232.7 57.5 %shard_map.70 = f32[16,2560]{1,0:T(8,128)} custom-call(f32[16,16,2560]{2,1,0:T(8,128)} %bitcast.65), custom_call_target="tpu_custom_call" | custom-call | tf_op jit(solution)/shard_map/pallas_call | solution.py:171
  290.1 3.6 %convolution_divide_fusion.x_ref = f32[16,2304]{1,0:T(8,128)} fusion(f32[256,2304]{1,0:T(8,128)} %param.7, f32[16,2560]{1,0:T(8,128)} %shard_map.70, s32[]{:T(128)S(6)} %select_n.7), kind=kOutput, calls=%fused_computation.8 | convolution fusion | flops 113319936 | bytes 2818052 | tf_op jit(solution)/shard_map/dot_general | solution.py:271
  293.7 45.2 %shard_map.71 = f32[16,16,2304]{2,1,0:T(8,128)} custom-call(f32[16,2304]{1,0:T(8,128)} %convolution_divide_fusion.x_ref), custom_call_target="tpu_custom_call" | custom-call | tf_op jit(solution)/shard_map/pallas_call | solution.py:116
  338.9 3.2 copy.69
  (16 shorter events, 0.1 us)
Async XLA Ops:
  0.6 1.9 copy-start
  2.5 3.5 %copy-start.5 = (s32[3072]{0:T(1024)S(1)}, s32[3072]{0:T(1024)}, u32[]{:S(2)}) copy-start(s32[3072]{0:T(1024)} %param.8) | copy-start | bytes 36868
  13.3 35.4 %all-to-all-start = ((f32[16,1,6336]{2,1,0:T(1,128)}), f32[16,1,6336]{2,1,0:T(1,128)}, u32[]{:S(2)}, u32[]{:S(2)}) async-start(f32[16,1,6336]{2,1,0:T(1,128)} %all_to_all.16), calls=%async_computation | async-start | bytes 819200 | tf_op jit(solution)/shard_map/all_to_all | solution.py:206
  22.6 13.4 %copy-start.2 = (f32[256,2304]{1,0:T(8,128)S(1)}, f32[256,2304]{1,0:T(8,128)}, u32[]{:S(2)}) copy-start(f32[256,2304]{1,0:T(8,128)} %param.7) | copy-start | bytes 7077892
  24.1 23.2 %collective-permute-start.2 = (f32[256]{0:T(256)}, f32[256]{0:T(256)}, u32[]{:S(2)}, u32[]{:S(2)}) collective-permute-start(f32[256]{0:T(256)} %bitcast.6), channel_id=1, source_target_pairs={{1,0},{2,1},{3,2},{4,3},{5,4},{6,5},{7,6},{8,7},{9,8},{10,9},{11,1... | collective-permute-start | bytes 3080 | tf_op jit(solution)/shard_map/ppermute | solution.py:17
  26.2 21.1 %collective-permute-start.3 = (f32[256]{0:T(256)}, f32[256]{0:T(256)}, u32[]{:S(2)}, u32[]{:S(2)}) collective-permute-start(f32[256]{0:T(256)} %bitcast.8), channel_id=1, source_target_pairs={{0,1},{1,2},{2,3},{3,4},{4,5},{5,6},{6,7},{7,8},{8,9},{9,10},{10,1... | collective-permute-start | bytes 3080 | tf_op jit(solution)/shard_map/ppermute | solution.py:17
  74.5 7.2 %collective-permute-start = (f32[256,32]{0,1:T(8,128)S(1)}, f32[256,32]{0,1:T(8,128)S(1)}, u32[]{:S(2)}, u32[]{:S(2)}) collective-permute-start(f32[256,32]{0,1:T(8,128)S(1)} %bitcast.72), channel_id=1, source_target_pairs={{1,0},{2,1},{3,2},{4,3},{5,4},{6,5},{7,6},{8,7},{9,8},{10,9},{11,1... | collective-permute-start | bytes 98312 | tf_op jit(solution)/shard_map/ppermute | solution.py:17
  76.5 6.2 %collective-permute-start.1 = (f32[256,32]{0,1:T(8,128)S(1)}, f32[256,32]{0,1:T(8,128)S(1)}, u32[]{:S(2)}, u32[]{:S(2)}) collective-permute-start(f32[256,32]{0,1:T(8,128)S(1)} %bitcast.73), channel_id=1, source_target_pairs={{0,1},{1,2},{2,3},{3,4},{4,5},{5,6},{6,7},{7,8},{8,9},{9,10},{10,1... | collective-permute-start | bytes 98312 | tf_op jit(solution)/shard_map/ppermute | solution.py:17
  83.0 3.7 %copy-start.4 = (s32[3072]{0:T(1024)S(1)}, s32[3072]{0:T(1024)}, u32[]{:S(2)}) copy-start(s32[3072]{0:T(1024)} %fusion.7) | copy-start | bytes 36868
  102.2 56.6 %all-to-all-start.1 = ((f32[16,1,6336]{2,1,0:T(1,128)}), f32[16,1,6336]{2,1,0:T(1,128)}, u32[]{:S(2)}, u32[]{:S(2)}) async-start(f32[16,1,6336]{2,1,0:T(1,128)} %all_to_all.17), calls=%async_computation.1 | async-start | bytes 819200 | tf_op jit(solution)/shard_map/all_to_all | solution.py:232
  212.5 3.4 copy-start.1
  228.2 2.7 copy-start.3

commit v5 on v4

--- a/solution.py
+++ b/solution.py
@@ -248,7 +248,9 @@
     numer_part = lax.dot_general(load_bf, counts, right_dims, preferred_element_type=jnp.float32)
     gram_part = lax.dot_general(load_bf, load_bf, right_dims, preferred_element_type=jnp.float32)
     both = jnp.concatenate([numer_part, gram_part], 1)
-    both = ring_scatter(both.reshape(gene_count, width, -1), "gene", 1)
+    both = lax.psum_scatter(
+        both.reshape(gene_count, width, -1), "gene", scatter_dimension=0, tiled=True
+    ).reshape(width, -1)
     numer_t, gram_rows = both[:, :row_count], both[:, row_count:]
     own = lax.dynamic_slice_in_dim(factors, gene_at * width, width, 1)
     smooth, degree = stencil_term(own, position, edge_codes)
@@ -269,7 +271,7 @@
     cross, fac_gram = both_bin[:, : cross_part.shape[1]], both_bin[:, cross_part.shape[1] :]
     own_load = lax.dynamic_slice_in_dim(loadings, bin_at * k_rows, k_rows, 0)
     new_load = own_load * cross / jnp.dot(fac_gram, loadings, precision=lax.Precision.HIGHEST)
-    loadings_new = ring_gather(new_load, "bin", 3).reshape(width_all, -1)
+    loadings_new = lax.all_gather(new_load, "bin", axis=0, tiled=True)
     return (factors_new, loadings_new)
 
 

time: 347 us -> 321 us (0.925)
  Pallas kernels: 182 us -> 88.7 us
  waiting for transfers between devices: 0.88 us -> 62.9 us
  between operations: 1.18 us -> 14.6 us
  matrix products: 50.2 us -> 45.9 us
    pallas_call x2 -> x1, Pallas kernels: 99.8 us -> 48.8 us  [ring_scatter(): pl.pallas_call(functools.partial(scatter_kernel, axis, count), out_shape=...]
    all_gather x0 -> x1, waiting for transfers between devices: none -> 46.3 us  [on_device(): loadings_new = lax.all_gather(new_load, 'bin', axis=0, tiled=True)]
    pallas_call x2 -> x1, Pallas kernels: 82.5 us -> 39.9 us  [ring_gather(): pl.pallas_call(functools.partial(gather_kernel, axis, count), out_shape=j...]
    all_to_all x1, waiting for transfers between devices: 0.01 us -> 15.1 us  [stencil_term(): lax.all_to_all(back_rows.reshape(bin_count, group_size * (width + 1)), 'b...]
    unnamed x21 -> x25, local copies, waits for them, and re-layouts: 13.8 us -> 14.6 us
  transfers between devices with their start and end apart: 6 -> 8, of which waited for: 1 -> 4; matrix products, arithmetic and copies ran while one was open for 7% -> 24% of each run, Pallas kernels for 12% -> 0%
where the time goes in v5:
time: 321 us; the launch traced here: 317 us
  Pallas kernels  88.7 us (28%)
  waiting for transfers between devices  62.9 us (20%)
  local copies, waits for them, and re-layouts  46.5 us (14%)
  matrix products  45.9 us (14%)
  starting transfers between devices  32.2 us (10%)
  other arithmetic  25.9 us (8%)
  between operations  14.6 us (5%)
    pallas_call x1, Pallas kernels, ring_scatter(): pl.pallas_call(functools.partial(scatter_kernel, axis, count), out_shape=...  48.8 us
    all_gather x1, waiting for transfers between devices, on_device(): loadings_new = lax.all_gather(new_load, 'bin', axis=0, tiled=True)  46.3 us
    pallas_call x1, Pallas kernels, ring_gather(): pl.pallas_call(functools.partial(gather_kernel, axis, count), out_shape=j...  39.9 us
    all_to_all x1, waiting for transfers between devices, stencil_term(): lax.all_to_all(back_rows.reshape(bin_count, group_size * (width + 1)), 'b...  15.1 us
    unnamed x25, local copies, waits for them, and re-layouts  14.6 us
    ppermute x4, starting transfers between devices, passed_along(): return lax.ppermute(block, axis, route)  14.5 us
    dot_general x1, matrix products, on_device(): lax.dot_general(load_bf, counts, right_dims, preferred_element_type=jnp.f...  10.7 us
    all_to_all x1, starting transfers between devices, stencil_term(): lax.all_to_all(payload.reshape(bin_count, group_size * (width + 1)), 'bin...  9.29 us
  transfers between devices with their start and end apart: 8, of which 4 were waited for; matrix products, arithmetic and copies ran while one was open for 24% of the time, Pallas kernels for 0%

profile of v5, /device:TPU:1, one launch (start us, length us, event | category | flops | bytes accessed | tf_op | source)
XLA Modules:
  0.0 316.5 jit_solution(14256635464280937616)
XLA Ops:
  7.2 1.9 copy-done
  9.1 1.6 constant_dynamic-slice_fusion
  10.7 1.8 copy.56
  12.5 0.8 pad_maximum_fusion.2
  13.4 2.7 copy.44
  16.0 3.8 %all_to_all.16 = f32[16,1,6336]{2,1,0:T(1,128)} reshape(f32[3072,33]{1,0:T(8,128)} %copy.44) | data formatting | bytes 811008 | tf_op jit(solution)/shard_map/all_to_all | solution.py:206
  19.9 9.3 %all-to-all-start = ((f32[16,1,6336]{2,1,0:T(1,128)}), f32[16,1,6336]{2,1,0:T(1,128)}, u32[]{:S(2)}, u32[]{:S(2)}) async-start(f32[16,1,6336]{2,1,0:T(1,128)} %all_to_all.16), calls=%async_computation.1 | async-start | bytes 819200 | tf_op jit(solution)/shard_map/all_to_all | solution.py:206
  29.2 0.0 reduce-scatter.2.cloned.1.call-start
  29.2 0.9 fusion.39
  30.1 0.6 fusion.44
  30.7 5.0 %collective-permute-start.3 = (f32[256]{0:T(256)}, f32[256]{0:T(256)}, u32[]{:S(2)}, u32[]{:S(2)}) collective-permute-start(f32[256]{0:T(256)} %bitcast.9), channel_id=1, source_target_pairs={{0,1},{1,2},{2,3},{3,4},{4,5},{5,6},{6,7},{7,8},{8,9},{9,10},{10,1... | collective-permute-start | bytes 3080 | tf_op jit(solution)/shard_map/ppermute | solution.py:17
  35.7 2.4 collective-permute-start.2
  38.1 2.9 fusion.20
  41.0 10.7 %fusion.22 = f32[256,3072]{1,0:T(8,128)} fusion(bf16[3072,2304]{1,0:T(8,128)(2,1)} %param.5, f32[256,2304]{1,0:T(8,128)S(1)} %copy-done.2), kind=kOutput, calls=%fused_computation.33 | convolution fusion | flops 3624468480 | bytes 19660800 | tf_op jit(solution)/shard_map/dot_general | solution.py:248
  51.7 3.9 %pad_maximum_fusion = f32[256,3328]{1,0:T(8,128)} fusion(f32[256,256]{1,0:T(8,128)S(1)} %fusion.20, f32[256,3072]{1,0:T(8,128)} %fusion.22), kind=kLoop, calls=%fused_computation.7 | loop fusion | flops 851968 | bytes 6815744 | tf_op jit(solution)/shard_map/concatenate | solution.py:250
  55.5 0.0 reduce-scatter.2.cloned.1.call-update
  55.6 0.7 fusion.43
  56.2 0.6 fusion.45
  56.9 0.9 fusion.35
  57.7 0.6 copy.62
  58.3 2.7 reduce
  61.1 4.0 %reshape.119 = f32[3072,33]{1,0:T(8,128)} reshape(f32[16,6336]{1,0:T(8,128)} %reduce) | data formatting | bytes 811008 | tf_op jit(solution)/shard_map/reshape | solution.py:208
  65.0 2.9 copy.57
  67.9 2.3 fusion.7
  70.2 1.1 reduce-precision_convert_fusion.3
  71.3 7.7 %fusion.1 = f32[3072,96]{0,1:T(8,128)S(1)} fusion(s32[3072]{0:T(1024)S(1)} %fusion.7, bf16[3072,32]{0,1:T(8,128)(2,1)S(1)} %get-tuple-element.12, bf16[3072,32]{0,1:T(8,128)(2,1)S(1)} %get-tuple-element.13, bf16[3072,32]{0,1:T(8,128)(2,1)S(1)} %get-tuple-element.11), kind=kOutput, calls=%fused_computation.2 | convolution fusion | flops 1823145984 | bytes 1781760 | tf_op jit(solution)/shard_map/dot_general | solution.py:212
  79.0 0.8 slice_add_fusion.2
  79.8 1.9 reshape.120
  81.7 1.1 broadcast_multiply_fusion
  82.9 1.9 collective-permute-start
  84.8 5.1 %collective-permute-start.1 = (f32[256,32]{0,1:T(8,128)S(1)}, f32[256,32]{0,1:T(8,128)S(1)}, u32[]{:S(2)}, u32[]{:S(2)}) collective-permute-start(f32[256,32]{0,1:T(8,128)S(1)} %bitcast.68), channel_id=1, source_target_pairs={{0,1},{1,2},{2,3},{3,4},{4,5},{5,6},{6,7},{7,8},{8,9},{9,10},{10,1... | collective-permute-start | bytes 98312 | tf_op jit(solution)/shard_map/ppermute | solution.py:17
  90.0 0.2 fusion.40
  90.2 0.1 fusion.42
  90.3 0.6 collective-permute-done
  90.9 0.8 collective-permute-done.1
  91.7 0.3 fusion.26
  92.0 0.2 copy.61
  92.3 0.8 constant_dynamic-update-slice_fusion
  93.0 1.6 dynamic-update-slice.1
  94.6 1.1 reduce-precision_convert_fusion.1
  95.8 8.0 %fusion = f32[3072,99]{0,1:T(8,128)S(1)} fusion(s32[3072]{0:T(1024)S(1)} %copy-done.6, bf16[3072,33]{0,1:T(8,128)(2,1)S(1)} %get-tuple-element.9, bf16[3072,33]{0,1:T(8,128)(2,1)S(1)} %get-tuple-element.10, bf16[3072,33]{0,1:T(8,128)(2,1)S(1)} %get-tuple-element.8), kind=kOutput, calls=%fused_computation.1 | convolution fusion | flops 1879824384 | bytes 1837056 | tf_op jit(solution)/shard_map/dot_general | solution.py:230
  103.8 0.9 slice_add_fusion
  104.7 2.7 copy.49
  107.4 3.8 %all_to_all.17 = f32[16,1,6336]{2,1,0:T(1,128)} reshape(f32[3072,33]{1,0:T(8,128)} %copy.49) | data formatting | bytes 811008 | tf_op jit(solution)/shard_map/all_to_all | solution.py:232
  111.2 8.1 %all-to-all-start.1 = ((f32[16,1,6336]{2,1,0:T(1,128)}), f32[16,1,6336]{2,1,0:T(1,128)}, u32[]{:S(2)}, u32[]{:S(2)}) async-start(f32[16,1,6336]{2,1,0:T(1,128)} %all_to_all.17), calls=%async_computation.2 | async-start | bytes 819200 | tf_op jit(solution)/shard_map/all_to_all | solution.py:232
  119.3 0.2 all-gather.2.cloned.1.call-start
  119.6 15.1 %all-to-all-done.1 = f32[16,1,6336]{2,1,0:T(1,128)} async-done(((f32[16,1,6336]{2,1,0:T(1,128)}), f32[16,1,6336]{2,1,0:T(1,128)}, u32[]{:S(2)}, u32[]{:S(2)}) %all-to-all-start.1) | async-done | bytes 405536 | tf_op jit(solution)/shard_map/all_to_all | solution.py:232
  134.7 2.7 reduce.2
  137.4 4.0 %reshape.123 = f32[3072,33]{1,0:T(8,128)} reshape(f32[16,6336]{1,0:T(8,128)} %reduce.2) | data formatting | bytes 811008 | tf_op jit(solution)/shard_map/reshape | solution.py:234
  141.4 2.6 copy.60
  144.0 2.3 fusion.5
  146.3 0.0 reduce-scatter.2.cloned.1.call-done
  146.3 4.8 %fusion.4.x_ref = f32[32,3072]{1,0:T(8,128)} fusion(f32[3072,256]{1,0:T(8,128)S(1)} %copy-done, f32[32,3328]{1,0:T(8,128)} %bitcast.69, f32[3072,32]{0,1:T(8,128)S(1)} %copy.56, f32[3072,32]{0,1:T(8,128)} %copy.60, f32[3072]{0:T(1024)S(1)} %fusion.5), kind=kOutput, calls=%fused_computation.6 | convolution fusion | flops 302579712 | bytes 4763648 | tf_op jit(solution)/shard_map/dot_general | solution.py:260
  151.2 39.9 %shard_map.68 = f32[8,32,3072]{2,1,0:T(8,128)} custom-call(f32[32,3072]{1,0:T(8,128)} %fusion.4.x_ref), custom_call_target="tpu_custom_call" | custom-call | tf_op jit(solution)/shard_map/pallas_call | solution.py:116
  191.1 2.2 convert_element_type.38
  193.4 0.6 copy-done.1
  193.9 7.6 %fusion.8 = f32[256,2304]{1,0:T(8,128)S(1)} fusion(bf16[3072,2304]{1,0:T(8,128)(2,1)} %param.5, f32[256,3072]{1,0:T(8,128)S(1)} %bitcast.56), kind=kOutput, calls=%fused_computation.15 | convolution fusion | flops 3624665088 | bytes 19660800 | tf_op jit(solution)/shard_map/dot_general | solution.py:267
  201.5 0.6 fusion.46
  202.1 1.8 pad_maximum_fusion.1
  204.0 48.8 %shard_map.69 = f32[16,2560]{1,0:T(8,128)} custom-call(f32[16,16,2560]{2,1,0:T(8,128)} %bitcast.61), custom_call_target="tpu_custom_call" | custom-call | tf_op jit(solution)/shard_map/pallas_call | solution.py:171
  252.8 3.6 %convolution_divide_fusion = f32[16,2304]{1,0:T(8,128)} fusion(f32[256,2304]{1,0:T(8,128)} %param.7, f32[16,2560]{1,0:T(8,128)} %shard_map.69, s32[]{:T(128)S(6)} %select_n.7), kind=kOutput, calls=%fused_computation.8 | convolution fusion | flops 113319936 | bytes 2818052 | tf_op jit(solution)/shard_map/dot_general | solution.py:273
  256.3 3.5 %copy.52 = f32[256,3072]{0,1:T(8,128)} copy(f32[256,3072]{1,0:T(8,128)} %bitcast.55) | data formatting | bytes 6291456 | tf_op jit(solution)/shard_map/reshape | solution.py:264
  259.9 46.3 %all-gather.2.cloned.1.call-done = f32[256,2304]{1,0:T(8,128)} async-done(((f32[16,2304]{1,0:T(8,128)}), f32[256,2304]{1,0:T(8,128)}) %all-gather.2.cloned.1.call-update) | async-done | bytes 2359312 | tf_op jit(solution)/shard_map/all_gather | solution.py:274
  306.2 3.2 %copy.69 = f32[256,2304]{1,0:T(8,128)} copy(f32[256,2304]{1,0:T(8,128)} %all-gather.2.cloned.1.call-done) | data formatting | bytes 4718592
  (24 shorter events, 0.2 us)
Async XLA Ops:
  7.2 1.9 copy-start
  9.1 3.5 %copy-start.7 = (s32[3072]{0:T(1024)S(1)}, s32[3072]{0:T(1024)}, u32[]{:S(2)}) copy-start(s32[3072]{0:T(1024)} %param.8) | copy-start | bytes 36868
  19.9 38.5 %all-to-all-start = ((f32[16,1,6336]{2,1,0:T(1,128)}), f32[16,1,6336]{2,1,0:T(1,128)}, u32[]{:S(2)}, u32[]{:S(2)}) async-start(f32[16,1,6336]{2,1,0:T(1,128)} %all_to_all.16), calls=%async_computation.1 | async-start | bytes 819200 | tf_op jit(solution)/shard_map/all_to_all | solution.py:206
  29.2 117.2 %reduce-scatter.2.cloned.1.call-start = ((), (), s32[]{:S(2)}) async-start(), calls=%async_computation.3 | async-start | bytes 3833856 | tf_op jit(solution)/shard_map/reduce_scatter | solution.py:251
  29.2 11.8 %copy-start.2 = (f32[256,2304]{1,0:T(8,128)S(1)}, f32[256,2304]{1,0:T(8,128)}, u32[]{:S(2)}) copy-start(f32[256,2304]{1,0:T(8,128)} %param.7) | copy-start | bytes 7077892
  30.1 5.6 %copy-start.3 = (f32[12,256]{1,0:T(8,128)}, f32[12,256]{1,0:T(8,128)S(1)}, u32[]{:S(2)}) copy-start(f32[12,256]{1,0:T(8,128)S(1)} %get-tuple-element.21) | copy-start | bytes 36868
  30.7 26.2 %collective-permute-start.3 = (f32[256]{0:T(256)}, f32[256]{0:T(256)}, u32[]{:S(2)}, u32[]{:S(2)}) collective-permute-start(f32[256]{0:T(256)} %bitcast.9), channel_id=1, source_target_pairs={{0,1},{1,2},{2,3},{3,4},{4,5},{5,6},{6,7},{7,8},{8,9},{9,10},{10,1... | collective-permute-start | bytes 3080 | tf_op jit(solution)/shard_map/ppermute | solution.py:17
  35.7 21.1 %collective-permute-start.2 = (f32[256]{0:T(256)}, f32[256]{0:T(256)}, u32[]{:S(2)}, u32[]{:S(2)}) collective-permute-start(f32[256]{0:T(256)} %bitcast.7), channel_id=1, source_target_pairs={{1,0},{2,1},{3,2},{4,3},{5,4},{6,5},{7,6},{8,7},{9,8},{10,9},{11,1... | collective-permute-start | bytes 3080 | tf_op jit(solution)/shard_map/ppermute | solution.py:17
  70.2 8.8 %copy-start.5 = (s32[3072]{0:T(1024)}, s32[3072]{0:T(1024)S(1)}, u32[]{:S(2)}) copy-start(s32[3072]{0:T(1024)S(1)} %fusion.7) | copy-start | bytes 36868
  79.0 2.7 copy-start.4
  82.9 8.0 %collective-permute-start = (f32[256,32]{0,1:T(8,128)S(1)}, f32[256,32]{0,1:T(8,128)S(1)}, u32[]{:S(2)}, u32[]{:S(2)}) collective-permute-start(f32[256,32]{0,1:T(8,128)S(1)} %bitcast.67), channel_id=1, source_target_pairs={{1,0},{2,1},{3,2},{4,3},{5,4},{6,5},{7,6},{8,7},{9,8},{10,9},{11,1... | collective-permute-start | bytes 98312 | tf_op jit(solution)/shard_map/ppermute | solution.py:17
  84.8 6.9 %collective-permute-start.1 = (f32[256,32]{0,1:T(8,128)S(1)}, f32[256,32]{0,1:T(8,128)S(1)}, u32[]{:S(2)}, u32[]{:S(2)}) collective-permute-start(f32[256,32]{0,1:T(8,128)S(1)} %bitcast.68), channel_id=1, source_target_pairs={{0,1},{1,2},{2,3},{3,4},{4,5},{5,6},{6,7},{7,8},{8,9},{9,10},{10,1... | collective-permute-start | bytes 98312 | tf_op jit(solution)/shard_map/ppermute | solution.py:17
  92.0 3.8 %copy-start.6 = (s32[3072]{0:T(1024)S(1)}, s32[3072]{0:T(1024)}, u32[]{:S(2)}) copy-start(s32[3072]{0:T(1024)} %copy-done.5) | copy-start | bytes 36868
  111.2 23.5 %all-to-all-start.1 = ((f32[16,1,6336]{2,1,0:T(1,128)}), f32[16,1,6336]{2,1,0:T(1,128)}, u32[]{:S(2)}, u32[]{:S(2)}) async-start(f32[16,1,6336]{2,1,0:T(1,128)} %all_to_all.17), calls=%async_computation.2 | async-start | bytes 819200 | tf_op jit(solution)/shard_map/all_to_all | solution.py:232
  119.3 186.9 %all-gather.2.cloned.1.call-start = ((), (), s32[]{:S(2)}) async-start(), calls=%async_computation.4 | async-start | bytes 2506752 | tf_op jit(solution)/shard_map/all_gather | solution.py:274
  191.1 2.8 copy-start.1
Sparse Core Ops, SparseCore 0:
  55.7 82.4 reduce-scatter.1
  256.4 49.7 all-gather.1

commit v6 on v5

--- a/solution.py
+++ b/solution.py
@@ -178,6 +178,83 @@
             pltpu.VMEM((2, count - 1, rows, lanes // 2), x.dtype),
             pltpu.SemaphoreType.DMA((2, count - 1)),
             pltpu.SemaphoreType.DMA((2, count - 1)),
+        ],
+        compiler_params=pltpu.CompilerParams(
+            collective_id=collective_id, has_side_effects=True
+        ),
+    )(x)
+
+
+def greet_all(axis, me, count):
+    barrier = pltpu.get_barrier_semaphore()
+    for shift in range(1, count):
+        pl.semaphore_signal(barrier, inc=1, device_id={axis: (me + shift) % count},
+                            device_id_type=pl.DeviceIdType.MESH)
+    pl.semaphore_wait(barrier, count - 1)
+
+
+def exchange_kernel(axis, count, summed, x_ref, out_ref, *rest):
+    if summed:
+        got, send_sem, recv_sem = rest
+    else:
+        got, (send_sem, recv_sem) = out_ref, rest
+    me = lax.axis_index(axis)
+    greet_all(axis, me, count)
+
+    def copy(shift):
+        target = (me + shift) % count
+        return pltpu.make_async_remote_copy(
+            src_ref=x_ref.at[target] if summed else x_ref,
+            dst_ref=got.at[me],
+            send_sem=send_sem.at[shift],
+            recv_sem=recv_sem.at[me],
+            device_id={axis: target},
+            device_id_type=pl.DeviceIdType.MESH,
+        )
+
+    def arrival(shift):
+        origin = (me + count - shift) % count
+        return pltpu.make_async_remote_copy(
+            src_ref=x_ref.at[origin] if summed else x_ref,
+            dst_ref=got.at[origin],
+            send_sem=send_sem.at[shift],
+            recv_sem=recv_sem.at[origin],
+            device_id={axis: origin},
+            device_id_type=pl.DeviceIdType.MESH,
+        )
+
+    for shift in range(1, count):
+        copy(shift).start()
+    if summed:
+        total = x_ref[me]
+        for shift in range(1, count):
+            arrival(shift).wait_recv()
+            total = total + got[(me + count - shift) % count]
+        out_ref[...] = total
+    else:
+        out_ref[me] = x_ref[...]
+        for shift in range(1, count):
+            arrival(shift).wait_recv()
+    for shift in range(1, count):
+        copy(shift).wait_send()
+
+
+def exchange(x, axis, collective_id, summed):
+    count = lax.axis_size(axis)
+    if summed:
+        out_shape = x.shape[1:]
+        scratch = [pltpu.VMEM(x.shape, x.dtype)]
+    else:
+        out_shape = (count,) + x.shape
+        scratch = []
+    return pl.pallas_call(
+        functools.partial(exchange_kernel, axis, count, summed),
+        out_shape=jax.ShapeDtypeStruct(out_shape, x.dtype),
+        in_specs=[pl.BlockSpec(memory_space=pltpu.VMEM)],
+        out_specs=pl.BlockSpec(memory_space=pltpu.VMEM),
+        scratch_shapes=scratch + [
+            pltpu.SemaphoreType.DMA((count,)),
+            pltpu.SemaphoreType.DMA((count,)),
         ],
         compiler_params=pltpu.CompilerParams(
             collective_id=collective_id, has_side_effects=True
@@ -267,11 +344,11 @@
     cross_part = jnp.dot(fac_bf_t, counts, preferred_element_type=jnp.float32)
     fgram_part = lax.dot_general(fac_bf_t, fac_bf_t, right_dims, preferred_element_type=jnp.float32)
     both_bin = jnp.concatenate([cross_part, fgram_part], 1)
-    both_bin = ring_scatter(both_bin.reshape(bin_count, k_rows, -1), "bin", 2)
+    both_bin = exchange(both_bin.reshape(bin_count, k_rows, -1), "bin", 2, True)
     cross, fac_gram = both_bin[:, : cross_part.shape[1]], both_bin[:, cross_part.shape[1] :]
     own_load = lax.dynamic_slice_in_dim(loadings, bin_at * k_rows, k_rows, 0)
     new_load = own_load * cross / jnp.dot(fac_gram, loadings, precision=lax.Precision.HIGHEST)
-    loadings_new = lax.all_gather(new_load, "bin", axis=0, tiled=True)
+    loadings_new = exchange(new_load, "bin", 3, False).reshape(width_all, -1)
     return (factors_new, loadings_new)
 
 

time: 321 us -> 304 us (0.947)
  waiting for transfers between devices: 62.9 us -> 16.6 us
  Pallas kernels: 88.7 us -> 115 us
    all_gather x1 -> x0, waiting for transfers between devices: 46.3 us -> none  [on_device(): loadings_new = lax.all_gather(new_load, 'bin', axis=0, tiled=True)]
    pallas_call x1 -> x2, Pallas kernels: 48.8 us -> 74.6 us  [exchange(): pl.pallas_call(functools.partial(exchange_kernel, axis, count, summed), o...]
    unnamed x25 -> x27, local copies, waits for them, and re-layouts: 14.6 us -> 14.1 us
  transfers between devices with their start and end apart: 8 -> 7, of which waited for: 4 -> 3; matrix products, arithmetic and copies ran while one was open for 24% -> 25% of each run, Pallas kernels for 0% -> 0%
where the time goes in v6:
time: 304 us; the launch traced here: 300 us
  Pallas kernels  115 us (38%)
  matrix products  48.8 us (16%)
  local copies, waits for them, and re-layouts  45.9 us (15%)
  starting transfers between devices  32.3 us (11%)
  other arithmetic  27 us (9%)
  waiting for transfers between devices  16.6 us (5%)
  between operations  14.6 us (5%)
    pallas_call x2, Pallas kernels, exchange(): pl.pallas_call(functools.partial(exchange_kernel, axis, count, summed), o...  74.6 us
    pallas_call x1, Pallas kernels, ring_gather(): pl.pallas_call(functools.partial(gather_kernel, axis, count), out_shape=j...  39.9 us
    all_to_all x1, waiting for transfers between devices, stencil_term(): lax.all_to_all(back_rows.reshape(bin_count, group_size * (width + 1)), 'b...  15.2 us
    ppermute x4, starting transfers between devices, passed_along(): return lax.ppermute(block, axis, route)  14.5 us
    unnamed x27, local copies, waits for them, and re-layouts  14.1 us
    dot_general x1, matrix products, on_device(): lax.dot_general(load_bf, counts, right_dims, preferred_element_type=jnp.f...  10.7 us
    all_to_all x1, starting transfers between devices, stencil_term(): lax.all_to_all(payload.reshape(bin_count, group_size * (width + 1)), 'bin...  9.29 us
    dot_general x1, matrix products, on_device(): cross_part = jnp.dot(fac_bf_t, counts, preferred_element_type=jnp.float32)  8.49 us
  transfers between devices with their start and end apart: 7, of which 3 were waited for; matrix products, arithmetic and copies ran while one was open for 25% of the time, Pallas kernels for 0%

profile of v6, /device:TPU:1, one launch (start us, length us, event | category | flops | bytes accessed | tf_op | source)
XLA Modules:
  0.0 299.7 jit_solution(3491625055176102184)
XLA Ops:
  7.2 0.0 copy-start
  7.2 1.9 copy-done
  9.1 1.6 constant_dynamic-slice_fusion
  10.7 1.8 copy.56
  12.5 0.8 pad_maximum_fusion.2
  13.4 2.7 copy.44
  16.0 3.8 %all_to_all.16 = f32[16,1,6336]{2,1,0:T(1,128)} reshape(f32[3072,33]{1,0:T(8,128)} %copy.44) | data formatting | bytes 811008 | tf_op jit(solution)/shard_map/all_to_all | solution.py:283
  19.9 9.3 %all-to-all-start = ((f32[16,1,6336]{2,1,0:T(1,128)}), f32[16,1,6336]{2,1,0:T(1,128)}, u32[]{:S(2)}, u32[]{:S(2)}) async-start(f32[16,1,6336]{2,1,0:T(1,128)} %all_to_all.16), calls=%async_computation.1 | async-start | bytes 819200 | tf_op jit(solution)/shard_map/all_to_all | solution.py:283
  29.2 0.0 reduce-scatter.2.cloned.1.call-start
  29.2 0.0 copy-start.2
  29.2 0.9 fusion.39
  30.1 0.6 fusion.44
  30.7 5.0 %collective-permute-start.3 = (f32[256]{0:T(256)}, f32[256]{0:T(256)}, u32[]{:S(2)}, u32[]{:S(2)}) collective-permute-start(f32[256]{0:T(256)} %bitcast.9), channel_id=1, source_target_pairs={{0,1},{1,2},{2,3},{3,4},{4,5},{5,6},{6,7},{7,8},{8,9},{9,10},{10,1... | collective-permute-start | bytes 3080 | tf_op jit(solution)/shard_map/ppermute | solution.py:17
  35.7 2.4 collective-permute-start.2
  38.1 2.9 fusion.20
  41.0 10.7 %fusion.22 = f32[256,3072]{1,0:T(8,128)} fusion(bf16[3072,2304]{1,0:T(8,128)(2,1)} %param.5, f32[256,2304]{1,0:T(8,128)S(1)} %copy-done.2), kind=kOutput, calls=%fused_computation.33 | convolution fusion | flops 3624468480 | bytes 19660800 | tf_op jit(solution)/shard_map/dot_general | solution.py:325
  51.7 3.8 %pad_maximum_fusion = f32[256,3328]{1,0:T(8,128)} fusion(f32[256,256]{1,0:T(8,128)S(1)} %fusion.20, f32[256,3072]{1,0:T(8,128)} %fusion.22), kind=kLoop, calls=%fused_computation.7 | loop fusion | flops 851968 | bytes 6815744 | tf_op jit(solution)/shard_map/concatenate | solution.py:327
  55.5 0.0 reduce-scatter.2.cloned.1.call-update
  55.6 0.7 fusion.43
  56.2 0.6 fusion.45
  56.9 0.9 fusion.35
  57.7 0.6 copy.62
  58.3 2.7 reduce
  61.1 4.0 %reshape.122 = f32[3072,33]{1,0:T(8,128)} reshape(f32[16,6336]{1,0:T(8,128)} %reduce) | data formatting | bytes 811008 | tf_op jit(solution)/shard_map/reshape | solution.py:285
  65.0 2.9 copy.57
  67.9 2.3 fusion.7
  70.2 1.1 reduce-precision_convert_fusion.3
  71.3 7.7 %fusion.1 = f32[3072,96]{0,1:T(8,128)S(1)} fusion(s32[3072]{0:T(1024)S(1)} %fusion.7, bf16[3072,32]{0,1:T(8,128)(2,1)S(1)} %get-tuple-element.12, bf16[3072,32]{0,1:T(8,128)(2,1)S(1)} %get-tuple-element.13, bf16[3072,32]{0,1:T(8,128)(2,1)S(1)} %get-tuple-element.11), kind=kOutput, calls=%fused_computation.2 | convolution fusion | flops 1823145984 | bytes 1781760 | tf_op jit(solution)/shard_map/dot_general | solution.py:289
  79.0 0.8 slice_add_fusion.2
  79.8 1.9 reshape.123
  81.7 1.1 broadcast_multiply_fusion
  82.9 1.9 collective-permute-start
  84.8 5.1 %collective-permute-start.1 = (f32[256,32]{0,1:T(8,128)S(1)}, f32[256,32]{0,1:T(8,128)S(1)}, u32[]{:S(2)}, u32[]{:S(2)}) collective-permute-start(f32[256,32]{0,1:T(8,128)S(1)} %bitcast.70), channel_id=1, source_target_pairs={{0,1},{1,2},{2,3},{3,4},{4,5},{5,6},{6,7},{7,8},{8,9},{9,10},{10,1... | collective-permute-start | bytes 98312 | tf_op jit(solution)/shard_map/ppermute | solution.py:17
  90.0 0.2 fusion.40
  90.2 0.1 fusion.42
  90.3 0.6 collective-permute-done
  90.9 0.8 collective-permute-done.1
  91.7 0.3 fusion.26
  92.0 0.2 copy.61
  92.3 0.8 constant_dynamic-update-slice_fusion
  93.1 1.6 dynamic-update-slice.1
  94.6 1.1 reduce-precision_convert_fusion.1
  95.8 8.0 %fusion = f32[3072,99]{0,1:T(8,128)S(1)} fusion(s32[3072]{0:T(1024)S(1)} %copy-done.7, bf16[3072,33]{0,1:T(8,128)(2,1)S(1)} %get-tuple-element.9, bf16[3072,33]{0,1:T(8,128)(2,1)S(1)} %get-tuple-element.10, bf16[3072,33]{0,1:T(8,128)(2,1)S(1)} %get-tuple-element.8), kind=kOutput, calls=%fused_computation.1 | convolution fusion | flops 1879824384 | bytes 1837056 | tf_op jit(solution)/shard_map/dot_general | solution.py:307
  103.8 0.9 slice_add_fusion
  104.7 2.7 copy.49
  107.4 3.8 %all_to_all.17 = f32[16,1,6336]{2,1,0:T(1,128)} reshape(f32[3072,33]{1,0:T(8,128)} %copy.49) | data formatting | bytes 811008 | tf_op jit(solution)/shard_map/all_to_all | solution.py:309
  111.2 8.4 %all-to-all-start.1 = ((f32[16,1,6336]{2,1,0:T(1,128)}), f32[16,1,6336]{2,1,0:T(1,128)}, u32[]{:S(2)}, u32[]{:S(2)}) async-start(f32[16,1,6336]{2,1,0:T(1,128)} %all_to_all.17), calls=%async_computation.2 | async-start | bytes 819200 | tf_op jit(solution)/shard_map/all_to_all | solution.py:309
  119.7 15.2 %all-to-all-done.1 = f32[16,1,6336]{2,1,0:T(1,128)} async-done(((f32[16,1,6336]{2,1,0:T(1,128)}), f32[16,1,6336]{2,1,0:T(1,128)}, u32[]{:S(2)}, u32[]{:S(2)}) %all-to-all-start.1) | async-done | bytes 405536 | tf_op jit(solution)/shard_map/all_to_all | solution.py:309
  134.9 2.7 reduce.2
  137.6 4.0 %reshape.126 = f32[3072,33]{1,0:T(8,128)} reshape(f32[16,6336]{1,0:T(8,128)} %reduce.2) | data formatting | bytes 811008 | tf_op jit(solution)/shard_map/reshape | solution.py:311
  141.6 2.6 copy.60
  144.2 2.3 fusion.5
  146.5 0.0 reduce-scatter.2.cloned.1.call-done
  146.5 4.8 %fusion.4.x_ref = f32[32,3072]{1,0:T(8,128)} fusion(f32[3072,256]{1,0:T(8,128)S(1)} %copy-done, f32[32,3328]{1,0:T(8,128)} %bitcast.71, f32[3072,32]{0,1:T(8,128)S(1)} %copy.56, f32[3072,32]{0,1:T(8,128)} %copy.60, f32[3072]{0:T(1024)S(1)} %fusion.5), kind=kOutput, calls=%fused_computation.6 | convolution fusion | flops 302579712 | bytes 4763648 | tf_op jit(solution)/shard_map/dot_general | solution.py:337
  151.4 39.9 %shard_map.68 = f32[8,32,3072]{2,1,0:T(8,128)} custom-call(f32[32,3072]{1,0:T(8,128)} %fusion.4.x_ref), custom_call_target="tpu_custom_call" | custom-call | tf_op jit(solution)/shard_map/pallas_call | solution.py:116
  191.3 3.4 %convert_element_type.38 = bf16[8,32,3072]{2,1,0:T(8,128)(2,1)} convert(f32[8,32,3072]{2,1,0:T(8,128)} %shard_map.68) | non-fusion elementwise | flops 786432 | bytes 4718592 | tf_op jit(solution)/shard_map/convert_element_type | solution.py:343
  194.7 8.5 %fusion.8 = f32[256,2304]{1,0:T(8,128)} fusion(bf16[3072,2304]{1,0:T(8,128)(2,1)} %param.5, f32[256,3072]{1,0:T(8,128)S(1)} %bitcast.57), kind=kOutput, calls=%fused_computation.15 | convolution fusion | flops 3624665088 | bytes 19660800 | tf_op jit(solution)/shard_map/dot_general | solution.py:344
  203.2 3.5 %copy.52 = f32[256,3072]{0,1:T(8,128)} copy(f32[256,3072]{1,0:T(8,128)} %bitcast.56) | data formatting | bytes 6291456 | tf_op jit(solution)/shard_map/reshape | solution.py:341
  206.8 2.6 fusion.46
  209.4 1.8 pad_maximum_fusion.1
  211.2 40.6 %shard_map.69 = f32[16,2560]{1,0:T(8,128)} custom-call(f32[16,16,2560]{2,1,0:T(8,128)} %bitcast.62), custom_call_target="tpu_custom_call" | custom-call | tf_op jit(solution)/shard_map/pallas_call | solution.py:250
  251.8 3.6 %convolution_divide_fusion.x_ref = f32[16,2304]{1,0:T(8,128)} fusion(f32[256,2304]{1,0:T(8,128)} %param.7, f32[16,2560]{1,0:T(8,128)} %shard_map.69, s32[]{:T(128)S(6)} %select_n.7), kind=kOutput, calls=%fused_computation.8 | convolution fusion | flops 113319936 | bytes 2818052 | tf_op jit(solution)/shard_map/dot_general | solution.py:350
  255.3 34.1 %shard_map.70 = f32[16,16,2304]{2,1,0:T(8,128)} custom-call(f32[16,2304]{1,0:T(8,128)} %convolution_divide_fusion.x_ref), custom_call_target="tpu_custom_call" | custom-call | tf_op jit(solution)/shard_map/pallas_call | solution.py:250
  289.4 3.2 %copy.69 = f32[256,2304]{1,0:T(8,128)} copy(f32[256,2304]{1,0:T(8,128)} %bitcast.63) | data formatting | bytes 4718592
  (24 shorter events, 0.1 us)
Async XLA Ops:
  7.2 1.9 copy-start
  9.1 3.5 %copy-start.8 = (s32[3072]{0:T(1024)S(1)}, s32[3072]{0:T(1024)}, u32[]{:S(2)}) copy-start(s32[3072]{0:T(1024)} %param.8) | copy-start | bytes 36868
  19.9 38.5 %all-to-all-start = ((f32[16,1,6336]{2,1,0:T(1,128)}), f32[16,1,6336]{2,1,0:T(1,128)}, u32[]{:S(2)}, u32[]{:S(2)}) async-start(f32[16,1,6336]{2,1,0:T(1,128)} %all_to_all.16), calls=%async_computation.1 | async-start | bytes 819200 | tf_op jit(solution)/shard_map/all_to_all | solution.py:283
  29.2 117.4 %reduce-scatter.2.cloned.1.call-start = ((), (), s32[]{:S(2)}) async-start(), calls=%async_computation.3 | async-start | bytes 3833856 | tf_op jit(solution)/shard_map/reduce_scatter | solution.py:328
  29.2 11.8 %copy-start.2 = (f32[256,2304]{1,0:T(8,128)S(1)}, f32[256,2304]{1,0:T(8,128)}, u32[]{:S(2)}) copy-start(f32[256,2304]{1,0:T(8,128)} %param.7) | copy-start | bytes 7077892
  30.1 5.6 %copy-start.4 = (f32[12,256]{1,0:T(8,128)}, f32[12,256]{1,0:T(8,128)S(1)}, u32[]{:S(2)}) copy-start(f32[12,256]{1,0:T(8,128)S(1)} %get-tuple-element.21) | copy-start | bytes 36868
  30.7 26.2 %collective-permute-start.3 = (f32[256]{0:T(256)}, f32[256]{0:T(256)}, u32[]{:S(2)}, u32[]{:S(2)}) collective-permute-start(f32[256]{0:T(256)} %bitcast.9), channel_id=1, source_target_pairs={{0,1},{1,2},{2,3},{3,4},{4,5},{5,6},{6,7},{7,8},{8,9},{9,10},{10,1... | collective-permute-start | bytes 3080 | tf_op jit(solution)/shard_map/ppermute | solution.py:17
  35.7 21.1 %collective-permute-start.2 = (f32[256]{0:T(256)}, f32[256]{0:T(256)}, u32[]{:S(2)}, u32[]{:S(2)}) collective-permute-start(f32[256]{0:T(256)} %bitcast.7), channel_id=1, source_target_pairs={{1,0},{2,1},{3,2},{4,3},{5,4},{6,5},{7,6},{8,7},{9,8},{10,9},{11,1... | collective-permute-start | bytes 3080 | tf_op jit(solution)/shard_map/ppermute | solution.py:17
  70.2 8.8 %copy-start.6 = (s32[3072]{0:T(1024)}, s32[3072]{0:T(1024)S(1)}, u32[]{:S(2)}) copy-start(s32[3072]{0:T(1024)S(1)} %fusion.7) | copy-start | bytes 36868
  79.0 2.7 copy-start.5
  82.9 8.0 %collective-permute-start = (f32[256,32]{0,1:T(8,128)S(1)}, f32[256,32]{0,1:T(8,128)S(1)}, u32[]{:S(2)}, u32[]{:S(2)}) collective-permute-start(f32[256,32]{0,1:T(8,128)S(1)} %bitcast.69), channel_id=1, source_target_pairs={{1,0},{2,1},{3,2},{4,3},{5,4},{6,5},{7,6},{8,7},{9,8},{10,9},{11,1... | collective-permute-start | bytes 98312 | tf_op jit(solution)/shard_map/ppermute | solution.py:17
  84.8 6.9 %collective-permute-start.1 = (f32[256,32]{0,1:T(8,128)S(1)}, f32[256,32]{0,1:T(8,128)S(1)}, u32[]{:S(2)}, u32[]{:S(2)}) collective-permute-start(f32[256,32]{0,1:T(8,128)S(1)} %bitcast.70), channel_id=1, source_target_pairs={{0,1},{1,2},{2,3},{3,4},{4,5},{5,6},{6,7},{7,8},{8,9},{9,10},{10,1... | collective-permute-start | bytes 98312 | tf_op jit(solution)/shard_map/ppermute | solution.py:17
  92.0 3.8 %copy-start.7 = (s32[3072]{0:T(1024)S(1)}, s32[3072]{0:T(1024)}, u32[]{:S(2)}) copy-start(s32[3072]{0:T(1024)} %copy-done.6) | copy-start | bytes 36868
  111.2 23.7 %all-to-all-start.1 = ((f32[16,1,6336]{2,1,0:T(1,128)}), f32[16,1,6336]{2,1,0:T(1,128)}, u32[]{:S(2)}, u32[]{:S(2)}) async-start(f32[16,1,6336]{2,1,0:T(1,128)} %all_to_all.17), calls=%async_computation.2 | async-start | bytes 819200 | tf_op jit(solution)/shard_map/all_to_all | solution.py:309
  191.3 3.4 %copy-start.1 = (f32[8,32,3072]{2,1,0:T(8,128)S(1)}, f32[8,32,3072]{2,1,0:T(8,128)}, u32[]{:S(2)}) copy-start(f32[8,32,3072]{2,1,0:T(8,128)} %shard_map.68) | copy-start | bytes 9437188
  206.8 2.6 copy-start.3
Sparse Core Ops, SparseCore 0:
  55.7 82.4 reduce-scatter.1

commit v7 on v6

--- a/solution.py
+++ b/solution.py
@@ -338,7 +338,7 @@
         + penalty * degree[None, :] * own_t
     )
     new_t = own_t * (numer_t + penalty * smooth.T) / denom_t
-    factors_t = ring_gather(new_t, "gene", 0).reshape(width_all, row_count)
+    factors_t = exchange(new_t, "gene", 0, False).reshape(width_all, row_count)
     factors_new = factors_t.T
     fac_bf_t = factors_t.astype(jnp.bfloat16)
     cross_part = jnp.dot(fac_bf_t, counts, preferred_element_type=jnp.float32)

time: 304 us -> 302 us (level)
    pallas_call x1 -> x0, Pallas kernels: 39.9 us -> none  [ring_gather(): pl.pallas_call(functools.partial(gather_kernel, axis, count), out_shape=j...]
    pallas_call x2 -> x3, Pallas kernels: 74.6 us -> 112 us  [exchange(): pl.pallas_call(functools.partial(exchange_kernel, axis, count, summed), o...]
where the time goes in v7:
time: 302 us; the launch traced here: 297 us
  Pallas kernels  112 us (37%)
  matrix products  48.8 us (16%)
  local copies, waits for them, and re-layouts  45.9 us (15%)
  starting transfers between devices  32.3 us (11%)
  other arithmetic  27 us (9%)
  waiting for transfers between devices  16.6 us (5%)
  between operations  14.6 us (5%)
    pallas_call x3, Pallas kernels, exchange(): pl.pallas_call(functools.partial(exchange_kernel, axis, count, summed), o...  112 us
    all_to_all x1, waiting for transfers between devices, stencil_term(): lax.all_to_all(back_rows.reshape(bin_count, group_size * (width + 1)), 'b...  15.2 us
    ppermute x4, starting transfers between devices, passed_along(): return lax.ppermute(block, axis, route)  14.5 us
    unnamed x27, local copies, waits for them, and re-layouts  14.1 us
    dot_general x1, matrix products, on_device(): lax.dot_general(load_bf, counts, right_dims, preferred_element_type=jnp.f...  10.7 us
    all_to_all x1, starting transfers between devices, stencil_term(): lax.all_to_all(payload.reshape(bin_count, group_size * (width + 1)), 'bin...  9.29 us
    dot_general x1, matrix products, on_device(): cross_part = jnp.dot(fac_bf_t, counts, preferred_element_type=jnp.float32)  8.51 us
    all_to_all x1, starting transfers between devices, stencil_term(): lax.all_to_all(back_rows.reshape(bin_count, group_size * (width + 1)), 'b...  8.44 us
  transfers between devices with their start and end apart: 7, of which 3 were waited for; matrix products, arithmetic and copies ran while one was open for 25% of the time, Pallas kernels for 0%

profile of v7, /device:TPU:1, one launch (start us, length us, event | category | flops | bytes accessed | tf_op | source)
XLA Modules:
  0.0 297.4 jit_solution(6559153195821497304)
XLA Ops:
  7.2 0.0 copy-start
  7.2 1.9 copy-done
  9.1 1.6 constant_dynamic-slice_fusion
  10.7 1.8 copy.56
  12.5 0.8 pad_maximum_fusion.2
  13.4 2.7 copy.44
  16.0 3.8 %all_to_all.16 = f32[16,1,6336]{2,1,0:T(1,128)} reshape(f32[3072,33]{1,0:T(8,128)} %copy.44) | data formatting | bytes 811008 | tf_op jit(solution)/shard_map/all_to_all | solution.py:283
  19.9 9.3 %all-to-all-start = ((f32[16,1,6336]{2,1,0:T(1,128)}), f32[16,1,6336]{2,1,0:T(1,128)}, u32[]{:S(2)}, u32[]{:S(2)}) async-start(f32[16,1,6336]{2,1,0:T(1,128)} %all_to_all.16), calls=%async_computation.1 | async-start | bytes 819200 | tf_op jit(solution)/shard_map/all_to_all | solution.py:283
  29.2 0.0 reduce-scatter.2.cloned.1.call-start
  29.2 0.0 copy-start.2
  29.2 0.9 fusion.39
  30.1 0.6 fusion.44
  30.7 5.0 %collective-permute-start.3 = (f32[256]{0:T(256)}, f32[256]{0:T(256)}, u32[]{:S(2)}, u32[]{:S(2)}) collective-permute-start(f32[256]{0:T(256)} %bitcast.9), channel_id=1, source_target_pairs={{0,1},{1,2},{2,3},{3,4},{4,5},{5,6},{6,7},{7,8},{8,9},{9,10},{10,1... | collective-permute-start | bytes 3080 | tf_op jit(solution)/shard_map/ppermute | solution.py:17
  35.7 2.4 collective-permute-start.2
  38.1 2.9 fusion.20
  41.0 10.7 %fusion.22 = f32[256,3072]{1,0:T(8,128)} fusion(bf16[3072,2304]{1,0:T(8,128)(2,1)} %param.5, f32[256,2304]{1,0:T(8,128)S(1)} %copy-done.2), kind=kOutput, calls=%fused_computation.33 | convolution fusion | flops 3624468480 | bytes 19660800 | tf_op jit(solution)/shard_map/dot_general | solution.py:325
  51.7 3.8 %pad_maximum_fusion = f32[256,3328]{1,0:T(8,128)} fusion(f32[256,256]{1,0:T(8,128)S(1)} %fusion.20, f32[256,3072]{1,0:T(8,128)} %fusion.22), kind=kLoop, calls=%fused_computation.7 | loop fusion | flops 851968 | bytes 6815744 | tf_op jit(solution)/shard_map/concatenate | solution.py:327
  55.5 0.0 reduce-scatter.2.cloned.1.call-update
  55.6 0.7 fusion.43
  56.2 0.6 fusion.45
  56.9 0.9 fusion.35
  57.7 0.6 copy.62
  58.3 2.7 reduce
  61.1 4.0 %reshape.122 = f32[3072,33]{1,0:T(8,128)} reshape(f32[16,6336]{1,0:T(8,128)} %reduce) | data formatting | bytes 811008 | tf_op jit(solution)/shard_map/reshape | solution.py:285
  65.0 2.9 copy.57
  67.9 2.3 fusion.7
  70.2 1.1 reduce-precision_convert_fusion.3
  71.3 7.7 %fusion.1 = f32[3072,96]{0,1:T(8,128)S(1)} fusion(s32[3072]{0:T(1024)S(1)} %fusion.7, bf16[3072,32]{0,1:T(8,128)(2,1)S(1)} %get-tuple-element.12, bf16[3072,32]{0,1:T(8,128)(2,1)S(1)} %get-tuple-element.13, bf16[3072,32]{0,1:T(8,128)(2,1)S(1)} %get-tuple-element.11), kind=kOutput, calls=%fused_computation.2 | convolution fusion | flops 1823145984 | bytes 1781760 | tf_op jit(solution)/shard_map/dot_general | solution.py:289
  79.0 0.8 slice_add_fusion.2
  79.8 1.9 reshape.123
  81.7 1.1 broadcast_multiply_fusion
  82.9 1.9 collective-permute-start
  84.8 5.1 %collective-permute-start.1 = (f32[256,32]{0,1:T(8,128)S(1)}, f32[256,32]{0,1:T(8,128)S(1)}, u32[]{:S(2)}, u32[]{:S(2)}) collective-permute-start(f32[256,32]{0,1:T(8,128)S(1)} %bitcast.70), channel_id=1, source_target_pairs={{0,1},{1,2},{2,3},{3,4},{4,5},{5,6},{6,7},{7,8},{8,9},{9,10},{10,1... | collective-permute-start | bytes 98312 | tf_op jit(solution)/shard_map/ppermute | solution.py:17
  90.0 0.2 fusion.40
  90.2 0.1 fusion.42
  90.3 0.6 collective-permute-done
  90.9 0.8 collective-permute-done.1
  91.7 0.3 fusion.26
  92.0 0.2 copy.61
  92.3 0.8 constant_dynamic-update-slice_fusion
  93.1 1.6 dynamic-update-slice.1
  94.6 1.1 reduce-precision_convert_fusion.1
  95.8 8.0 %fusion = f32[3072,99]{0,1:T(8,128)S(1)} fusion(s32[3072]{0:T(1024)S(1)} %copy-done.7, bf16[3072,33]{0,1:T(8,128)(2,1)S(1)} %get-tuple-element.9, bf16[3072,33]{0,1:T(8,128)(2,1)S(1)} %get-tuple-element.10, bf16[3072,33]{0,1:T(8,128)(2,1)S(1)} %get-tuple-element.8), kind=kOutput, calls=%fused_computation.1 | convolution fusion | flops 1879824384 | bytes 1837056 | tf_op jit(solution)/shard_map/dot_general | solution.py:307
  103.8 0.9 slice_add_fusion
  104.7 2.7 copy.49
  107.4 3.8 %all_to_all.17 = f32[16,1,6336]{2,1,0:T(1,128)} reshape(f32[3072,33]{1,0:T(8,128)} %copy.49) | data formatting | bytes 811008 | tf_op jit(solution)/shard_map/all_to_all | solution.py:309
  111.2 8.4 %all-to-all-start.1 = ((f32[16,1,6336]{2,1,0:T(1,128)}), f32[16,1,6336]{2,1,0:T(1,128)}, u32[]{:S(2)}, u32[]{:S(2)}) async-start(f32[16,1,6336]{2,1,0:T(1,128)} %all_to_all.17), calls=%async_computation.2 | async-start | bytes 819200 | tf_op jit(solution)/shard_map/all_to_all | solution.py:309
  119.7 15.2 %all-to-all-done.1 = f32[16,1,6336]{2,1,0:T(1,128)} async-done(((f32[16,1,6336]{2,1,0:T(1,128)}), f32[16,1,6336]{2,1,0:T(1,128)}, u32[]{:S(2)}, u32[]{:S(2)}) %all-to-all-start.1) | async-done | bytes 405536 | tf_op jit(solution)/shard_map/all_to_all | solution.py:309
  134.9 2.7 reduce.2
  137.6 4.0 %reshape.126 = f32[3072,33]{1,0:T(8,128)} reshape(f32[16,6336]{1,0:T(8,128)} %reduce.2) | data formatting | bytes 811008 | tf_op jit(solution)/shard_map/reshape | solution.py:311
  141.6 2.6 copy.60
  144.2 2.3 fusion.5
  146.5 0.0 reduce-scatter.2.cloned.1.call-done
  146.5 4.8 %fusion.4.x_ref = f32[32,3072]{1,0:T(8,128)} fusion(f32[3072,256]{1,0:T(8,128)S(1)} %copy-done, f32[32,3328]{1,0:T(8,128)} %bitcast.71, f32[3072,32]{0,1:T(8,128)S(1)} %copy.56, f32[3072,32]{0,1:T(8,128)} %copy.60, f32[3072]{0:T(1024)S(1)} %fusion.5), kind=kOutput, calls=%fused_computation.6 | convolution fusion | flops 302579712 | bytes 4763648 | tf_op jit(solution)/shard_map/dot_general | solution.py:337
  151.4 40.9 %shard_map.68 = f32[8,32,3072]{2,1,0:T(8,128)} custom-call(f32[32,3072]{1,0:T(8,128)} %fusion.4.x_ref), custom_call_target="tpu_custom_call" | custom-call | tf_op jit(solution)/shard_map/pallas_call | solution.py:250
  192.2 3.4 %convert_element_type.38 = bf16[8,32,3072]{2,1,0:T(8,128)(2,1)} convert(f32[8,32,3072]{2,1,0:T(8,128)} %shard_map.68) | non-fusion elementwise | flops 786432 | bytes 4718592 | tf_op jit(solution)/shard_map/convert_element_type | solution.py:343
  195.6 8.5 %fusion.8 = f32[256,2304]{1,0:T(8,128)} fusion(bf16[3072,2304]{1,0:T(8,128)(2,1)} %param.5, f32[256,3072]{1,0:T(8,128)S(1)} %bitcast.57), kind=kOutput, calls=%fused_computation.15 | convolution fusion | flops 3624665088 | bytes 19660800 | tf_op jit(solution)/shard_map/dot_general | solution.py:344
  204.2 3.5 %copy.52 = f32[256,3072]{0,1:T(8,128)} copy(f32[256,3072]{1,0:T(8,128)} %bitcast.56) | data formatting | bytes 6291456 | tf_op jit(solution)/shard_map/reshape | solution.py:341
  207.7 2.6 fusion.46
  210.4 1.8 pad_maximum_fusion.1
  212.2 37.3 %shard_map.69 = f32[16,2560]{1,0:T(8,128)} custom-call(f32[16,16,2560]{2,1,0:T(8,128)} %bitcast.62), custom_call_target="tpu_custom_call" | custom-call | tf_op jit(solution)/shard_map/pallas_call | solution.py:250
  249.4 3.6 %convolution_divide_fusion.x_ref = f32[16,2304]{1,0:T(8,128)} fusion(f32[256,2304]{1,0:T(8,128)} %param.7, f32[16,2560]{1,0:T(8,128)} %shard_map.69, s32[]{:T(128)S(6)} %select_n.7), kind=kOutput, calls=%fused_computation.8 | convolution fusion | flops 113319936 | bytes 2818052 | tf_op jit(solution)/shard_map/dot_general | solution.py:350
  253.0 34.1 %shard_map.70 = f32[16,16,2304]{2,1,0:T(8,128)} custom-call(f32[16,2304]{1,0:T(8,128)} %convolution_divide_fusion.x_ref), custom_call_target="tpu_custom_call" | custom-call | tf_op jit(solution)/shard_map/pallas_call | solution.py:250
  287.1 3.2 %copy.69 = f32[256,2304]{1,0:T(8,128)} copy(f32[256,2304]{1,0:T(8,128)} %bitcast.63) | data formatting | bytes 4718592
  (24 shorter events, 0.1 us)
Async XLA Ops:
  7.2 1.9 copy-start
  9.1 3.5 %copy-start.8 = (s32[3072]{0:T(1024)S(1)}, s32[3072]{0:T(1024)}, u32[]{:S(2)}) copy-start(s32[3072]{0:T(1024)} %param.8) | copy-start | bytes 36868
  19.9 38.5 %all-to-all-start = ((f32[16,1,6336]{2,1,0:T(1,128)}), f32[16,1,6336]{2,1,0:T(1,128)}, u32[]{:S(2)}, u32[]{:S(2)}) async-start(f32[16,1,6336]{2,1,0:T(1,128)} %all_to_all.16), calls=%async_computation.1 | async-start | bytes 819200 | tf_op jit(solution)/shard_map/all_to_all | solution.py:283
  29.2 117.4 %reduce-scatter.2.cloned.1.call-start = ((), (), s32[]{:S(2)}) async-start(), calls=%async_computation.3 | async-start | bytes 3833856 | tf_op jit(solution)/shard_map/reduce_scatter | solution.py:328
  29.2 11.8 %copy-start.2 = (f32[256,2304]{1,0:T(8,128)S(1)}, f32[256,2304]{1,0:T(8,128)}, u32[]{:S(2)}) copy-start(f32[256,2304]{1,0:T(8,128)} %param.7) | copy-start | bytes 7077892
  30.1 5.6 %copy-start.4 = (f32[12,256]{1,0:T(8,128)}, f32[12,256]{1,0:T(8,128)S(1)}, u32[]{:S(2)}) copy-start(f32[12,256]{1,0:T(8,128)S(1)} %get-tuple-element.21) | copy-start | bytes 36868
  30.7 26.2 %collective-permute-start.3 = (f32[256]{0:T(256)}, f32[256]{0:T(256)}, u32[]{:S(2)}, u32[]{:S(2)}) collective-permute-start(f32[256]{0:T(256)} %bitcast.9), channel_id=1, source_target_pairs={{0,1},{1,2},{2,3},{3,4},{4,5},{5,6},{6,7},{7,8},{8,9},{9,10},{10,1... | collective-permute-start | bytes 3080 | tf_op jit(solution)/shard_map/ppermute | solution.py:17
  35.7 21.1 %collective-permute-start.2 = (f32[256]{0:T(256)}, f32[256]{0:T(256)}, u32[]{:S(2)}, u32[]{:S(2)}) collective-permute-start(f32[256]{0:T(256)} %bitcast.7), channel_id=1, source_target_pairs={{1,0},{2,1},{3,2},{4,3},{5,4},{6,5},{7,6},{8,7},{9,8},{10,9},{11,1... | collective-permute-start | bytes 3080 | tf_op jit(solution)/shard_map/ppermute | solution.py:17
  70.2 8.8 %copy-start.6 = (s32[3072]{0:T(1024)}, s32[3072]{0:T(1024)S(1)}, u32[]{:S(2)}) copy-start(s32[3072]{0:T(1024)S(1)} %fusion.7) | copy-start | bytes 36868
  79.0 2.7 copy-start.5
  82.9 8.0 %collective-permute-start = (f32[256,32]{0,1:T(8,128)S(1)}, f32[256,32]{0,1:T(8,128)S(1)}, u32[]{:S(2)}, u32[]{:S(2)}) collective-permute-start(f32[256,32]{0,1:T(8,128)S(1)} %bitcast.69), channel_id=1, source_target_pairs={{1,0},{2,1},{3,2},{4,3},{5,4},{6,5},{7,6},{8,7},{9,8},{10,9},{11,1... | collective-permute-start | bytes 98312 | tf_op jit(solution)/shard_map/ppermute | solution.py:17
  84.8 6.9 %collective-permute-start.1 = (f32[256,32]{0,1:T(8,128)S(1)}, f32[256,32]{0,1:T(8,128)S(1)}, u32[]{:S(2)}, u32[]{:S(2)}) collective-permute-start(f32[256,32]{0,1:T(8,128)S(1)} %bitcast.70), channel_id=1, source_target_pairs={{0,1},{1,2},{2,3},{3,4},{4,5},{5,6},{6,7},{7,8},{8,9},{9,10},{10,1... | collective-permute-start | bytes 98312 | tf_op jit(solution)/shard_map/ppermute | solution.py:17
  92.0 3.8 %copy-start.7 = (s32[3072]{0:T(1024)S(1)}, s32[3072]{0:T(1024)}, u32[]{:S(2)}) copy-start(s32[3072]{0:T(1024)} %copy-done.6) | copy-start | bytes 36868
  111.2 23.7 %all-to-all-start.1 = ((f32[16,1,6336]{2,1,0:T(1,128)}), f32[16,1,6336]{2,1,0:T(1,128)}, u32[]{:S(2)}, u32[]{:S(2)}) async-start(f32[16,1,6336]{2,1,0:T(1,128)} %all_to_all.17), calls=%async_computation.2 | async-start | bytes 819200 | tf_op jit(solution)/shard_map/all_to_all | solution.py:309
  192.2 3.4 %copy-start.1 = (f32[8,32,3072]{2,1,0:T(8,128)S(1)}, f32[8,32,3072]{2,1,0:T(8,128)}, u32[]{:S(2)}) copy-start(f32[8,32,3072]{2,1,0:T(8,128)} %shard_map.68) | copy-start | bytes 9437188
  207.7 2.6 copy-start.3
Sparse Core Ops, SparseCore 0:
  55.7 82.4 reduce-scatter.1

commit v8 on v7

--- a/solution.py
+++ b/solution.py
@@ -193,18 +193,19 @@
     pl.semaphore_wait(barrier, count - 1)
 
 
-def exchange_kernel(axis, count, summed, x_ref, out_ref, *rest):
-    if summed:
+def exchange_kernel(axis, count, mode, x_ref, out_ref, *rest):
+    if mode == "sum":
         got, send_sem, recv_sem = rest
     else:
         got, (send_sem, recv_sem) = out_ref, rest
     me = lax.axis_index(axis)
     greet_all(axis, me, count)
+    split = mode != "gather"
 
     def copy(shift):
         target = (me + shift) % count
         return pltpu.make_async_remote_copy(
-            src_ref=x_ref.at[target] if summed else x_ref,
+            src_ref=x_ref.at[target] if split else x_ref,
             dst_ref=got.at[me],
             send_sem=send_sem.at[shift],
             recv_sem=recv_sem.at[me],
@@ -215,7 +216,7 @@
     def arrival(shift):
         origin = (me + count - shift) % count
         return pltpu.make_async_remote_copy(
-            src_ref=x_ref.at[origin] if summed else x_ref,
+            src_ref=x_ref.at[origin] if split else x_ref,
             dst_ref=got.at[origin],
             send_sem=send_sem.at[shift],
             recv_sem=recv_sem.at[origin],
@@ -225,30 +226,32 @@
 
     for shift in range(1, count):
         copy(shift).start()
-    if summed:
+    if mode == "sum":
         total = x_ref[me]
         for shift in range(1, count):
             arrival(shift).wait_recv()
             total = total + got[(me + count - shift) % count]
         out_ref[...] = total
     else:
-        out_ref[me] = x_ref[...]
+        out_ref[me] = x_ref[me] if split else x_ref[...]
         for shift in range(1, count):
             arrival(shift).wait_recv()
     for shift in range(1, count):
         copy(shift).wait_send()
 
 
-def exchange(x, axis, collective_id, summed):
+def exchange(x, axis, collective_id, mode):
     count = lax.axis_size(axis)
-    if summed:
+    scratch = []
+    if mode == "sum":
         out_shape = x.shape[1:]
         scratch = [pltpu.VMEM(x.shape, x.dtype)]
+    elif mode == "gather":
+        out_shape = (count,) + x.shape
     else:
-        out_shape = (count,) + x.shape
-        scratch = []
+        out_shape = x.shape
     return pl.pallas_call(
-        functools.partial(exchange_kernel, axis, count, summed),
+        functools.partial(exchange_kernel, axis, count, mode),
         out_shape=jax.ShapeDtypeStruct(out_shape, x.dtype),
         in_specs=[pl.BlockSpec(memory_space=pltpu.VMEM)],
         out_specs=pl.BlockSpec(memory_space=pltpu.VMEM),
@@ -262,6 +265,15 @@
     )(x)
 
 
+def swap_rows(rows, collective_id):
+    bin_count = lax.axis_size("bin")
+    row_count, width = rows.shape
+    wide = 48
+    padded = jnp.pad(rows, ((0, 0), (0, wide - width)))
+    moved = exchange(padded.reshape(bin_count, -1, 128), "bin", collective_id, "swap")
+    return moved.reshape(row_count, wide)[:, :width]
+
+
 def split_three(values):
     high = lax.reduce_precision(values, exponent_bits=8, mantissa_bits=7)
     rest = values - high
@@ -280,9 +292,7 @@
     group_size = row_count // bin_count
     grid_rows, grid_cols = edge_codes.shape
     payload = jnp.concatenate([own, position.astype(jnp.float32)[:, None]], 1)
-    got = lax.all_to_all(
-        payload.reshape(bin_count, group_size * (width + 1)), "bin", 0, 0, tiled=True
-    ).reshape(row_count, width + 1)
+    got = swap_rows(payload, 4)
     tile_slot = got[:, width].astype(jnp.int32) - lax.axis_index("bin") * row_count
     cells = lax.broadcasted_iota(jnp.int32, (row_count, row_count), 1)
     onehot = (tile_slot[:, None] == cells).astype(jnp.bfloat16)
@@ -306,9 +316,7 @@
     back_rows = join_three(
         jnp.dot(onehot, split_three(back), preferred_element_type=jnp.float32), width + 1
     )
-    ret = lax.all_to_all(
-        back_rows.reshape(bin_count, group_size * (width + 1)), "bin", 0, 0, tiled=True
-    ).reshape(row_count, width + 1)
+    ret = swap_rows(back_rows, 5)
     return (ret[:, :width], ret[:, width])
 
 
@@ -338,17 +346,17 @@
         + penalty * degree[None, :] * own_t
     )
     new_t = own_t * (numer_t + penalty * smooth.T) / denom_t
-    factors_t = exchange(new_t, "gene", 0, False).reshape(width_all, row_count)
+    factors_t = exchange(new_t, "gene", 0, "gather").reshape(width_all, row_count)
     factors_new = factors_t.T
     fac_bf_t = factors_t.astype(jnp.bfloat16)
     cross_part = jnp.dot(fac_bf_t, counts, preferred_element_type=jnp.float32)
     fgram_part = lax.dot_general(fac_bf_t, fac_bf_t, right_dims, preferred_element_type=jnp.float32)
     both_bin = jnp.concatenate([cross_part, fgram_part], 1)
-    both_bin = exchange(both_bin.reshape(bin_count, k_rows, -1), "bin", 2, True)
+    both_bin = exchange(both_bin.reshape(bin_count, k_rows, -1), "bin", 2, "sum")
     cross, fac_gram = both_bin[:, : cross_part.shape[1]], both_bin[:, cross_part.shape[1] :]
     own_load = lax.dynamic_slice_in_dim(loadings, bin_at * k_rows, k_rows, 0)
     new_load = own_load * cross / jnp.dot(fac_gram, loadings, precision=lax.Precision.HIGHEST)
-    loadings_new = exchange(new_load, "bin", 3, False).reshape(width_all, -1)
+    loadings_new = exchange(new_load, "bin", 3, "gather").reshape(width_all, -1)
     return (factors_new, loadings_new)
 
 

time: 302 us -> 309 us (1.023)
  Pallas kernels: 112 us -> 154 us
  starting transfers between devices: 32.3 us -> 12.4 us
  waiting for transfers between devices: 16.6 us -> 1.11 us
  local copies, waits for them, and re-layouts: 45.9 us -> 50.5 us
  other arithmetic: 27 us -> 22.9 us
    pallas_call x3 -> x5, Pallas kernels: 112 us -> 154 us  [exchange(): pl.pallas_call(functools.partial(exchange_kernel, axis, count, mode), out...]
    all_to_all x2 -> x0, starting transfers between devices: 17.7 us -> none  [the longest x1 9.29 us: stencil_term(): lax.all_to_all(payload.reshape(bin_count, group_size * (width + 1)), 'bin...]
    all_to_all x2 -> x0, waiting for transfers between devices: 15.2 us -> none  [the longest x1 15.2 us: stencil_term(): lax.all_to_all(back_rows.reshape(bin_count, group_size * (width + 1)), 'b...]
    all_to_all x2 -> x0, local copies, waits for them, and re-layouts: 7.68 us -> none  [the longest x1 3.85 us: stencil_term(): lax.all_to_all(payload.reshape(bin_count, group_size * (width + 1)), 'bin...]
    all_to_all x2 -> x0, other arithmetic: 5.45 us -> none  [the longest x1 2.73 us: stencil_term(): lax.all_to_all(payload.reshape(bin_count, group_size * (width + 1)), 'bin...]
    pad x0 -> x2, local copies, waits for them, and re-layouts: none -> 5.31 us  [swap_rows(): padded = jnp.pad(rows, ((0, 0), (0, wide - width)))]
    unnamed x27 -> x25, local copies, waits for them, and re-layouts: 14.1 us -> 18.7 us
    reshape x3 -> x5, local copies, waits for them, and re-layouts: 11.5 us -> 15.7 us  [the longest x2 6.57 us: swap_rows(): padded.reshape(bin_count, -1, 128)]
  transfers between devices with their start and end apart: 7 -> 5, of which waited for: 3 -> 1; matrix products, arithmetic and copies ran while one was open for 25% -> 24% of each run, Pallas kernels for 0% -> 13%
where the time goes in v8:
time: 309 us; the launch traced here: 304 us
  Pallas kernels  154 us (50%)
  local copies, waits for them, and re-layouts  50.5 us (16%)
  matrix products  48.8 us (16%)
  other arithmetic  22.9 us (7%)
  between operations  14.5 us (5%)
  starting transfers between devices  12.4 us (4%)
    pallas_call x5, Pallas kernels, exchange(): pl.pallas_call(functools.partial(exchange_kernel, axis, count, mode), out...  154 us
    unnamed x25, local copies, waits for them, and re-layouts  18.7 us
    ppermute x4, starting transfers between devices, passed_along(): return lax.ppermute(block, axis, route)  12.4 us
    dot_general x1, matrix products, on_device(): lax.dot_general(load_bf, counts, right_dims, preferred_element_type=jnp.f...  10.7 us
    dot_general x1, matrix products, on_device(): cross_part = jnp.dot(fac_bf_t, counts, preferred_element_type=jnp.float32)  8.5 us
    dot_general x1, matrix products, stencil_term(): jnp.dot(onehot, split_three(back), preferred_element_type=jnp.float32)  8.05 us
    dot_general x1, matrix products, stencil_term(): lax.dot_general(onehot, split_three(got[:, :width]), (((0,), (0,)), ((),...  7.54 us
    reshape x2, local copies, waits for them, and re-layouts, swap_rows(): padded.reshape(bin_count, -1, 128)  6.57 us
  transfers between devices with their start and end apart: 5, of which 1 were waited for; matrix products, arithmetic and copies ran while one was open for 24% of the time, Pallas kernels for 13%

profile of v8, /device:TPU:1, one launch (start us, length us, event | category | flops | bytes accessed | tf_op | source)
XLA Modules:
  0.0 303.9 jit_solution(277786129758343411)
XLA Ops:
  7.2 0.0 reduce-scatter.2.cloned.1.call-start
  7.2 3.0 %fusion.20 = f32[256,256]{1,0:T(8,128)S(1)} fusion(f32[256,2304]{1,0:T(8,128)} %param.7), kind=kOutput, calls=%fused_computation.31 | convolution fusion | flops 302579712 | bytes 2621440 | tf_op jit(solution)/shard_map/dot_general | solution.py:334
  10.3 0.2 copy-done.2
  10.5 10.7 %fusion.22 = f32[256,3072]{1,0:T(8,128)} fusion(bf16[3072,2304]{1,0:T(8,128)(2,1)} %param.5, f32[256,2304]{1,0:T(8,128)S(1)} %copy-done.2), kind=kOutput, calls=%fused_computation.33 | convolution fusion | flops 3624468480 | bytes 19660800 | tf_op jit(solution)/shard_map/dot_general | solution.py:333
  21.1 3.8 %pad_maximum_fusion = f32[256,3328]{1,0:T(8,128)} fusion(f32[256,256]{1,0:T(8,128)S(1)} %fusion.20, f32[256,3072]{1,0:T(8,128)} %fusion.22), kind=kLoop, calls=%fused_computation.7 | loop fusion | flops 851968 | bytes 6815744 | tf_op jit(solution)/shard_map/concatenate | solution.py:335
  25.0 0.0 reduce-scatter.2.cloned.1.call-update
  25.0 1.6 constant_dynamic-slice_fusion
  26.6 1.8 copy.44
  28.5 0.8 pad_maximum_fusion.2
  29.3 2.7 copy.49
  32.0 2.7 pad.23.clone
  34.6 3.3 %reshape.118.x_ref = f32[16,72,128]{2,1,0:T(8,128)} reshape(f32[3072,48]{1,0:T(8,128)} %pad.23.clone) | data formatting | bytes 1179648 | tf_op jit(solution)/shard_map/reshape | solution.py:273
  38.0 24.5 %shard_map.68 = f32[16,72,128]{2,1,0:T(8,128)} custom-call(f32[16,72,128]{2,1,0:T(8,128)} %reshape.118.x_ref), custom_call_target="tpu_custom_call" | custom-call | tf_op jit(solution)/shard_map/pallas_call | solution.py:253
  62.5 2.8 reshape.119
  65.3 2.3 fusion.7
  67.6 2.6 copy.45
  70.2 1.1 reduce-precision_convert_fusion.3
  71.3 7.5 %fusion.1 = f32[3072,96]{0,1:T(8,128)S(1)} fusion(s32[3072]{0:T(1024)S(1)} %fusion.7, bf16[3072,32]{0,1:T(8,128)(2,1)S(1)} %get-tuple-element.12, bf16[3072,32]{0,1:T(8,128)(2,1)S(1)} %get-tuple-element.13, bf16[3072,32]{0,1:T(8,128)(2,1)S(1)} %get-tuple-element.11), kind=kOutput, calls=%fused_computation.2 | convolution fusion | flops 1823145984 | bytes 1781760 | tf_op jit(solution)/shard_map/dot_general | solution.py:299
  78.9 0.8 slice_add_fusion.2
  79.7 1.9 reshape.120
  81.6 0.7 fusion.39
  82.3 1.1 broadcast_multiply_fusion
  83.4 0.6 copy.56
  84.1 1.9 collective-permute-start
  86.0 0.6 copy.55
  86.6 5.1 %collective-permute-start.1 = (f32[256,32]{0,1:T(8,128)}, f32[256,32]{0,1:T(8,128)}, u32[]{:S(2)}, u32[]{:S(2)}) collective-permute-start(f32[256,32]{0,1:T(8,128)} %bitcast.52), channel_id=1, source_target_pairs={{0,1},{1,2},{2,3},{3,4},{4,5},{5,6},{6,7},{7,8},{8,9},{9,10},{10,1... | collective-permute-start | bytes 98312 | tf_op jit(solution)/shard_map/ppermute | solution.py:17
  91.7 0.6 fusion.44
  92.3 2.1 collective-permute-start.3
  94.4 3.3 %collective-permute-start.2 = (f32[256]{0:T(256)}, f32[256]{0:T(256)}, u32[]{:S(2)}, u32[]{:S(2)}) collective-permute-start(f32[256]{0:T(256)} %bitcast.7), channel_id=1, source_target_pairs={{1,0},{2,1},{3,2},{4,3},{5,4},{6,5},{7,6},{8,7},{9,8},{10,9},{11,1... | collective-permute-start | bytes 3080 | tf_op jit(solution)/shard_map/ppermute | solution.py:17
  97.7 0.7 fusion.43
  98.4 1.1 fusion.40
  99.5 1.0 fusion.42
  100.5 0.6 fusion.45
  101.2 1.1 collective-permute-done.2
  102.2 0.9 fusion.35
  103.1 0.6 copy.52
  103.7 0.8 broadcast_in_dim.16
  104.5 0.8 broadcast_in_dim.17
  105.3 1.8 fusion.26
  107.1 0.2 copy.51
  107.4 0.8 constant_dynamic-update-slice_fusion
  108.2 1.6 dynamic-update-slice.1
  109.7 1.1 reduce-precision_convert_fusion.1
  110.9 8.0 %fusion = f32[3072,99]{0,1:T(8,128)S(1)} fusion(s32[3072]{0:T(1024)S(1)} %copy-done.5, bf16[3072,33]{0,1:T(8,128)(2,1)S(1)} %get-tuple-element.9, bf16[3072,33]{0,1:T(8,128)(2,1)S(1)} %get-tuple-element.10, bf16[3072,33]{0,1:T(8,128)(2,1)S(1)} %get-tuple-element.8), kind=kOutput, calls=%fused_computation.1 | convolution fusion | flops 1879824384 | bytes 1837056 | tf_op jit(solution)/shard_map/dot_general | solution.py:317
  118.9 0.9 slice_add_fusion
  119.8 2.7 copy.50
  122.5 2.7 pad.28.clone
  125.1 3.2 %reshape.123.x_ref = f32[16,72,128]{2,1,0:T(8,128)} reshape(f32[3072,48]{1,0:T(8,128)} %pad.28.clone) | data formatting | bytes 1179648 | tf_op jit(solution)/shard_map/reshape | solution.py:273
  128.4 16.3 %shard_map.69 = f32[16,72,128]{2,1,0:T(8,128)} custom-call(f32[16,72,128]{2,1,0:T(8,128)} %reshape.123.x_ref), custom_call_target="tpu_custom_call" | custom-call | tf_op jit(solution)/shard_map/pallas_call | solution.py:253
  144.7 2.8 reshape.124
  147.5 2.6 copy.48
  150.1 2.3 fusion.5
  152.4 0.0 reduce-scatter.2.cloned.1.call-done
  152.4 4.8 %fusion.4.x_ref = f32[32,3072]{1,0:T(8,128)} fusion(f32[3072,256]{1,0:T(8,128)S(1)} %copy-done, f32[32,3328]{1,0:T(8,128)} %bitcast.69, f32[3072,32]{0,1:T(8,128)S(1)} %copy.44, f32[3072,32]{0,1:T(8,128)} %copy.48, f32[3072]{0:T(1024)S(1)} %fusion.5), kind=kOutput, calls=%fused_computation.6 | convolution fusion | flops 302579712 | bytes 4763648 | tf_op jit(solution)/shard_map/dot_general | solution.py:345
  157.2 40.8 %shard_map.70 = f32[8,32,3072]{2,1,0:T(8,128)} custom-call(f32[32,3072]{1,0:T(8,128)} %fusion.4.x_ref), custom_call_target="tpu_custom_call" | custom-call | tf_op jit(solution)/shard_map/pallas_call | solution.py:253
  198.0 3.4 %convert_element_type.41 = bf16[8,32,3072]{2,1,0:T(8,128)(2,1)} convert(f32[8,32,3072]{2,1,0:T(8,128)} %shard_map.70) | non-fusion elementwise | flops 786432 | bytes 4718592 | tf_op jit(solution)/shard_map/convert_element_type | solution.py:351
  201.4 8.5 %fusion.8 = f32[256,2304]{1,0:T(8,128)} fusion(bf16[3072,2304]{1,0:T(8,128)(2,1)} %param.5, f32[256,3072]{1,0:T(8,128)S(1)} %bitcast.57), kind=kOutput, calls=%fused_computation.15 | convolution fusion | flops 3624665088 | bytes 19660800 | tf_op jit(solution)/shard_map/dot_general | solution.py:352
  209.9 3.5 %copy.40 = f32[256,3072]{0,1:T(8,128)} copy(f32[256,3072]{1,0:T(8,128)} %bitcast.56) | data formatting | bytes 6291456 | tf_op jit(solution)/shard_map/reshape | solution.py:349
  213.5 2.6 fusion.46
  216.1 1.8 pad_maximum_fusion.1
  217.9 37.9 %shard_map.71 = f32[16,2560]{1,0:T(8,128)} custom-call(f32[16,16,2560]{2,1,0:T(8,128)} %bitcast.62), custom_call_target="tpu_custom_call" | custom-call | tf_op jit(solution)/shard_map/pallas_call | solution.py:253
  255.8 3.6 %convolution_divide_fusion.x_ref = f32[16,2304]{1,0:T(8,128)} fusion(f32[256,2304]{1,0:T(8,128)} %param.7, f32[16,2560]{1,0:T(8,128)} %shard_map.71, s32[]{:T(128)S(6)} %select_n.7), kind=kOutput, calls=%fused_computation.8 | convolution fusion | flops 113319936 | bytes 2818052 | tf_op jit(solution)/shard_map/dot_general | solution.py:358
  259.4 34.3 %shard_map.72 = f32[16,16,2304]{2,1,0:T(8,128)} custom-call(f32[16,2304]{1,0:T(8,128)} %convolution_divide_fusion.x_ref), custom_call_target="tpu_custom_call" | custom-call | tf_op jit(solution)/shard_map/pallas_call | solution.py:253
  293.6 3.2 %copy.59 = f32[256,2304]{1,0:T(8,128)} copy(f32[256,2304]{1,0:T(8,128)} %bitcast.63) | data formatting | bytes 4718592
  (18 shorter events, 0.1 us)
Async XLA Ops:
  7.2 17.8 %copy-start = (f32[3072,256]{1,0:T(8,128)S(1)}, f32[3072,256]{1,0:T(8,128)}, u32[]{:S(2)}) copy-start(f32[3072,256]{1,0:T(8,128)} %param.6) | copy-start | bytes 9437188
  7.2 145.2 %reduce-scatter.2.cloned.1.call-start = ((), (), s32[]{:S(2)}) async-start(), calls=%async_computation.1 | async-start | bytes 3833856 | tf_op jit(solution)/shard_map/reduce_scatter | solution.py:336
  7.2 3.2 %copy-start.2 = (f32[256,2304]{1,0:T(8,128)S(1)}, f32[256,2304]{1,0:T(8,128)}, u32[]{:S(2)}) copy-start(f32[256,2304]{1,0:T(8,128)} %param.7) | copy-start | bytes 7077892
  25.0 3.5 %copy-start.6 = (s32[3072]{0:T(1024)S(1)}, s32[3072]{0:T(1024)}, u32[]{:S(2)}) copy-start(s32[3072]{0:T(1024)} %param.8) | copy-start | bytes 36868
  67.6 11.3 %copy-start.4 = (s32[3072]{0:T(1024)}, s32[3072]{0:T(1024)S(1)}, u32[]{:S(2)}) copy-start(s32[3072]{0:T(1024)S(1)} %fusion.7) | copy-start | bytes 36868
  84.1 19.7 %collective-permute-start = (f32[256,32]{0,1:T(8,128)}, f32[256,32]{0,1:T(8,128)}, u32[]{:S(2)}, u32[]{:S(2)}) collective-permute-start(f32[256,32]{0,1:T(8,128)} %bitcast.53), channel_id=1, source_target_pairs={{1,0},{2,1},{3,2},{4,3},{5,4},{6,5},{7,6},{8,7},{9,8},{10,9},{11,1... | collective-permute-start | bytes 98312 | tf_op jit(solution)/shard_map/ppermute | solution.py:17
  86.6 17.9 %collective-permute-start.1 = (f32[256,32]{0,1:T(8,128)}, f32[256,32]{0,1:T(8,128)}, u32[]{:S(2)}, u32[]{:S(2)}) collective-permute-start(f32[256,32]{0,1:T(8,128)} %bitcast.52), channel_id=1, source_target_pairs={{0,1},{1,2},{2,3},{3,4},{4,5},{5,6},{6,7},{7,8},{8,9},{9,10},{10,1... | collective-permute-start | bytes 98312 | tf_op jit(solution)/shard_map/ppermute | solution.py:17
  92.3 8.8 %collective-permute-start.3 = (f32[256]{0:T(256)}, f32[256]{0:T(256)}, u32[]{:S(2)}, u32[]{:S(2)}) collective-permute-start(f32[256]{0:T(256)} %bitcast.9), channel_id=1, source_target_pairs={{0,1},{1,2},{2,3},{3,4},{4,5},{5,6},{6,7},{7,8},{8,9},{9,10},{10,1... | collective-permute-start | bytes 3080 | tf_op jit(solution)/shard_map/ppermute | solution.py:17
  94.4 7.8 %collective-permute-start.2 = (f32[256]{0:T(256)}, f32[256]{0:T(256)}, u32[]{:S(2)}, u32[]{:S(2)}) collective-permute-start(f32[256]{0:T(256)} %bitcast.7), channel_id=1, source_target_pairs={{1,0},{2,1},{3,2},{4,3},{5,4},{6,5},{7,6},{8,7},{9,8},{10,9},{11,1... | collective-permute-start | bytes 3080 | tf_op jit(solution)/shard_map/ppermute | solution.py:17
  107.1 3.7 %copy-start.5 = (s32[3072]{0:T(1024)S(1)}, s32[3072]{0:T(1024)}, u32[]{:S(2)}) copy-start(s32[3072]{0:T(1024)} %copy-done.4) | copy-start | bytes 36868
  198.0 3.4 %copy-start.1 = (f32[8,32,3072]{2,1,0:T(8,128)S(1)}, f32[8,32,3072]{2,1,0:T(8,128)}, u32[]{:S(2)}) copy-start(f32[8,32,3072]{2,1,0:T(8,128)} %shard_map.70) | copy-start | bytes 9437188
  213.5 2.6 copy-start.3
Sparse Core Ops, SparseCore 0:
  25.1 86.3 reduce-scatter.1

commit v9 on v7

--- a/solution.py
+++ b/solution.py
@@ -260,6 +260,92 @@
             collective_id=collective_id, has_side_effects=True
         ),
     )(x)
+
+
+def loadings_kernel(count, x_ref, own_ref, load_ref, out_ref, got, sem_a, sem_b, sem_c, sem_d):
+    me = lax.axis_index("bin")
+    greet_all("bin", me, count)
+
+    def partial_copy(shift):
+        target = (me + shift) % count
+        return pltpu.make_async_remote_copy(
+            src_ref=x_ref.at[target],
+            dst_ref=got.at[me],
+            send_sem=sem_a.at[shift],
+            recv_sem=sem_b.at[me],
+            device_id={"bin": target},
+            device_id_type=pl.DeviceIdType.MESH,
+        )
+
+    def partial_arrival(shift):
+        origin = (me + count - shift) % count
+        return pltpu.make_async_remote_copy(
+            src_ref=x_ref.at[origin],
+            dst_ref=got.at[origin],
+            send_sem=sem_a.at[shift],
+            recv_sem=sem_b.at[origin],
+            device_id={"bin": origin},
+            device_id_type=pl.DeviceIdType.MESH,
+        )
+
+    def result_copy(shift):
+        target = (me + shift) % count
+        return pltpu.make_async_remote_copy(
+            src_ref=out_ref.at[me],
+            dst_ref=out_ref.at[me],
+            send_sem=sem_c.at[shift],
+            recv_sem=sem_d.at[me],
+            device_id={"bin": target},
+            device_id_type=pl.DeviceIdType.MESH,
+        )
+
+    def result_arrival(shift):
+        origin = (me + count - shift) % count
+        return pltpu.make_async_remote_copy(
+            src_ref=out_ref.at[origin],
+            dst_ref=out_ref.at[origin],
+            send_sem=sem_c.at[shift],
+            recv_sem=sem_d.at[origin],
+            device_id={"bin": origin},
+            device_id_type=pl.DeviceIdType.MESH,
+        )
+
+    for shift in range(1, count):
+        partial_copy(shift).start()
+    total = x_ref[me]
+    for shift in range(1, count):
+        partial_arrival(shift).wait_recv()
+        total = total + got[(me + count - shift) % count]
+    genes = own_ref.shape[1]
+    denom = jnp.dot(
+        total[:, genes:], load_ref[...], precision=lax.Precision.HIGHEST,
+        preferred_element_type=jnp.float32,
+    )
+    out_ref[me] = own_ref[...] * total[:, :genes] / denom
+    for shift in range(1, count):
+        partial_copy(shift).wait_send()
+    for shift in range(1, count):
+        result_copy(shift).start()
+    for shift in range(1, count):
+        result_arrival(shift).wait_recv()
+    for shift in range(1, count):
+        result_copy(shift).wait_send()
+
+
+def loadings_update(parts, own_load, loadings, collective_id):
+    count = lax.axis_size("bin")
+    vmem = pl.BlockSpec(memory_space=pltpu.VMEM)
+    return pl.pallas_call(
+        functools.partial(loadings_kernel, count),
+        out_shape=jax.ShapeDtypeStruct((count,) + own_load.shape, own_load.dtype),
+        in_specs=[vmem, vmem, vmem],
+        out_specs=vmem,
+        scratch_shapes=[pltpu.VMEM(parts.shape, parts.dtype)]
+        + [pltpu.SemaphoreType.DMA((count,))] * 4,
+        compiler_params=pltpu.CompilerParams(
+            collective_id=collective_id, has_side_effects=True
+        ),
+    )(parts, own_load, loadings)
 
 
 def split_three(values):
@@ -344,11 +430,10 @@
     cross_part = jnp.dot(fac_bf_t, counts, preferred_element_type=jnp.float32)
     fgram_part = lax.dot_general(fac_bf_t, fac_bf_t, right_dims, preferred_element_type=jnp.float32)
     both_bin = jnp.concatenate([cross_part, fgram_part], 1)
-    both_bin = exchange(both_bin.reshape(bin_count, k_rows, -1), "bin", 2, True)
-    cross, fac_gram = both_bin[:, : cross_part.shape[1]], both_bin[:, cross_part.shape[1] :]
     own_load = lax.dynamic_slice_in_dim(loadings, bin_at * k_rows, k_rows, 0)
-    new_load = own_load * cross / jnp.dot(fac_gram, loadings, precision=lax.Precision.HIGHEST)
-    loadings_new = exchange(new_load, "bin", 3, False).reshape(width_all, -1)
+    loadings_new = loadings_update(
+        both_bin.reshape(bin_count, k_rows, -1), own_load, loadings, 2
+    ).reshape(width_all, -1)
     return (factors_new, loadings_new)
 
 

time: 302 us -> 294 us (0.974)
  Pallas kernels: 112 us -> 108 us
  matrix products: 48.8 us -> 45.3 us
    pallas_call x3 -> x1, Pallas kernels: 112 us -> 40.9 us  [exchange(): pl.pallas_call(functools.partial(exchange_kernel, axis, count, summed), o...]
    pallas_call x0 -> x1, Pallas kernels: none -> 66.8 us  [loadings_update(): pl.pallas_call(functools.partial(loadings_kernel, count), out_shape=jax.S...]
    dot_general x1 -> x0, matrix products: 3.55 us -> none  [on_device(): jnp.dot(fac_gram, loadings, precision=lax.Precision.HIGHEST)]
  transfers between devices with their start and end apart: 7 -> 7, of which waited for: 3 -> 3; matrix products, arithmetic and copies ran while one was open for 25% -> 26% of each run, Pallas kernels for 0% -> 0%
where the time goes in v9:
time: 294 us; the launch traced here: 289 us
  Pallas kernels  108 us (37%)
  local copies, waits for them, and re-layouts  47.5 us (16%)
  matrix products  45.3 us (15%)
  starting transfers between devices  32.3 us (11%)
  other arithmetic  27 us (9%)
  waiting for transfers between devices  15 us (5%)
  between operations  14.6 us (5%)
    pallas_call x1, Pallas kernels, loadings_update(): pl.pallas_call(functools.partial(loadings_kernel, count), out_shape=jax.S...  66.8 us
    pallas_call x1, Pallas kernels, exchange(): pl.pallas_call(functools.partial(exchange_kernel, axis, count, summed), o...  40.9 us
    ppermute x4, starting transfers between devices, passed_along(): return lax.ppermute(block, axis, route)  14.5 us
    unnamed x27, local copies, waits for them, and re-layouts  14.1 us
    all_to_all x1, waiting for transfers between devices, stencil_term(): lax.all_to_all(back_rows.reshape(bin_count, group_size * (width + 1)), 'b...  13.6 us
    dot_general x1, matrix products, on_device(): lax.dot_general(load_bf, counts, right_dims, preferred_element_type=jnp.f...  10.7 us
    all_to_all x1, starting transfers between devices, stencil_term(): lax.all_to_all(payload.reshape(bin_count, group_size * (width + 1)), 'bin...  9.29 us
    dot_general x1, matrix products, on_device(): cross_part = jnp.dot(fac_bf_t, counts, preferred_element_type=jnp.float32)  8.51 us
  transfers between devices with their start and end apart: 7, of which 3 were waited for; matrix products, arithmetic and copies ran while one was open for 26% of the time, Pallas kernels for 0%

profile of v9, /device:TPU:1, one launch (start us, length us, event | category | flops | bytes accessed | tf_op | source)
XLA Modules:
  0.0 289.2 jit_solution(2798900889435453215)
XLA Ops:
  7.2 0.0 copy-start
  7.2 1.9 copy-done
  9.1 1.6 constant_dynamic-slice_fusion.1
  10.7 1.8 copy.56
  12.5 0.8 pad_maximum_fusion.2
  13.4 2.7 copy.44
  16.0 3.8 %all_to_all.16 = f32[16,1,6336]{2,1,0:T(1,128)} reshape(f32[3072,33]{1,0:T(8,128)} %copy.44) | data formatting | bytes 811008 | tf_op jit(solution)/shard_map/all_to_all | solution.py:369
  19.9 9.3 %all-to-all-start = ((f32[16,1,6336]{2,1,0:T(1,128)}), f32[16,1,6336]{2,1,0:T(1,128)}, u32[]{:S(2)}, u32[]{:S(2)}) async-start(f32[16,1,6336]{2,1,0:T(1,128)} %all_to_all.16), calls=%async_computation.1 | async-start | bytes 819200 | tf_op jit(solution)/shard_map/all_to_all | solution.py:369
  29.2 0.0 reduce-scatter.2.cloned.1.call-start
  29.2 0.0 copy-start.2
  29.2 0.9 fusion.38
  30.1 0.6 fusion.43
  30.7 5.0 %collective-permute-start.3 = (f32[256]{0:T(256)}, f32[256]{0:T(256)}, u32[]{:S(2)}, u32[]{:S(2)}) collective-permute-start(f32[256]{0:T(256)} %bitcast.9), channel_id=1, source_target_pairs={{0,1},{1,2},{2,3},{3,4},{4,5},{5,6},{6,7},{7,8},{8,9},{9,10},{10,1... | collective-permute-start | bytes 3080 | tf_op jit(solution)/shard_map/ppermute | solution.py:17
  35.7 2.4 collective-permute-start.2
  38.1 2.9 fusion.20
  41.0 10.7 %fusion.22 = f32[256,3072]{1,0:T(8,128)} fusion(bf16[3072,2304]{1,0:T(8,128)(2,1)} %param.5, f32[256,2304]{1,0:T(8,128)S(1)} %copy-done.2), kind=kOutput, calls=%fused_computation.32 | convolution fusion | flops 3624468480 | bytes 19660800 | tf_op jit(solution)/shard_map/dot_general | solution.py:411
  51.7 3.8 %pad_maximum_fusion = f32[256,3328]{1,0:T(8,128)} fusion(f32[256,256]{1,0:T(8,128)S(1)} %fusion.20, f32[256,3072]{1,0:T(8,128)} %fusion.22), kind=kLoop, calls=%fused_computation.7 | loop fusion | flops 851968 | bytes 6815744 | tf_op jit(solution)/shard_map/concatenate | solution.py:413
  55.5 0.0 reduce-scatter.2.cloned.1.call-update
  55.6 0.7 fusion.42
  56.2 0.6 fusion.44
  56.9 0.0 collective-permute-done.3
  56.9 0.9 fusion.35
  57.7 0.6 copy.62
  58.3 2.7 reduce
  61.1 4.0 %reshape.122 = f32[3072,33]{1,0:T(8,128)} reshape(f32[16,6336]{1,0:T(8,128)} %reduce) | data formatting | bytes 811008 | tf_op jit(solution)/shard_map/reshape | solution.py:371
  65.0 2.9 copy.57
  67.9 2.3 fusion.7
  70.2 1.1 reduce-precision_convert_fusion.3
  71.3 7.7 %fusion.1 = f32[3072,96]{0,1:T(8,128)S(1)} fusion(s32[3072]{0:T(1024)S(1)} %fusion.7, bf16[3072,32]{0,1:T(8,128)(2,1)S(1)} %get-tuple-element.12, bf16[3072,32]{0,1:T(8,128)(2,1)S(1)} %get-tuple-element.13, bf16[3072,32]{0,1:T(8,128)(2,1)S(1)} %get-tuple-element.11), kind=kOutput, calls=%fused_computation.2 | convolution fusion | flops 1823145984 | bytes 1781760 | tf_op jit(solution)/shard_map/dot_general | solution.py:375
  79.0 0.8 slice_add_fusion.2
  79.8 1.9 reshape.123
  81.7 1.1 broadcast_multiply_fusion
  82.9 1.9 collective-permute-start
  84.8 5.1 %collective-permute-start.1 = (f32[256,32]{0,1:T(8,128)S(1)}, f32[256,32]{0,1:T(8,128)S(1)}, u32[]{:S(2)}, u32[]{:S(2)}) collective-permute-start(f32[256,32]{0,1:T(8,128)S(1)} %bitcast.69), channel_id=1, source_target_pairs={{0,1},{1,2},{2,3},{3,4},{4,5},{5,6},{6,7},{7,8},{8,9},{9,10},{10,1... | collective-permute-start | bytes 98312 | tf_op jit(solution)/shard_map/ppermute | solution.py:17
  90.0 0.2 fusion.39
  90.2 0.1 fusion.41
  90.3 0.6 collective-permute-done
  90.9 0.8 collective-permute-done.1
  91.7 0.3 fusion.26
  92.0 0.2 copy.61
  92.3 0.8 constant_dynamic-update-slice_fusion
  93.1 1.6 dynamic-update-slice.1
  94.6 1.1 reduce-precision_convert_fusion.1
  95.8 8.0 %fusion = f32[3072,99]{0,1:T(8,128)S(1)} fusion(s32[3072]{0:T(1024)S(1)} %copy-done.7, bf16[3072,33]{0,1:T(8,128)(2,1)S(1)} %get-tuple-element.9, bf16[3072,33]{0,1:T(8,128)(2,1)S(1)} %get-tuple-element.10, bf16[3072,33]{0,1:T(8,128)(2,1)S(1)} %get-tuple-element.8), kind=kOutput, calls=%fused_computation.1 | convolution fusion | flops 1879824384 | bytes 1837056 | tf_op jit(solution)/shard_map/dot_general | solution.py:393
  103.8 0.9 slice_add_fusion
  104.7 2.7 copy.49
  107.4 3.8 %all_to_all.17 = f32[16,1,6336]{2,1,0:T(1,128)} reshape(f32[3072,33]{1,0:T(8,128)} %copy.49) | data formatting | bytes 811008 | tf_op jit(solution)/shard_map/all_to_all | solution.py:395
  111.2 8.4 %all-to-all-start.1 = ((f32[16,1,6336]{2,1,0:T(1,128)}), f32[16,1,6336]{2,1,0:T(1,128)}, u32[]{:S(2)}, u32[]{:S(2)}) async-start(f32[16,1,6336]{2,1,0:T(1,128)} %all_to_all.17), calls=%async_computation.2 | async-start | bytes 819200 | tf_op jit(solution)/shard_map/all_to_all | solution.py:395
  119.7 1.6 constant_dynamic-slice_fusion.own_ref
  121.3 13.6 %all-to-all-done.1 = f32[16,1,6336]{2,1,0:T(1,128)} async-done(((f32[16,1,6336]{2,1,0:T(1,128)}), f32[16,1,6336]{2,1,0:T(1,128)}, u32[]{:S(2)}, u32[]{:S(2)}) %all-to-all-start.1) | async-done | bytes 405536 | tf_op jit(solution)/shard_map/all_to_all | solution.py:395
  134.9 2.7 reduce.2
  137.6 4.0 %reshape.126 = f32[3072,33]{1,0:T(8,128)} reshape(f32[16,6336]{1,0:T(8,128)} %reduce.2) | data formatting | bytes 811008 | tf_op jit(solution)/shard_map/reshape | solution.py:397
  141.6 2.6 copy.60
  144.2 2.3 fusion.5
  146.5 0.0 reduce-scatter.2.cloned.1.call-done
  146.5 4.8 %fusion.4.x_ref = f32[32,3072]{1,0:T(8,128)} fusion(f32[3072,256]{1,0:T(8,128)S(1)} %copy-done, f32[32,3328]{1,0:T(8,128)} %bitcast.70, f32[3072,32]{0,1:T(8,128)S(1)} %copy.56, f32[3072,32]{0,1:T(8,128)} %copy.60, f32[3072]{0:T(1024)S(1)} %fusion.5), kind=kOutput, calls=%fused_computation.6 | convolution fusion | flops 302579712 | bytes 4763648 | tf_op jit(solution)/shard_map/dot_general | solution.py:423
  151.4 40.9 %shard_map.68 = f32[8,32,3072]{2,1,0:T(8,128)} custom-call(f32[32,3072]{1,0:T(8,128)} %fusion.4.x_ref), custom_call_target="tpu_custom_call" | custom-call | tf_op jit(solution)/shard_map/pallas_call | solution.py:250
  192.2 3.4 %convert_element_type.38 = bf16[8,32,3072]{2,1,0:T(8,128)(2,1)} convert(f32[8,32,3072]{2,1,0:T(8,128)} %shard_map.68) | non-fusion elementwise | flops 786432 | bytes 4718592 | tf_op jit(solution)/shard_map/convert_element_type | solution.py:429
  195.6 8.5 %fusion.8 = f32[256,2304]{1,0:T(8,128)} fusion(bf16[3072,2304]{1,0:T(8,128)(2,1)} %param.5, f32[256,3072]{1,0:T(8,128)S(1)} %bitcast.56), kind=kOutput, calls=%fused_computation.14 | convolution fusion | flops 3624665088 | bytes 19660800 | tf_op jit(solution)/shard_map/dot_general | solution.py:430
  204.2 3.5 %copy.52 = f32[256,3072]{0,1:T(8,128)} copy(f32[256,3072]{1,0:T(8,128)} %bitcast.55) | data formatting | bytes 6291456 | tf_op jit(solution)/shard_map/reshape | solution.py:427
  207.7 2.6 fusion.45
  210.4 1.8 pad_maximum_fusion.1
  212.2 66.8 %shard_map.69 = f32[16,16,2304]{2,1,0:T(8,128)} custom-call(f32[16,16,2560]{2,1,0:T(8,128)} %bitcast.61, f32[16,2304]{1,0:T(8,128)} %constant_dynamic-slice_fusion.own_ref, f32[256,2304]{1,0:T(8,128)} %load_ref.1), custom_call_target="tpu_custom_call" | custom-call | tf_op jit(solution)/shard_map/pallas_call | solution.py:338
  278.9 3.2 %copy.69 = f32[256,2304]{1,0:T(8,128)} copy(f32[256,2304]{1,0:T(8,128)} %bitcast.62) | data formatting | bytes 4718592
  (23 shorter events, 0.1 us)
Async XLA Ops:
  7.2 1.9 copy-start
  9.1 3.5 %copy-start.8 = (s32[3072]{0:T(1024)S(1)}, s32[3072]{0:T(1024)}, u32[]{:S(2)}) copy-start(s32[3072]{0:T(1024)} %param.8) | copy-start | bytes 36868
  19.9 38.5 %all-to-all-start = ((f32[16,1,6336]{2,1,0:T(1,128)}), f32[16,1,6336]{2,1,0:T(1,128)}, u32[]{:S(2)}, u32[]{:S(2)}) async-start(f32[16,1,6336]{2,1,0:T(1,128)} %all_to_all.16), calls=%async_computation.1 | async-start | bytes 819200 | tf_op jit(solution)/shard_map/all_to_all | solution.py:369
  29.2 117.4 %reduce-scatter.2.cloned.1.call-start = ((), (), s32[]{:S(2)}) async-start(), calls=%async_computation.3 | async-start | bytes 3833856 | tf_op jit(solution)/shard_map/reduce_scatter | solution.py:414
  29.2 11.8 %copy-start.2 = (f32[256,2304]{1,0:T(8,128)S(1)}, f32[256,2304]{1,0:T(8,128)}, u32[]{:S(2)}) copy-start(f32[256,2304]{1,0:T(8,128)} %load_ref.1) | copy-start | bytes 7077892
  30.1 5.6 %copy-start.4 = (f32[12,256]{1,0:T(8,128)}, f32[12,256]{1,0:T(8,128)S(1)}, u32[]{:S(2)}) copy-start(f32[12,256]{1,0:T(8,128)S(1)} %get-tuple-element.21) | copy-start | bytes 36868
  30.7 26.2 %collective-permute-start.3 = (f32[256]{0:T(256)}, f32[256]{0:T(256)}, u32[]{:S(2)}, u32[]{:S(2)}) collective-permute-start(f32[256]{0:T(256)} %bitcast.9), channel_id=1, source_target_pairs={{0,1},{1,2},{2,3},{3,4},{4,5},{5,6},{6,7},{7,8},{8,9},{9,10},{10,1... | collective-permute-start | bytes 3080 | tf_op jit(solution)/shard_map/ppermute | solution.py:17
  35.7 21.1 %collective-permute-start.2 = (f32[256]{0:T(256)}, f32[256]{0:T(256)}, u32[]{:S(2)}, u32[]{:S(2)}) collective-permute-start(f32[256]{0:T(256)} %bitcast.7), channel_id=1, source_target_pairs={{1,0},{2,1},{3,2},{4,3},{5,4},{6,5},{7,6},{8,7},{9,8},{10,9},{11,1... | collective-permute-start | bytes 3080 | tf_op jit(solution)/shard_map/ppermute | solution.py:17
  70.2 8.8 %copy-start.6 = (s32[3072]{0:T(1024)}, s32[3072]{0:T(1024)S(1)}, u32[]{:S(2)}) copy-start(s32[3072]{0:T(1024)S(1)} %fusion.7) | copy-start | bytes 36868
  79.0 2.7 copy-start.5
  82.9 8.0 %collective-permute-start = (f32[256,32]{0,1:T(8,128)S(1)}, f32[256,32]{0,1:T(8,128)S(1)}, u32[]{:S(2)}, u32[]{:S(2)}) collective-permute-start(f32[256,32]{0,1:T(8,128)S(1)} %bitcast.68), channel_id=1, source_target_pairs={{1,0},{2,1},{3,2},{4,3},{5,4},{6,5},{7,6},{8,7},{9,8},{10,9},{11,1... | collective-permute-start | bytes 98312 | tf_op jit(solution)/shard_map/ppermute | solution.py:17
  84.8 6.9 %collective-permute-start.1 = (f32[256,32]{0,1:T(8,128)S(1)}, f32[256,32]{0,1:T(8,128)S(1)}, u32[]{:S(2)}, u32[]{:S(2)}) collective-permute-start(f32[256,32]{0,1:T(8,128)S(1)} %bitcast.69), channel_id=1, source_target_pairs={{0,1},{1,2},{2,3},{3,4},{4,5},{5,6},{6,7},{7,8},{8,9},{9,10},{10,1... | collective-permute-start | bytes 98312 | tf_op jit(solution)/shard_map/ppermute | solution.py:17
  92.0 3.8 %copy-start.7 = (s32[3072]{0:T(1024)S(1)}, s32[3072]{0:T(1024)}, u32[]{:S(2)}) copy-start(s32[3072]{0:T(1024)} %copy-done.6) | copy-start | bytes 36868
  111.2 23.7 %all-to-all-start.1 = ((f32[16,1,6336]{2,1,0:T(1,128)}), f32[16,1,6336]{2,1,0:T(1,128)}, u32[]{:S(2)}, u32[]{:S(2)}) async-start(f32[16,1,6336]{2,1,0:T(1,128)} %all_to_all.17), calls=%async_computation.2 | async-start | bytes 819200 | tf_op jit(solution)/shard_map/all_to_all | solution.py:395
  192.2 3.4 %copy-start.1 = (f32[8,32,3072]{2,1,0:T(8,128)S(1)}, f32[8,32,3072]{2,1,0:T(8,128)}, u32[]{:S(2)}) copy-start(f32[8,32,3072]{2,1,0:T(8,128)} %shard_map.68) | copy-start | bytes 9437188
  207.7 2.6 copy-start.3
Sparse Core Ops, SparseCore 0:
  55.7 82.4 reduce-scatter.1
